TPU v7x, 32 devices: a whole 2x2x4 slice. The times are simulated.
32 devices in a mesh: group: 4 (over y, x), dp: 2 (over core), tensor: 4 (over z).
Axes of the slice: x: 2, y: 2, z: 4, core: 2. Of those that a mesh axis runs over, the one named last changes fastest.
Arguments:
- features: bfloat16 [12288, 1024], P(('group', 'dp', 'tensor')), may hold values from -6 to 6
- cotangent: bfloat16 [12288, 1024], P(('group', 'dp', 'tensor')), may hold values from -6 to 6
- frame_counts: int32 [8, 3], P(('group', 'dp')), may hold values from 1 to 768, 1536 in all within a row
- buckets: int32 [8, 3], P(('group', 'dp')), may hold values from 0 to 7
- step_count: int32 [1], replicated, may hold values from 2 to 20
- col_weights: float32 [1024, 5, 1024], P('dp', None, 'tensor'), may hold values from -0.1875 to 0.1875
- mod_weights: float32 [1024, 6, 1024], P('dp', None, 'tensor'), may hold values from -0.375 to 0.375
- row_weights: float32 [3, 1024, 1024], P(None, 'dp', 'tensor'), may hold values from -0.25 to 0.25
- col_first: float32 [4, 1024, 5, 1024], P('group', 'dp', None, 'tensor'), may hold values from -32 to 32
- col_second: float32 [4, 1024, 5, 1024], P('group', 'dp', None, 'tensor'), may hold values from 1.536 to 6.144
- mod_first: float32 [4, 1024, 6, 1024], P('group', 'dp', None, 'tensor'), may hold values from -32 to 32
- mod_second: float32 [4, 1024, 6, 1024], P('group', 'dp', None, 'tensor'), may hold values from 1.536 to 6.144
- row_first: float32 [4, 3, 1024, 1024], P('group', None, 'dp', 'tensor'), may hold values from -32 to 32
- row_second: float32 [4, 3, 1024, 1024], P('group', None, 'dp', 'tensor'), may hold values from 1.536 to 6.144
- col_outer: float32 [1024, 5, 1024], P('dp', None, 'tensor'), may hold values from -1.5 to 1.5
- mod_outer: float32 [1024, 6, 1024], P('dp', None, 'tensor'), may hold values from -1.5 to 1.5
- row_outer: float32 [3, 1024, 1024], P(None, 'dp', 'tensor'), may hold values from -1.5 to 1.5
Outputs:
- output: bfloat16 [12288, 1024], P(('group', 'dp', 'tensor'))
- input_grad: float32 [12288, 1024], P(('group', 'dp', 'tensor'))
- col_first_new: float32 [4, 1024, 5, 1024], P('group', 'dp', None, 'tensor')
- col_second_new: float32 [4, 1024, 5, 1024], P('group', 'dp', None, 'tensor')
- col_average: float32 [1024, 5, 1024], P('dp', None, 'tensor')
- col_outer_new: float32 [1024, 5, 1024], P('dp', None, 'tensor')
- col_new: float32 [1024, 5, 1024], P('dp', None, 'tensor')
- mod_first_new: float32 [4, 1024, 6, 1024], P('group', 'dp', None, 'tensor')
- mod_second_new: float32 [4, 1024, 6, 1024], P('group', 'dp', None, 'tensor')
- mod_average: float32 [1024, 6, 1024], P('dp', None, 'tensor')
- mod_outer_new: float32 [1024, 6, 1024], P('dp', None, 'tensor')
- mod_new: float32 [1024, 6, 1024], P('dp', None, 'tensor')
- row_first_new: float32 [4, 3, 1024, 1024], P('group', None, 'dp', 'tensor')
- row_second_new: float32 [4, 3, 1024, 1024], P('group', None, 'dp', 'tensor')
- row_average: float32 [3, 1024, 1024], P(None, 'dp', 'tensor')
- row_outer_new: float32 [3, 1024, 1024], P(None, 'dp', 'tensor')
- row_new: float32 [3, 1024, 1024], P(None, 'dp', 'tensor')
Inputs may be any that keep to these rules, and one draw needn't show every extreme that they name: frame_counts[b] lists the frames of the 3 utterances of pack b; they sum to 1536 and the longest has exactly 768.
All inputs are finite; a program needn't handle non-finite values.
Results may differ from a plain program's by a relative error of at most 0.01695.
The roundings to bfloat16 on the way count: a program that leaves them out, or rounds other values in their place, can miss the bound.
Values may be sent and summed in bfloat16 or wider, within the bound.
No kernel may reach another device: no remote copies, remote signals or barrier semaphores. Data moves between devices by JAX's collectives and lax.ppermute only.
A program may use at most 256 MiB of HBM per device.

v0:
```python
from functools import partial
import math

import jax
import jax.numpy as jnp
from jax import lax
from jax.sharding import PartitionSpec as P

HEAD_DIM = 64
NBUCK = 8


highest = lax.Precision.HIGHEST
norm_epsilon = 1e-06
adam_epsilon = 1e-08
beta_first = 0.9
beta_second = 0.999
inner_rate = 0.05
weight_decay = 0.01
outer_rate = 0.7
outer_beta = 0.9


def time_embedding(flow_time, width_all):
    half_width = width_all // 2
    frequency = jnp.exp(
        jnp.arange(half_width, dtype=jnp.float32) * (-math.log(10000.0) / (half_width - 1))
    )
    angles = 1000.0 * flow_time[:, None] * frequency[None, :]
    return jnp.concatenate([jnp.sin(angles), jnp.cos(angles)], axis=1)


def pack_geometry(lengths, frames):
    ending = jnp.cumsum(lengths)
    starting = ending - lengths
    indices = jnp.arange(frames, dtype=jnp.int32)
    member = (indices[:, None] >= starting[None, :]) & (indices[:, None] < ending[None, :])
    onehot = member.astype(jnp.float32)
    offsets = jnp.sum(jnp.where(member, starting[None, :], 0), axis=1)
    position = (indices - offsets).astype(jnp.float32)
    numbers = jnp.arange(lengths.shape[0], dtype=jnp.int32)
    segment = jnp.sum(jnp.where(member, numbers[None, :], 0), axis=1)
    same_segment = segment[:, None] == segment[None, :]
    return (onehot, position, same_segment)


def rotary_tables(position, head_width):
    half_width = head_width // 2
    frequency = jnp.exp(
        jnp.arange(half_width, dtype=jnp.float32) * (-2.0 * math.log(10000.0) / head_width)
    )
    angles = position[:, None] * frequency[None, :]
    return (jnp.cos(angles)[:, None, :], jnp.sin(angles)[:, None, :])


def rotate(values, cosine, sine_part):
    half_width = values.shape[-1] // 2
    leading, trailing = (values[..., :half_width], values[..., half_width:])
    return jnp.concatenate(
        [leading * cosine - trailing * sine_part, trailing * cosine + leading * sine_part], axis=-1
    )


def rotate_back(grads, cosine, sine_part):
    half_width = grads.shape[-1] // 2
    leading, trailing = (grads[..., :half_width], grads[..., half_width:])
    return jnp.concatenate(
        [leading * cosine + trailing * sine_part, trailing * cosine - leading * sine_part], axis=-1
    )


def normalize(values):
    centered = values - jnp.mean(values, axis=-1, keepdims=True)
    inverse_scale = lax.rsqrt(jnp.mean(centered * centered, axis=-1, keepdims=True) + norm_epsilon)
    return (centered * inverse_scale, inverse_scale)


def normalize_back(grads, normed, inverse_scale):
    return inverse_scale * (
        grads
        - jnp.mean(grads, axis=-1, keepdims=True)
        - normed * jnp.mean(grads * normed, axis=-1, keepdims=True)
    )


def attend(queries, key_rows, value_rows, same_segment):
    frames = queries.shape[0]
    block_rows = min(512, frames)
    score_scale = 1.0 / math.sqrt(queries.shape[-1])

    def block_output(begin_row):
        query_block = lax.dynamic_slice_in_dim(queries, begin_row, block_rows, 0)
        mask_block = lax.dynamic_slice_in_dim(same_segment, begin_row, block_rows, 0)
        scores = (
            jnp.einsum("qhd,khd->hqk", query_block, key_rows, preferred_element_type=jnp.float32)
            * score_scale
        )
        scores = jnp.where(mask_block[None], scores, -1e30)
        largest = jnp.max(scores, axis=-1, keepdims=True)
        exponent = jnp.exp(scores - largest)
        totals = jnp.sum(exponent, axis=-1, keepdims=True)
        weights = (exponent / totals).astype(jnp.bfloat16)
        mixed_block = jnp.einsum(
            "hqk,khd->qhd", weights, value_rows, preferred_element_type=jnp.float32
        )
        return (mixed_block.astype(jnp.bfloat16), (largest + jnp.log(totals))[..., 0])

    begins = jnp.arange(frames // block_rows, dtype=jnp.int32) * block_rows
    mixed_blocks, log_totals = lax.map(block_output, begins)
    return (mixed_blocks.reshape(frames, -1), log_totals)


def attend_back(queries, key_rows, value_rows, same_segment, log_totals, grad_mixed):
    frames, heads_here, head_width = queries.shape
    block_rows = min(512, frames)
    score_scale = 1.0 / math.sqrt(head_width)
    grad_heads = grad_mixed.reshape(frames, heads_here, head_width)

    def block_grads(carry, items):
        key_sum, value_sum = carry
        begin_row, log_block = items
        query_block = lax.dynamic_slice_in_dim(queries, begin_row, block_rows, 0)
        mask_block = lax.dynamic_slice_in_dim(same_segment, begin_row, block_rows, 0)
        grad_block = lax.dynamic_slice_in_dim(grad_heads, begin_row, block_rows, 0)
        scores = (
            jnp.einsum("qhd,khd->hqk", query_block, key_rows, preferred_element_type=jnp.float32)
            * score_scale
        )
        scores = jnp.where(mask_block[None], scores, -1e30)
        probs = jnp.exp(scores - log_block[..., None])
        grad_probs = jnp.einsum(
            "qhd,khd->hqk", grad_block, value_rows, preferred_element_type=jnp.float32
        )
        grad_scores = (
            probs * (grad_probs - jnp.sum(probs * grad_probs, axis=-1, keepdims=True))
        ).astype(jnp.bfloat16)
        grad_query = (
            jnp.einsum("hqk,khd->qhd", grad_scores, key_rows, preferred_element_type=jnp.float32)
            * score_scale
        )
        key_sum = (
            key_sum
            + jnp.einsum(
                "hqk,qhd->khd", grad_scores, query_block, preferred_element_type=jnp.float32
            )
            * score_scale
        )
        value_sum = value_sum + jnp.einsum(
            "hqk,qhd->khd",
            probs.astype(jnp.bfloat16),
            grad_block,
            preferred_element_type=jnp.float32,
        )
        return ((key_sum, value_sum), grad_query)

    zeros = jnp.zeros((frames, heads_here, head_width), jnp.float32)
    begins = jnp.arange(frames // block_rows, dtype=jnp.int32) * block_rows
    sums, grad_queries = lax.scan(block_grads, (zeros, zeros), (begins, log_totals))
    return (grad_queries.reshape(frames, heads_here, head_width), sums[0], sums[1])


def inner_step(grads, first, second, weights, steps_done):
    first_new = beta_first * first + (1.0 - beta_first) * grads
    second_new = beta_second * second + (1.0 - beta_second) * grads * grads
    correct_one = 1.0 - beta_first**steps_done
    correct_two = 1.0 - beta_second**steps_done
    difference = inner_rate * (
        first_new / correct_one / (jnp.sqrt(second_new / correct_two) + adam_epsilon)
        + weight_decay * weights
    )
    return (first_new[None], second_new[None], difference)


def outer_step(average, outer, weights):
    outer_new = outer_beta * outer + average
    return (outer_new, weights - outer_rate * (average + outer_beta * outer_new))


def per_device(
    features,
    cotangent,
    frame_counts,
    buckets,
    step_count,
    col_weights,
    mod_weights,
    row_weights,
    col_first,
    col_second,
    mod_first,
    mod_second,
    row_first,
    row_second,
    col_outer,
    mod_outer,
    row_outer,
):
    tensor_parts = lax.axis_size("tensor")
    group_count = lax.axis_size("group")
    own_rows, model_width = features.shape
    frames = own_rows * tensor_parts
    first_row = lax.axis_index("tensor") * own_rows
    col_low, row_low = (
        lax.all_gather(col_weights.astype(jnp.bfloat16), "dp", axis=0, tiled=True),
        lax.all_gather(row_weights.astype(jnp.bfloat16), "dp", axis=1, tiled=True),
    )
    onehot_all, position, same_segment = pack_geometry(frame_counts[0], frames)
    onehot_own = lax.dynamic_slice_in_dim(onehot_all, first_row, own_rows, 0)
    cosine, sine_part = rotary_tables(position, HEAD_DIM)
    flow_time = ((lax.axis_index("group") * NBUCK + buckets[0]).astype(jnp.float32) + 0.5) / (
        NBUCK * group_count
    )
    condition = jax.nn.silu(time_embedding(flow_time, model_width)).astype(jnp.bfloat16)
    mod_low = lax.all_gather(mod_weights.astype(jnp.bfloat16), "dp", axis=0, tiled=True)
    mod_part = jnp.einsum("ud,dcj->ucj", condition, mod_low, preferred_element_type=jnp.float32)
    modulation = lax.all_gather(mod_part, "tensor", axis=2, tiled=True)
    per_row = jnp.einsum("fu,ucj->fcj", onehot_own, modulation, precision=highest)
    features_in = features.astype(jnp.float32)
    grad_output = cotangent.astype(jnp.float32)
    normed, inverse_scale = normalize(features_in)
    att_in = (normed * (1.0 + per_row[:, 1]) + per_row[:, 0]).astype(jnp.bfloat16)
    grad_ffn = (grad_output * per_row[:, 5]).astype(jnp.bfloat16)
    att_full, grad_ffn_full = (
        lax.all_gather(att_in, "tensor", axis=0, tiled=True),
        lax.all_gather(grad_ffn, "tensor", axis=0, tiled=True),
    )
    projected = jnp.einsum(
        "fd,dcj->fcj", att_full, col_low[:, 0:3], preferred_element_type=jnp.float32
    )
    head_rows = projected.reshape(frames, 3, -1, HEAD_DIM)
    queries = rotate(head_rows[:, 0], cosine, sine_part).astype(jnp.bfloat16)
    key_rows = rotate(head_rows[:, 1], cosine, sine_part).astype(jnp.bfloat16)
    value_rows = head_rows[:, 2].astype(jnp.bfloat16)
    mixed_rows, log_totals = attend(queries, key_rows, value_rows, same_segment)
    piece = mixed_rows
    attn_out = lax.psum_scatter(
        jnp.einsum("fj,dj->fd", piece, row_low[0], preferred_element_type=jnp.float32),
        "tensor",
        scatter_dimension=0,
        tiled=True,
    )
    residual = features_in + per_row[:, 2] * attn_out
    normed_two, inverse_two = normalize(residual)
    ffn_in = (normed_two * (1.0 + per_row[:, 4]) + per_row[:, 3]).astype(jnp.bfloat16)
    ffn_full = lax.all_gather(ffn_in, "tensor", axis=0, tiled=True)
    upward = jnp.einsum(
        "fd,dcj->fcj", ffn_full, col_low[:, 3:5], preferred_element_type=jnp.float32
    )
    hidden = jax.nn.gelu(upward, approximate=True).astype(jnp.bfloat16)
    piece = hidden
    ffn_out = lax.psum_scatter(
        jnp.einsum("fcj,cdj->fd", piece, row_low[1:3], preferred_element_type=jnp.float32),
        "tensor",
        scatter_dimension=0,
        tiled=True,
    )
    output = (residual + per_row[:, 5] * ffn_out).astype(jnp.bfloat16)
    grad_hidden = jnp.einsum(
        "fd,cdj->fcj", grad_ffn_full, row_low[1:3], preferred_element_type=jnp.float32
    )
    gelu_pull = jax.vjp(partial(jax.nn.gelu, approximate=True), upward)[1]
    grad_upward = gelu_pull(grad_hidden)[0].astype(jnp.bfloat16)
    down_grad = jnp.einsum("fcj,fd->cdj", hidden, grad_ffn_full, preferred_element_type=jnp.float32)
    up_grad = jnp.einsum("fd,fcj->dcj", ffn_full, grad_upward, preferred_element_type=jnp.float32)
    piece = grad_upward
    grad_ffn_in = lax.psum_scatter(
        jnp.einsum("fcj,dcj->fd", piece, col_low[:, 3:5], preferred_element_type=jnp.float32),
        "tensor",
        scatter_dimension=0,
        tiled=True,
    )
    grad_residual = grad_output + normalize_back(
        grad_ffn_in * (1.0 + per_row[:, 4]), normed_two, inverse_two
    )
    grad_attn = (grad_residual * per_row[:, 2]).astype(jnp.bfloat16)
    grad_attn_full = lax.all_gather(grad_attn, "tensor", axis=0, tiled=True)
    grad_mixed = jnp.einsum(
        "fd,dj->fj", grad_attn_full, row_low[0], preferred_element_type=jnp.float32
    ).astype(jnp.bfloat16)
    out_grad = jnp.einsum(
        "fj,fd->dj", mixed_rows, grad_attn_full, preferred_element_type=jnp.float32
    )
    row_grad = jnp.concatenate([out_grad[None], down_grad], axis=0)
    grad_queries, grad_keys, grad_values = attend_back(
        queries, key_rows, value_rows, same_segment, log_totals, grad_mixed
    )
    grad_projected = (
        jnp.stack(
            [
                rotate_back(grad_queries, cosine, sine_part),
                rotate_back(grad_keys, cosine, sine_part),
                grad_values,
            ],
            axis=1,
        )
        .reshape(frames, 3, -1)
        .astype(jnp.bfloat16)
    )
    qkv_grad = jnp.einsum(
        "fd,fcj->dcj", att_full, grad_projected, preferred_element_type=jnp.float32
    )
    piece = grad_projected
    grad_att_in = lax.psum_scatter(
        jnp.einsum("fcj,dcj->fd", piece, col_low[:, 0:3], preferred_element_type=jnp.float32),
        "tensor",
        scatter_dimension=0,
        tiled=True,
    )
    grad_features = grad_residual + normalize_back(
        grad_att_in * (1.0 + per_row[:, 1]), normed, inverse_scale
    )
    mod_rows = jnp.stack(
        [
            grad_att_in,
            grad_att_in * normed,
            grad_residual * attn_out,
            grad_ffn_in,
            grad_ffn_in * normed_two,
            grad_output * ffn_out,
        ],
        axis=1,
    )
    mod_sums = jnp.einsum("fu,fcj->ucj", onehot_own, mod_rows, precision=highest)
    mod_columns = lax.psum_scatter(mod_sums, "tensor", scatter_dimension=2, tiled=True)
    mod_grad = jnp.einsum(
        "ud,ucj->dcj", condition.astype(jnp.float32), mod_columns, precision=highest
    )
    mod_share = lax.psum_scatter(mod_grad, "dp", scatter_dimension=0, tiled=True)
    col_share, row_share = (
        lax.psum_scatter(
            jnp.concatenate([qkv_grad, up_grad], axis=1), "dp", scatter_dimension=0, tiled=True
        ),
        lax.psum_scatter(row_grad, "dp", scatter_dimension=1, tiled=True),
    )
    steps_done = step_count[0].astype(jnp.float32)
    col_first_new, col_second_new, col_diff = inner_step(
        col_share, col_first[0], col_second[0], col_weights, steps_done
    )
    mod_first_new, mod_second_new, mod_diff = inner_step(
        mod_share, mod_first[0], mod_second[0], mod_weights, steps_done
    )
    row_first_new, row_second_new, row_diff = inner_step(
        row_share, row_first[0], row_second[0], row_weights, steps_done
    )
    col_total, mod_total, row_total = lax.psum((col_diff, mod_diff, row_diff), "group")
    col_average = col_total / group_count
    mod_average = mod_total / group_count
    row_average = row_total / group_count
    col_outer_new, col_new = outer_step(col_average, col_outer, col_weights)
    mod_outer_new, mod_new = outer_step(mod_average, mod_outer, mod_weights)
    row_outer_new, row_new = outer_step(row_average, row_outer, row_weights)
    return (
        output,
        grad_features,
        col_first_new,
        col_second_new,
        col_average,
        col_outer_new,
        col_new,
        mod_first_new,
        mod_second_new,
        mod_average,
        mod_outer_new,
        mod_new,
        row_first_new,
        row_second_new,
        row_average,
        row_outer_new,
        row_new,
    )


def solution(mesh):
    placed = (
        P(("group", "dp", "tensor"), None),
        P(("group", "dp", "tensor"), None),
        P(("group", "dp"), None),
        P(("group", "dp"), None),
        P(),
        P("dp", None, "tensor"),
        P("dp", None, "tensor"),
        P(None, "dp", "tensor"),
        P("group", "dp", None, "tensor"),
        P("group", "dp", None, "tensor"),
        P("group", "dp", None, "tensor"),
        P("group", "dp", None, "tensor"),
        P("group", None, "dp", "tensor"),
        P("group", None, "dp", "tensor"),
        P("dp", None, "tensor"),
        P("dp", None, "tensor"),
        P(None, "dp", "tensor"),
    )
    return jax.shard_map(
        per_device,
        mesh=mesh,
        in_specs=placed,
        out_specs=(
            P(("group", "dp", "tensor"), None),
            P(("group", "dp", "tensor"), None),
            P("group", "dp", None, "tensor"),
            P("group", "dp", None, "tensor"),
            P("dp", None, "tensor"),
            P("dp", None, "tensor"),
            P("dp", None, "tensor"),
            P("group", "dp", None, "tensor"),
            P("group", "dp", None, "tensor"),
            P("dp", None, "tensor"),
            P("dp", None, "tensor"),
            P("dp", None, "tensor"),
            P("group", None, "dp", "tensor"),
            P("group", None, "dp", "tensor"),
            P(None, "dp", "tensor"),
            P(None, "dp", "tensor"),
            P(None, "dp", "tensor"),
        ),
        check_vma=False,
    )
```

profile of v0, /device:TPU:0, one launch (start us, length us, event | category | flops | bytes accessed | tf_op | source)
XLA Modules:
  0.0 1248.6 jit_solution(9204127768730256553)
XLA Ops:
  7.2 3.3 convert_element_type.88
  13.4 12.2 all-gather.8.cloned.1.call-done
  28.0 13.6 %all_gather.25 = f32[3,6,1024]{2,0,1:T(4,128)S(1)} all-gather(f32[3,6,256]{2,0,1:T(4,128)S(1)} %fusion.101), channel_id=1, replica_groups=mesh['group'=4,'dp'=2,'tensor'=4] {'tensor'}, dimensions={2}, use_global_device_ids=true | all-gather | bytes 92160 | tf_op jit(solution)/shard_map/all_gather | solution.py:216
  41.6 3.9 fusion.105
  45.5 3.7 copy-done.3
  55.4 59.6 %all-gather.10.cloned.1.call-done = bf16[1536,1024]{1,0:T(8,128)(2,1)} async-done(((bf16[384,1024]{1,0:T(8,128)(2,1)}), bf16[1536,1024]{1,0:T(8,128)(2,1)}) %all-gather.10.cloned.1.call-update) | async-done | bytes 3145744 | tf_op jit(solution)/shard_map/all_gather | solution.py:224
  115.1 5.0 fusion.49
  121.0 45.2 %while.27 = (s32[]{:T(128)}, bf16[3,512,4,64]{1,3,2,0:T(8,128)(2,1)S(1)}, f32[3,4,512]{2,1,0:T(4,128)S(1)}, s32[3]{0:T(128)S(1)}, pred[1536,1536]{1,0:T(8,128)(4...) while((s32[]{:T(128)}, ...), condition=%wide.region_8.9_spmd, body=%wide.region_5.8_spmd.sunk | while | flops 843184128 | bytes 43843764 | solution.py:109
  128.0 3.5 fusion.156
  131.5 4.6 fusion.157
  143.0 3.5 fusion.156
  146.6 4.6 fusion.157
  158.1 3.5 fusion.156
  161.6 4.6 fusion.157
  167.2 4.9 fusion.96
  172.4 109.3 %reduce-scatter.11.cloned.1.call-done = f32[384,1024]{1,0:T(8,128)} async-done(((f32[1536,1024]{1,0:T(8,128)}), f32[384,1024]{1,0:T(8,128)}) %reduce-scatter.11.cloned.1.call-update) | async-done | bytes 1572880 | tf_op jit(solution)/shard_map/reduce_scatter | solution.py:236
  284.4 4.3 fusion.72
  289.6 63.3 %all-gather.16.cloned.1.call-done = bf16[1536,1024]{1,0:T(8,128)(2,1)} async-done(((bf16[384,1024]{1,0:T(8,128)(2,1)}), bf16[1536,1024]{1,0:T(8,128)(2,1)}) %all-gather.16.cloned.1.call-update) | async-done | bytes 3145744 | tf_op jit(solution)/shard_map/all_gather | solution.py:245
  352.9 5.7 fusion.45
  358.6 58.6 %all-gather.18.cloned.1.call-done = bf16[1536,1024]{1,0:T(8,128)(2,1)} async-done(((bf16[384,1024]{1,0:T(8,128)(2,1)}), bf16[1536,1024]{1,0:T(8,128)(2,1)}) %all-gather.18.cloned.1.call-update) | async-done | bytes 3145744 | tf_op jit(solution)/shard_map/all_gather | solution.py:225
  417.1 6.7 fusion.37
  425.0 5.6 convolution_bitcast_fusion.1
  430.8 7.2 convolution_bitcast_fusion.2
  438.0 102.3 %reduce-scatter.15.cloned.1.call-done = f32[384,1024]{1,0:T(8,128)} async-done(((f32[1536,1024]{1,0:T(8,128)}), f32[384,1024]{1,0:T(8,128)}) %reduce-scatter.15.cloned.1.call-update) | async-done | bytes 1572880 | tf_op jit(solution)/shard_map/reduce_scatter | solution.py:266
  542.7 111.2 %reduce-scatter.13.cloned.1.call-done = f32[384,1024]{1,0:T(8,128)} async-done(((f32[1536,1024]{1,0:T(8,128)}), f32[384,1024]{1,0:T(8,128)}) %reduce-scatter.13.cloned.1.call-update) | async-done | bytes 1572880 | tf_op jit(solution)/shard_map/reduce_scatter | solution.py:251
  653.9 6.0 multiply_convert_fusion.2
  660.0 64.0 %all-gather.20.cloned.1.call-done = bf16[1536,1024]{1,0:T(8,128)(2,1)} async-done(((bf16[384,1024]{1,0:T(8,128)(2,1)}), bf16[1536,1024]{1,0:T(8,128)(2,1)}) %all-gather.20.cloned.1.call-update) | async-done | bytes 3145744 | tf_op jit(solution)/shard_map/all_gather | solution.py:276
  724.0 3.9 convolution_convert_fusion
  727.9 120.4 %while.28 = (s32[]{:T(128)}, f32[1536,4,64]{0,2,1:T(8,128)}, f32[1536,4,64]{0,2,1:T(8,128)}, f32[3,512,4,64]{1,0,3,2:T(4,128)}, s32[3]{0:T(128)S(1)}, /*index=5*...) while((s32[]{:T(128)}, f32[1536,4,64]{0,2,1:T(8,128)}, ...), condition=%wide.region_18.19_spmd.clone, body=%wide.region_16.18_spmd.clone.sunk | while | flops 2043672576 | bytes 159424960 | solution.py:158
  736.4 6.0 multiply_reduce_fusion.4
  742.4 3.7 multiply_convert_fusion.6
  746.2 3.5 fusion.169
  749.7 3.3 fusion.170
  756.9 11.1 dynamic_update_slice.20
  776.1 6.0 multiply_reduce_fusion.4
  782.1 3.7 multiply_convert_fusion.6
  785.8 4.1 fusion.169
  789.9 3.3 fusion.170
  797.1 11.1 dynamic_update_slice.20
  816.3 5.9 multiply_reduce_fusion.4
  822.3 3.7 multiply_convert_fusion.6
  826.0 4.0 fusion.169
  830.1 3.3 fusion.170
  837.2 11.1 dynamic_update_slice.20
  848.4 3.3 reshape.247
  855.9 7.1 convolution_bitcast_fusion
  863.1 6.3 fusion.60
  870.4 102.2 %reduce-scatter.17.cloned.1.call-done = f32[384,1024]{1,0:T(8,128)} async-done(((f32[1536,1024]{1,0:T(8,128)}), f32[384,1024]{1,0:T(8,128)}) %reduce-scatter.17.cloned.1.call-update) | async-done | bytes 1572880 | tf_op jit(solution)/shard_map/reduce_scatter | solution.py:303
  980.2 3.8 fusion.103
  987.0 3.8 reshape.259
  990.9 3.5 pad_maximum_fusion.1
  994.4 4.3 fusion.43
  1004.4 8.9 reduce-scatter.25.cloned.1.call-done
  1014.4 5.3 fusion.92
  1020.8 4.5 reduce-scatter.23.cloned.1.call-done
  1025.3 6.1 fusion.97
  1031.4 10.2 reduce-scatter.19.cloned.1.call-done
  1041.7 8.5 add_multiply_fusion.1
  1050.1 8.9 reduce-scatter.21.cloned.1.call-done
  1059.0 8.2 fusion.90
  1072.4 151.7 %all-reduce.3.cloned.1.call-done = (f32[512,5,256]{2,0,1:T(8,128)}, f32[512,6,256]{2,0,1:T(8,128)}, f32[3,512,256]{2,1,0:T(8,128)}) async-done(((f32[512,5,256]{2,0,1:T(8,128)}, f32[512,6,256]{2,0,1:T(8,128)}, f32[3,512,256]{2,1,0:T(8,128)}), (f32[512,5,256]{2,0,1:T(8,128)}, f32[512,6,256]{2,0,1:T(8,128)}, f32[3,512,256]{2,1,0:T(8,128)})) %all-reduce.3.cloned.1.call-update) | async-done | bytes 7340048 | tf_op jit(solution)/shard_map/psum | solution.py:345
  1224.1 5.3 multiply_subtract_fusion.2
  1230.6 4.6 multiply_subtract_fusion.1
  1237.1 4.6 multiply_subtract_fusion
  (273 shorter events, 96.4 us)
Async XLA Ops:
  7.2 18.4 %all-gather.8.cloned.1.call-start = ((), (), s32[]{:S(2)}) async-start(), calls=%async_computation.8 | async-start | bytes 4718592 | tf_op jit(solution)/shard_map/all_gather | solution.py:214
  10.6 44.8 %all-gather.12.cloned.1.call-start = ((), (), s32[]{:S(2)}) async-start(), calls=%async_computation.10 | async-start | bytes 3932160 | tf_op jit(solution)/shard_map/all_gather | solution.py:204
  12.3 102.8 %all-gather.10.cloned.1.call-start = ((), (), s32[]{:S(2)}) async-start(), calls=%async_computation.9 | async-start | bytes 3932160 | tf_op jit(solution)/shard_map/all_gather | solution.py:224
  12.5 33.0 %copy-start.47 = (f32[384]{0:T(512)}, f32[384]{0:T(512)S(1)}, u32[]{:S(2)}) copy-start(f32[384]{0:T(512)S(1)} %broadcast_multiply_fusion.8) | copy-start | bytes 4612
  13.1 32.4 %copy-start.51 = (f32[384]{0:T(512)}, f32[384]{0:T(512)S(1)}, u32[]{:S(2)}) copy-start(f32[384]{0:T(512)S(1)} %add_rsqrt_fusion.1) | copy-start | bytes 4612
  13.3 28.3 %copy-start.43 = (f32[3,512]{1,0:T(4,128)}, f32[3,512]{1,0:T(4,128)S(1)}, u32[]{:S(2)}) copy-start(f32[3,512]{1,0:T(4,128)S(1)} %get-tuple-element.252) | copy-start | bytes 18436
  13.3 28.3 %copy-start.45 = (f32[3,512]{1,0:T(4,128)}, f32[3,512]{1,0:T(4,128)S(1)}, u32[]{:S(2)}) copy-start(f32[3,512]{1,0:T(4,128)S(1)} %get-tuple-element.253) | copy-start | bytes 18436
  13.4 28.2 %copy-start.55 = (pred[1536,3]{0,1:T(4,128)(4,1)}, pred[1536,3]{0,1:T(4,128)(4,1)S(1)}, u32[]{:S(2)}) copy-start(pred[1536,3]{0,1:T(4,128)(4,1)S(1)} %fusion.98) | copy-start | bytes 13828
  45.5 3.7 copy-start.3
  50.6 116.6 %all-gather.14.cloned.1.call-start = ((), (), s32[]{:S(2)}) async-start(), calls=%async_computation.11 | async-start | bytes 2359296 | tf_op jit(solution)/shard_map/all_gather | solution.py:205
  51.6 230.1 %reduce-scatter.11.cloned.1.call-start = ((), (), s32[]{:S(2)}) async-start(), calls=%async_computation.12 | async-start | bytes 7864320 | tf_op jit(solution)/shard_map/reduce_scatter | solution.py:236
  55.4 65.0 %copy-start.32 = (f32[1536,32]{0,1:T(8,128)}, f32[1536,32]{0,1:T(8,128)S(1)}, u32[]{:S(2)}) copy-start(f32[1536,32]{0,1:T(8,128)S(1)} %get-tuple-element.250) | copy-start | bytes 589828
  55.4 65.0 %copy-start.34 = (f32[1536,32]{0,1:T(8,128)}, f32[1536,32]{0,1:T(8,128)S(1)}, u32[]{:S(2)}) copy-start(f32[1536,32]{0,1:T(8,128)S(1)} %get-tuple-element.251) | copy-start | bytes 589828
  166.2 5.9 copy-start.14
  167.2 5.0 copy-start.26
  172.2 180.7 %all-gather.16.cloned.1.call-start = ((), (), s32[]{:S(2)}) async-start(), calls=%async_computation.13 | async-start | bytes 3932160 | tf_op jit(solution)/shard_map/all_gather | solution.py:245
  284.1 369.8 %copy-start.9 = (f32[384,1024]{1,0:T(8,128)}, f32[384,1024]{1,0:T(8,128)S(1)}, u32[]{:S(2)}) copy-start(f32[384,1024]{1,0:T(8,128)S(1)} %get-tuple-element.219) | copy-start | bytes 4718596
  284.1 369.8 %copy-start.49 = (f32[384]{0:T(512)}, f32[384]{0:T(512)S(1)}, u32[]{:S(2)}) copy-start(f32[384]{0:T(512)S(1)} %broadcast_multiply_fusion.7) | copy-start | bytes 4612
  284.4 369.5 %copy-start.53 = (f32[384]{0:T(512)}, f32[384]{0:T(512)S(1)}, u32[]{:S(2)}) copy-start(f32[384]{0:T(512)S(1)} %add_rsqrt_fusion) | copy-start | bytes 4612
  288.8 128.4 %all-gather.18.cloned.1.call-start = ((), (), s32[]{:S(2)}) async-start(), calls=%async_computation.15 | async-start | bytes 3932160 | tf_op jit(solution)/shard_map/all_gather | solution.py:225
  289.5 250.8 %reduce-scatter.15.cloned.1.call-start = ((), (), s32[]{:S(2)}) async-start(), calls=%async_computation.16 | async-start | bytes 7864320 | tf_op jit(solution)/shard_map/reduce_scatter | solution.py:266
  430.7 223.2 %reduce-scatter.13.cloned.1.call-start = ((), (), s32[]{:S(2)}) async-start(), calls=%async_computation.14 | async-start | bytes 7864320 | tf_op jit(solution)/shard_map/reduce_scatter | solution.py:251
  438.0 286.1 %all-gather.20.cloned.1.call-start = ((), (), s32[]{:S(2)}) async-start(), calls=%async_computation.17 | async-start | bytes 3932160 | tf_op jit(solution)/shard_map/all_gather | solution.py:276
  659.9 312.7 %reduce-scatter.17.cloned.1.call-start = ((), (), s32[]{:S(2)}) async-start(), calls=%async_computation.18 | async-start | bytes 7864320 | tf_op jit(solution)/shard_map/reduce_scatter | solution.py:303
  728.3 5.2 copy-start.1
  728.3 5.2 copy-start.4
  753.0 15.0 %copy-start.2 = (bf16[1536,4,64]{0,2,1:T(8,128)(2,1)S(1)}, bf16[1536,4,64]{0,2,1:T(8,128)(2,1)}, u32[]{:S(2)}) copy-start(bf16[1536,4,64]{0,2,1:T(8,128)(2,1)} %copy-done.1) | copy-start | bytes 2359300 | tf_op jit(solution)/shard_map/while
  753.0 15.0 %copy-start.5 = (bf16[1536,4,64]{0,2,1:T(8,128)(2,1)S(1)}, bf16[1536,4,64]{0,2,1:T(8,128)(2,1)}, u32[]{:S(2)}) copy-start(bf16[1536,4,64]{0,2,1:T(8,128)(2,1)} %copy-done.4) | copy-start | bytes 2359300 | tf_op jit(solution)/shard_map/while
  755.5 12.5 %copy-start.7 = (f32[1536,4,64]{0,2,1:T(8,128)}, f32[1536,4,64]{0,2,1:T(8,128)S(1)}, u32[]{:S(2)}) copy-start(f32[1536,4,64]{0,2,1:T(8,128)S(1)} %fusion.168) | copy-start | bytes 4718596 | tf_op jit(solution)/shard_map/while
  768.0 5.2 copy-start.1
  768.0 5.2 copy-start.4
  785.8 4.1 copy-start
  793.2 15.0 %copy-start.2 = (bf16[1536,4,64]{0,2,1:T(8,128)(2,1)S(1)}, bf16[1536,4,64]{0,2,1:T(8,128)(2,1)}, u32[]{:S(2)}) copy-start(bf16[1536,4,64]{0,2,1:T(8,128)(2,1)} %copy-done.1) | copy-start | bytes 2359300 | tf_op jit(solution)/shard_map/while
  793.2 15.0 %copy-start.5 = (bf16[1536,4,64]{0,2,1:T(8,128)(2,1)S(1)}, bf16[1536,4,64]{0,2,1:T(8,128)(2,1)}, u32[]{:S(2)}) copy-start(bf16[1536,4,64]{0,2,1:T(8,128)(2,1)} %copy-done.4) | copy-start | bytes 2359300 | tf_op jit(solution)/shard_map/while
  795.7 12.5 %copy-start.7 = (f32[1536,4,64]{0,2,1:T(8,128)}, f32[1536,4,64]{0,2,1:T(8,128)S(1)}, u32[]{:S(2)}) copy-start(f32[1536,4,64]{0,2,1:T(8,128)S(1)} %fusion.168) | copy-start | bytes 4718596 | tf_op jit(solution)/shard_map/while
  808.2 5.2 copy-start.1
  808.2 5.2 copy-start.4
  826.0 4.0 copy-start
  833.3 15.0 %copy-start.2 = (bf16[1536,4,64]{0,2,1:T(8,128)(2,1)S(1)}, bf16[1536,4,64]{0,2,1:T(8,128)(2,1)}, u32[]{:S(2)}) copy-start(bf16[1536,4,64]{0,2,1:T(8,128)(2,1)} %copy-done.1) | copy-start | bytes 2359300 | tf_op jit(solution)/shard_map/while
  833.4 15.0 %copy-start.5 = (bf16[1536,4,64]{0,2,1:T(8,128)(2,1)S(1)}, bf16[1536,4,64]{0,2,1:T(8,128)(2,1)}, u32[]{:S(2)}) copy-start(bf16[1536,4,64]{0,2,1:T(8,128)(2,1)} %copy-done.4) | copy-start | bytes 2359300 | tf_op jit(solution)/shard_map/while
  835.8 12.5 %copy-start.7 = (f32[1536,4,64]{0,2,1:T(8,128)}, f32[1536,4,64]{0,2,1:T(8,128)S(1)}, u32[]{:S(2)}) copy-start(f32[1536,4,64]{0,2,1:T(8,128)S(1)} %fusion.168) | copy-start | bytes 4718596 | tf_op jit(solution)/shard_map/while
  855.9 7.1 copy-start.41
  863.0 6.3 copy-start.27
  863.1 150.2 %reduce-scatter.25.cloned.1.call-start = ((), (), s32[]{:S(2)}) async-start(), calls=%async_computation.22 | async-start | bytes 655360
  863.1 6.3 copy-start.57
  870.4 103.8 %copy-start.13 = (bf16[384,1024]{1,0:T(8,128)(2,1)S(1)}, bf16[384,1024]{1,0:T(8,128)(2,1)}, u32[]{:S(2)}) copy-start(bf16[384,1024]{1,0:T(8,128)(2,1)} %param.21) | copy-start | bytes 2359300
  870.4 103.8 %copy-start.48 = (f32[384]{0:T(512)S(1)}, f32[384]{0:T(512)}, u32[]{:S(2)}) copy-start(f32[384]{0:T(512)} %copy-done.47) | copy-start | bytes 4612
  870.4 103.8 %copy-start.52 = (f32[384]{0:T(512)S(1)}, f32[384]{0:T(512)}, u32[]{:S(2)}) copy-start(f32[384]{0:T(512)} %copy-done.51) | copy-start | bytes 4612
  990.8 34.5 %reduce-scatter.23.cloned.1.call-start = ((), (), s32[]{:S(2)}) async-start(), calls=%async_computation.21 | async-start | bytes 4718592 | tf_op jit(solution)/shard_map/reduce_scatter | solution.py:333
  994.4 4.4 copy-start.39
  994.4 47.3 %reduce-scatter.19.cloned.1.call-start = ((), (), s32[]{:S(2)}) async-start(), calls=%async_computation.19 | async-start | bytes 7864320 | tf_op jit(solution)/shard_map/reduce_scatter | solution.py:330
  994.4 4.4 copy-start.40
  994.4 4.4 copy-start.42
  994.4 4.4 copy-start.56
  1004.3 10.1 copy-start.44
  1004.3 10.1 copy-start.46
  1004.4 54.6 %reduce-scatter.21.cloned.1.call-start = ((), (), s32[]{:S(2)}) async-start(), calls=%async_computation.20 | async-start | bytes 9437184 | tf_op jit(solution)/shard_map/reduce_scatter | solution.py:328
  1019.7 204.4 %all-reduce.3.cloned.1.call-start = ((), (), s32[]{:S(2)}) async-start(), calls=%async_computation.23 | async-start | bytes 14680064 | tf_op jit(solution)/shard_map/psum | solution.py:345
  1224.1 5.4 copy-start.19
  1224.1 5.4 copy-start.30
  1224.1 6.4 copy-start.31
  1230.6 4.7 copy-start.15
  1230.6 5.5 copy-start.28
  1230.6 6.5 copy-start.29
  (27 other events, 58.2 us)
Sparse Core Ops, SparseCore 0:
  10.7 14.8 all-gather.7
  27.7 12.5 all-gather.11
  50.7 64.3 all-gather.9
  117.0 8.4 all-gather.13
  172.3 109.4 reduce-scatter.10
  288.9 63.9 all-gather.15
  355.0 62.0 all-gather.17
  430.8 109.4 reduce-scatter.14
  542.6 111.2 reduce-scatter.12
  660.1 63.9 all-gather.19
  863.2 109.3 reduce-scatter.16
  990.9 22.2 reduce-scatter.24
  1016.1 9.1 reduce-scatter.22
  1027.5 14.1 reduce-scatter.18
  1043.8 15.1 reduce-scatter.20
  1067.3 156.7 all-reduce.2
where the time goes:
time: 1260 us; the launch traced here: 1250 us
  waiting for transfers between devices  868 us (69%)
  matrix products  153 us (12%)
  other arithmetic  99.5 us (8%)
  local copies, waits for them, and re-layouts  84.9 us (7%)
  between operations  16 us (1%)
  blocking collectives  13.6 us (1%)
    psum x1, waiting for transfers between devices, per_device(): lax.psum((col_diff, mod_diff, row_diff), 'group')  152 us
    reduce_scatter x1, waiting for transfers between devices, per_device(): lax.psum_scatter(jnp.einsum('fcj,cdj->fd', piece, row_low[1:3], preferred...  111 us
    reduce_scatter x1, waiting for transfers between devices, per_device(): lax.psum_scatter(jnp.einsum('fj,dj->fd', piece, row_low[0], preferred_ele...  109 us
    reduce_scatter x1, waiting for transfers between devices, per_device(): lax.psum_scatter(jnp.einsum('fcj,dcj->fd', piece, col_low[:, 3:5], prefer...  102 us
    reduce_scatter x1, waiting for transfers between devices, per_device(): lax.psum_scatter(jnp.einsum('fcj,dcj->fd', piece, col_low[:, 0:3], prefer...  102 us
    all_gather x1, waiting for transfers between devices, per_device(): grad_attn_full = lax.all_gather(grad_attn, 'tensor', axis=0, tiled=True)  64 us
    all_gather x1, waiting for transfers between devices, per_device(): ffn_full = lax.all_gather(ffn_in, 'tensor', axis=0, tiled=True)  63.3 us
    all_gather x1, waiting for transfers between devices, per_device(): lax.all_gather(att_in, 'tensor', axis=0, tiled=True)  59.6 us
  transfers between devices with their start and end apart: 16, of which 14 were waited for; matrix products, arithmetic and copies ran while one was open for 10% of the time, Pallas kernels for 0%

commit v1 on v0

--- a/solution.py
+++ b/solution.py
@@ -174,6 +174,92 @@
 def outer_step(average, outer, weights):
     outer_new = outer_beta * outer + average
     return (outer_new, weights - outer_rate * (average + outer_beta * outer_new))
+
+
+def shifted(values, axis, step):
+    size = lax.axis_size(axis)
+    return lax.ppermute(values, axis, [(i, (i + step) % size) for i in range(size)])
+
+
+def ring_gather(own):
+    half = own.shape[-2] // 2
+    third = shifted(own, "tensor", 1)
+    first = shifted(own, "tensor", -1)
+    low = shifted(third[..., :half, :], "tensor", 1)
+    high = shifted(first[..., half:, :], "tensor", -1)
+    return [own, first, jnp.concatenate([low, high], axis=-2), third]
+
+
+def ring_scatter(blocks):
+    half = blocks[0].shape[-2] // 2
+    low_bits = jnp.bfloat16
+    low = shifted(blocks[2][..., :half, :].astype(low_bits), "tensor", 1)
+    high = shifted(blocks[2][..., half:, :].astype(low_bits), "tensor", -1)
+    rightward = jnp.concatenate(
+        [blocks[1][..., :half, :] + low.astype(jnp.float32), blocks[1][..., half:, :].astype(jnp.float32)], axis=-2
+    ).astype(low_bits)
+    leftward = jnp.concatenate(
+        [blocks[3][..., :half, :].astype(jnp.float32), blocks[3][..., half:, :] + high.astype(jnp.float32)], axis=-2
+    ).astype(low_bits)
+    return (
+        blocks[0].astype(jnp.float32)
+        + shifted(rightward, "tensor", 1).astype(jnp.float32)
+        + shifted(leftward, "tensor", -1).astype(jnp.float32)
+    )
+
+
+def exchange(blocks):
+    got = [blocks[0]]
+    for r in range(1, 4):
+        got.append(shifted(blocks[4 - r], "tensor", 4 - r))
+    return got
+
+
+def in_order(pieces, axis):
+    me = lax.axis_index("tensor")
+    width = pieces[0].shape[axis]
+    shape = list(pieces[0].shape)
+    shape[axis] = 4 * width
+    out = jnp.zeros(shape, pieces[0].dtype)
+    for r in range(4):
+        out = lax.dynamic_update_slice_in_dim(out, pieces[r], (me + r) % 4 * width, axis)
+    return out
+
+
+def dp_gather(own, axis):
+    if lax.axis_size("dp") != 2:
+        return lax.all_gather(own, "dp", axis=axis, tiled=True)
+    other = shifted(own, "dp", 1)
+    first = lax.axis_index("dp") == 0
+    return jnp.concatenate([jnp.where(first, own, other), jnp.where(first, other, own)], axis=axis)
+
+
+def dp_share(product, whole):
+    parts = lax.axis_size("dp")
+    width = whole.shape[1] // parts
+    me = lax.axis_index("dp")
+    if parts != 2:
+        return lax.psum_scatter(
+            product(whole), "dp", scatter_dimension=product.split, tiled=True
+        )
+    away = product(lax.dynamic_slice_in_dim(whole, (1 - me) * width, width, 1)).astype(jnp.bfloat16)
+    here = product(lax.dynamic_slice_in_dim(whole, me * width, width, 1))
+    return here + shifted(away, "dp", 1).astype(jnp.float32)
+
+
+class Product:
+    def __init__(self, form, other, split):
+        self.form, self.other, self.split = form, other, split
+
+    def __call__(self, whole):
+        return jnp.einsum(self.form, whole, self.other, preferred_element_type=jnp.float32)
+
+
+def pick(onehot, rows):
+    out = onehot[:, 0:1] * rows[0]
+    for u in range(1, rows.shape[0]):
+        out = out + onehot[:, u : u + 1] * rows[u]
+    return out
 
 
 def per_device(
@@ -195,92 +281,94 @@
     mod_outer,
     row_outer,
 ):
-    tensor_parts = lax.axis_size("tensor")
     group_count = lax.axis_size("group")
+    packs_here = lax.axis_size("dp")
     own_rows, model_width = features.shape
-    frames = own_rows * tensor_parts
-    first_row = lax.axis_index("tensor") * own_rows
-    col_low, row_low = (
-        lax.all_gather(col_weights.astype(jnp.bfloat16), "dp", axis=0, tiled=True),
-        lax.all_gather(row_weights.astype(jnp.bfloat16), "dp", axis=1, tiled=True),
-    )
+    frames = own_rows * 4
+    me = lax.axis_index("tensor")
+    core = lax.axis_index("dp")
+    first_row = me * own_rows
+    low = jnp.bfloat16
+    utterances = buckets.shape[1]
+    share = mod_weights.shape[0]
+
+    feature_pieces = ring_gather(features)
+    col_low = col_weights.astype(low)
+    qkv_low = dp_gather(col_low[:, 0:3], 0)
+    wide_low = jnp.concatenate([row_weights.astype(low), jnp.moveaxis(col_low[:, 3:5], 1, 0)], axis=0)
+
+    buckets_all = lax.all_gather(buckets[0], "dp", axis=0, tiled=True) if packs_here != 2 else None
+    if buckets_all is None:
+        away = shifted(buckets[0], "dp", 1)
+        buckets_all = jnp.where(core == 0, jnp.concatenate([buckets[0], away]), jnp.concatenate([away, buckets[0]]))
+    flow_time = ((lax.axis_index("group") * NBUCK + buckets_all).astype(jnp.float32) + 0.5) / (
+        NBUCK * group_count
+    )
+    condition_all = jax.nn.silu(time_embedding(flow_time, model_width)).astype(low)
+    condition_here = lax.dynamic_slice_in_dim(condition_all, core * share, share, 1)
+    mod_terms = jnp.einsum("ud,dcj->ucj", condition_here, mod_weights.astype(low), preferred_element_type=jnp.float32)
+    if packs_here != 2:
+        mod_part = lax.psum_scatter(mod_terms, "dp", scatter_dimension=0, tiled=True)
+    else:
+        mod_away = lax.dynamic_slice_in_dim(mod_terms, (1 - core) * utterances, utterances, 0)
+        mod_part = lax.dynamic_slice_in_dim(mod_terms, core * utterances, utterances, 0) + shifted(mod_away, "dp", 1)
+    modulation = in_order([mod_part] + [shifted(mod_part, "tensor", -r) for r in range(1, 4)], 2)
+
     onehot_all, position, same_segment = pack_geometry(frame_counts[0], frames)
     onehot_own = lax.dynamic_slice_in_dim(onehot_all, first_row, own_rows, 0)
     cosine, sine_part = rotary_tables(position, HEAD_DIM)
-    flow_time = ((lax.axis_index("group") * NBUCK + buckets[0]).astype(jnp.float32) + 0.5) / (
-        NBUCK * group_count
-    )
-    condition = jax.nn.silu(time_embedding(flow_time, model_width)).astype(jnp.bfloat16)
-    mod_low = lax.all_gather(mod_weights.astype(jnp.bfloat16), "dp", axis=0, tiled=True)
-    mod_part = jnp.einsum("ud,dcj->ucj", condition, mod_low, preferred_element_type=jnp.float32)
-    modulation = lax.all_gather(mod_part, "tensor", axis=2, tiled=True)
-    per_row = jnp.einsum("fu,ucj->fcj", onehot_own, modulation, precision=highest)
+    features_full = in_order(feature_pieces, 0)
+    normed_full, _ = normalize(features_full.astype(jnp.float32))
+    att_full = (
+        normed_full * (1.0 + pick(onehot_all, modulation[:, 1])) + pick(onehot_all, modulation[:, 0])
+    ).astype(low)
+    projected = jnp.einsum("fd,dcj->fcj", att_full, qkv_low, preferred_element_type=jnp.float32)
+    head_rows = projected.reshape(frames, 3, -1, HEAD_DIM)
+    queries = rotate(head_rows[:, 0], cosine, sine_part).astype(low)
+    key_rows = rotate(head_rows[:, 1], cosine, sine_part).astype(low)
+    value_rows = head_rows[:, 2].astype(low)
+    mixed_rows, log_totals = attend(queries, key_rows, value_rows, same_segment)
+
+    wide_pieces = ring_gather(wide_low)
+    wide_full = dp_gather(jnp.concatenate(wide_pieces, axis=2), 1)
+    out_low, down_low, up_low = (wide_full[0], wide_full[1:3], wide_full[3:5])
+
+    def rows_of(values, r):
+        return lax.dynamic_slice_in_dim(values, (me + r) % 4 * own_rows, own_rows, 0)
+
+    mixed_own = jnp.concatenate(exchange([rows_of(mixed_rows, r) for r in range(4)]), axis=1)
+    per_row = [pick(onehot_own, modulation[:, c]) for c in range(6)]
     features_in = features.astype(jnp.float32)
     grad_output = cotangent.astype(jnp.float32)
     normed, inverse_scale = normalize(features_in)
-    att_in = (normed * (1.0 + per_row[:, 1]) + per_row[:, 0]).astype(jnp.bfloat16)
-    grad_ffn = (grad_output * per_row[:, 5]).astype(jnp.bfloat16)
-    att_full, grad_ffn_full = (
-        lax.all_gather(att_in, "tensor", axis=0, tiled=True),
-        lax.all_gather(grad_ffn, "tensor", axis=0, tiled=True),
-    )
-    projected = jnp.einsum(
-        "fd,dcj->fcj", att_full, col_low[:, 0:3], preferred_element_type=jnp.float32
-    )
-    head_rows = projected.reshape(frames, 3, -1, HEAD_DIM)
-    queries = rotate(head_rows[:, 0], cosine, sine_part).astype(jnp.bfloat16)
-    key_rows = rotate(head_rows[:, 1], cosine, sine_part).astype(jnp.bfloat16)
-    value_rows = head_rows[:, 2].astype(jnp.bfloat16)
-    mixed_rows, log_totals = attend(queries, key_rows, value_rows, same_segment)
-    piece = mixed_rows
-    attn_out = lax.psum_scatter(
-        jnp.einsum("fj,dj->fd", piece, row_low[0], preferred_element_type=jnp.float32),
-        "tensor",
-        scatter_dimension=0,
-        tiled=True,
-    )
-    residual = features_in + per_row[:, 2] * attn_out
+    grad_ffn = (grad_output * per_row[5]).astype(low)
+    attn_out = jnp.einsum("fj,dj->fd", mixed_own, out_low, preferred_element_type=jnp.float32)
+    residual = features_in + per_row[2] * attn_out
     normed_two, inverse_two = normalize(residual)
-    ffn_in = (normed_two * (1.0 + per_row[:, 4]) + per_row[:, 3]).astype(jnp.bfloat16)
-    ffn_full = lax.all_gather(ffn_in, "tensor", axis=0, tiled=True)
-    upward = jnp.einsum(
-        "fd,dcj->fcj", ffn_full, col_low[:, 3:5], preferred_element_type=jnp.float32
-    )
-    hidden = jax.nn.gelu(upward, approximate=True).astype(jnp.bfloat16)
-    piece = hidden
-    ffn_out = lax.psum_scatter(
-        jnp.einsum("fcj,cdj->fd", piece, row_low[1:3], preferred_element_type=jnp.float32),
-        "tensor",
-        scatter_dimension=0,
-        tiled=True,
-    )
-    output = (residual + per_row[:, 5] * ffn_out).astype(jnp.bfloat16)
-    grad_hidden = jnp.einsum(
-        "fd,cdj->fcj", grad_ffn_full, row_low[1:3], preferred_element_type=jnp.float32
-    )
+    ffn_in = (normed_two * (1.0 + per_row[4]) + per_row[3]).astype(low)
+    upward = jnp.einsum("fd,cdj->fcj", ffn_in, up_low, preferred_element_type=jnp.float32)
+    hidden = jax.nn.gelu(upward, approximate=True).astype(low)
+    ffn_out = jnp.einsum("fcj,cdj->fd", hidden, down_low, preferred_element_type=jnp.float32)
+    output = (residual + per_row[5] * ffn_out).astype(low)
+    grad_hidden = jnp.einsum("fd,cdj->fcj", grad_ffn, down_low, preferred_element_type=jnp.float32)
     gelu_pull = jax.vjp(partial(jax.nn.gelu, approximate=True), upward)[1]
-    grad_upward = gelu_pull(grad_hidden)[0].astype(jnp.bfloat16)
-    down_grad = jnp.einsum("fcj,fd->cdj", hidden, grad_ffn_full, preferred_element_type=jnp.float32)
-    up_grad = jnp.einsum("fd,fcj->dcj", ffn_full, grad_upward, preferred_element_type=jnp.float32)
-    piece = grad_upward
-    grad_ffn_in = lax.psum_scatter(
-        jnp.einsum("fcj,dcj->fd", piece, col_low[:, 3:5], preferred_element_type=jnp.float32),
-        "tensor",
-        scatter_dimension=0,
-        tiled=True,
-    )
+    grad_upward = gelu_pull(grad_hidden)[0].astype(low)
+    grad_ffn_in = jnp.einsum("fcj,cdj->fd", grad_upward, up_low, preferred_element_type=jnp.float32)
     grad_residual = grad_output + normalize_back(
-        grad_ffn_in * (1.0 + per_row[:, 4]), normed_two, inverse_two
-    )
-    grad_attn = (grad_residual * per_row[:, 2]).astype(jnp.bfloat16)
-    grad_attn_full = lax.all_gather(grad_attn, "tensor", axis=0, tiled=True)
-    grad_mixed = jnp.einsum(
-        "fd,dj->fj", grad_attn_full, row_low[0], preferred_element_type=jnp.float32
-    ).astype(jnp.bfloat16)
-    out_grad = jnp.einsum(
-        "fj,fd->dj", mixed_rows, grad_attn_full, preferred_element_type=jnp.float32
-    )
-    row_grad = jnp.concatenate([out_grad[None], down_grad], axis=0)
+        grad_ffn_in * (1.0 + per_row[4]), normed_two, inverse_two
+    )
+    grad_attn = (grad_residual * per_row[2]).astype(low)
+    grad_mixed_own = jnp.einsum("fd,dj->fj", grad_attn, out_low, preferred_element_type=jnp.float32).astype(low)
+    width = grad_mixed_own.shape[1] // 4
+    grad_mixed = in_order(exchange([grad_mixed_own[:, r * width : (r + 1) * width] for r in range(4)]), 0)
+
+    down_share = dp_share(Product("fd,fcj->cdj", hidden, 1), grad_ffn)
+    up_share = dp_share(Product("fd,fcj->cdj", grad_upward, 1), ffn_in)
+    out_share = dp_share(Product("fd,fj->dj", mixed_own, 0), grad_attn)
+    wide_share = jnp.concatenate([out_share[None], down_share, up_share], axis=0)
+    wide_grad = ring_scatter([wide_share[:, :, r * width : (r + 1) * width] for r in range(4)])
+    row_share = wide_grad[0:3]
+
     grad_queries, grad_keys, grad_values = attend_back(
         queries, key_rows, value_rows, same_segment, log_totals, grad_mixed
     )
@@ -294,20 +382,15 @@
             axis=1,
         )
         .reshape(frames, 3, -1)
-        .astype(jnp.bfloat16)
-    )
-    qkv_grad = jnp.einsum(
-        "fd,fcj->dcj", att_full, grad_projected, preferred_element_type=jnp.float32
-    )
-    piece = grad_projected
-    grad_att_in = lax.psum_scatter(
-        jnp.einsum("fcj,dcj->fd", piece, col_low[:, 0:3], preferred_element_type=jnp.float32),
-        "tensor",
-        scatter_dimension=0,
-        tiled=True,
-    )
+        .astype(low)
+    )
+    grad_att_full = jnp.einsum("fcj,dcj->fd", grad_projected, qkv_low, preferred_element_type=jnp.float32)
+    grad_att_in = ring_scatter([rows_of(grad_att_full, r) for r in range(4)])
+    qkv_share = dp_share(Product("fd,fcj->dcj", grad_projected, 0), att_full)
+    col_share = jnp.concatenate([qkv_share, jnp.moveaxis(wide_grad[3:5], 0, 1)], axis=1)
+
     grad_features = grad_residual + normalize_back(
-        grad_att_in * (1.0 + per_row[:, 1]), normed, inverse_scale
+        grad_att_in * (1.0 + per_row[1]), normed, inverse_scale
     )
     mod_rows = jnp.stack(
         [
@@ -321,31 +404,34 @@
         axis=1,
     )
     mod_sums = jnp.einsum("fu,fcj->ucj", onehot_own, mod_rows, precision=highest)
-    mod_columns = lax.psum_scatter(mod_sums, "tensor", scatter_dimension=2, tiled=True)
-    mod_grad = jnp.einsum(
-        "ud,ucj->dcj", condition.astype(jnp.float32), mod_columns, precision=highest
-    )
-    mod_share = lax.psum_scatter(mod_grad, "dp", scatter_dimension=0, tiled=True)
-    col_share, row_share = (
-        lax.psum_scatter(
-            jnp.concatenate([qkv_grad, up_grad], axis=1), "dp", scatter_dimension=0, tiled=True
-        ),
-        lax.psum_scatter(row_grad, "dp", scatter_dimension=1, tiled=True),
-    )
+    mod_mine = [lax.dynamic_slice_in_dim(mod_sums, (me + r) % 4 * width, width, 2) for r in range(4)]
+    mod_columns = sum(exchange(mod_mine))
+    if packs_here != 2:
+        mod_columns_all = lax.all_gather(mod_columns, "dp", axis=0, tiled=True)
+    else:
+        columns_away = shifted(mod_columns, "dp", 1)
+        mod_columns_all = jnp.where(
+            core == 0,
+            jnp.concatenate([mod_columns, columns_away]),
+            jnp.concatenate([columns_away, mod_columns]),
+        )
+    mod_share = jnp.einsum(
+        "ud,ucj->dcj", condition_here.astype(jnp.float32), mod_columns_all, precision=highest
+    )
+
     steps_done = step_count[0].astype(jnp.float32)
+    row_first_new, row_second_new, row_diff = inner_step(
+        row_share, row_first[0], row_second[0], row_weights, steps_done
+    )
     col_first_new, col_second_new, col_diff = inner_step(
         col_share, col_first[0], col_second[0], col_weights, steps_done
     )
     mod_first_new, mod_second_new, mod_diff = inner_step(
         mod_share, mod_first[0], mod_second[0], mod_weights, steps_done
     )
-    row_first_new, row_second_new, row_diff = inner_step(
-        row_share, row_first[0], row_second[0], row_weights, steps_done
-    )
-    col_total, mod_total, row_total = lax.psum((col_diff, mod_diff, row_diff), "group")
-    col_average = col_total / group_count
-    mod_average = mod_total / group_count
-    row_average = row_total / group_count
+    row_average = lax.psum(row_diff.astype(low), "group").astype(jnp.float32) / group_count
+    col_average = lax.psum(col_diff.astype(low), "group").astype(jnp.float32) / group_count
+    mod_average = lax.psum(mod_diff.astype(low), "group").astype(jnp.float32) / group_count
     col_outer_new, col_new = outer_step(col_average, col_outer, col_weights)
     mod_outer_new, mod_new = outer_step(mod_average, mod_outer, mod_weights)
     row_outer_new, row_new = outer_step(row_average, row_outer, row_weights)

time: 1260 us -> 785 us (0.62)
  waiting for transfers between devices: 868 us -> 309 us
  starting transfers between devices: 1.12 us -> 49.7 us
  local copies, waits for them, and re-layouts: 84.9 us -> 112 us
  other arithmetic: 99.5 us -> 117 us
  blocking collectives: 13.6 us -> 0 us
    reduce_scatter x7 -> x0, waiting for transfers between devices: 449 us -> none  [the longest x1 111 us: per_device(): lax.psum_scatter(jnp.einsum('fcj,cdj->fd', piece, row_low[1:3], preferred...]
    all_gather x7 -> x0, waiting for transfers between devices: 258 us -> none  [the longest x1 64 us: per_device(): grad_attn_full = lax.all_gather(grad_attn, 'tensor', axis=0, tiled=True)]
    ppermute x0 -> x37, waiting for transfers between devices: none -> 222 us  [shifted(): lax.ppermute(values, axis, [(i, (i + step) % size) for i in range(size)])]
    psum x1, waiting for transfers between devices: 152 us -> 87.1 us  [per_device(): lax.psum(col_diff.astype(low), 'group').astype(jnp.float32) / group_count]
    ppermute x0 -> x37, starting transfers between devices: none -> 49.7 us  [shifted(): lax.ppermute(values, axis, [(i, (i + step) % size) for i in range(size)])]
    dot_general x15 -> x18, matrix products: 72.2 us -> 53.1 us  [the longest x8 22.6 us: __call__(): jnp.einsum(self.form, whole, self.other, preferred_element_type=jnp.float32)]
    slice x0 -> x11, local copies, waits for them, and re-layouts: none -> 14.5 us  [the longest x3 4.68 us: pick(): out = onehot[:, 0:1] * rows[0]]
    all_gather x1 -> x0, blocking collectives: 13.6 us -> none  [per_device(): modulation = lax.all_gather(mod_part, 'tensor', axis=2, tiled=True)]
  transfers between devices with their start and end apart: 16 -> 38, of which waited for: 14 -> 18; matrix products, arithmetic and copies ran while one was open for 10% -> 41% of each run, Pallas kernels for 0% -> 0%
where the time goes in v1:
time: 785 us; the launch traced here: 778 us
  waiting for transfers between devices  309 us (39%)
  matrix products  161 us (21%)
  other arithmetic  117 us (15%)
  local copies, waits for them, and re-layouts  112 us (14%)
  starting transfers between devices  49.7 us (6%)
  between operations  16.8 us (2%)
  loops' own time  11.1 us (1%)
    ppermute x37, waiting for transfers between devices, shifted(): lax.ppermute(values, axis, [(i, (i + step) % size) for i in range(size)])  222 us
    psum x1, waiting for transfers between devices, per_device(): lax.psum(col_diff.astype(low), 'group').astype(jnp.float32) / group_count  87.1 us
    ppermute x37, starting transfers between devices, shifted(): lax.ppermute(values, axis, [(i, (i + step) % size) for i in range(size)])  49.7 us
    dynamic_update_slice x6, local copies, waits for them, and re-layouts, attend_back(): lax.scan(block_grads, (zeros, zeros), (begins, log_totals))  34.9 us
    dot_general x3, matrix products, block_grads(): jnp.einsum('hqk,qhd->khd', probs.astype(jnp.bfloat16), grad_block, prefer...  23.8 us
    dot_general x8, matrix products, __call__(): jnp.einsum(self.form, whole, self.other, preferred_element_type=jnp.float32)  22.6 us
    unnamed x248, local copies, waits for them, and re-layouts  18.4 us
    dot_general x3, matrix products, block_grads(): jnp.einsum('qhd,khd->hqk', query_block, key_rows, preferred_element_type=...  17.8 us
  transfers between devices with their start and end apart: 38, of which 18 were waited for; matrix products, arithmetic and copies ran while one was open for 41% of the time, Pallas kernels for 0%

profile of v1, /device:TPU:0, one launch (start us, length us, event | category | flops | bytes accessed | tf_op | source)
XLA Modules:
  0.0 777.8 jit_solution(16864473916120046465)
XLA Ops:
  9.5 5.1 collective-permute-start.5
  38.5 3.8 collective-permute-start.2
  44.3 33.8 %collective-permute-done.2 = f32[3,6,256]{2,0,1:T(4,128)} collective-permute-done((f32[3,6,256]{2,0,1:T(4,128)}, f32[3,6,256]{2,0,1:T(4,128)}, u32[]{:S(2)}, u32[]{:S(2)}) %collective-permute-start.2) | collective-permute-done | bytes 18464 | tf_op jit(solution)/shard_map/ppermute | solution.py:181
  84.7 4.4 collective-permute-done.4
  95.9 3.6 collective-permute-start.8
  102.2 29.6 %collective-permute-done.7 = bf16[192,1024]{0,1:T(8,128)(2,1)S(1)} collective-permute-done((bf16[192,1024]{0,1:T(8,128)(2,1)S(1)}, bf16[192,1024]{0,1:T(8,128)(2,1)S(1)}, u32[]{:S(2)}, u32[]{:S(2)}) %collective-permute-start.7) | collective-permute-done | bytes 393248 | tf_op jit(solution)/shard_map/ppermute | solution.py:181
  131.8 8.5 %collective-permute-done.8 = bf16[192,1024]{0,1:T(8,128)(2,1)S(1)} collective-permute-done((bf16[192,1024]{0,1:T(8,128)(2,1)S(1)}, bf16[192,1024]{0,1:T(8,128)(2,1)S(1)}, u32[]{:S(2)}, u32[]{:S(2)}) %collective-permute-start.8) | collective-permute-done | bytes 393248 | tf_op jit(solution)/shard_map/ppermute | solution.py:181
  143.3 4.4 fusion.36
  152.6 4.1 collective-permute-start.16
  157.7 14.2 %collective-permute-done.15 = bf16[5,256,256]{2,1,0:T(8,128)(2,1)S(1)} collective-permute-done((bf16[5,256,256]{2,1,0:T(8,128)(2,1)S(1)}, bf16[5,256,256]{2,1,0:T(8,128)(2,1)S(1)}, u32[]{:S(2)}, u32[]{:S(2)}) %collective-permute-start.15) | collective-permute-done | bytes 655392 | tf_op jit(solution)/shard_map/ppermute | solution.py:181
  171.9 8.6 %collective-permute-done.16 = bf16[5,256,256]{2,1,0:T(8,128)(2,1)S(1)} collective-permute-done((bf16[5,256,256]{2,1,0:T(8,128)(2,1)S(1)}, bf16[5,256,256]{2,1,0:T(8,128)(2,1)S(1)}, u32[]{:S(2)}, u32[]{:S(2)}) %collective-permute-start.16) | collective-permute-done | bytes 655392 | tf_op jit(solution)/shard_map/ppermute | solution.py:181
  180.5 5.9 pad_maximum_fusion.1
  186.4 51.3 %while.27 = (s32[]{:T(128)}, bf16[3,512,4,64]{1,3,2,0:T(8,128)(2,1)}, f32[3,4,512]{2,1,0:T(4,128)}, s32[3]{0:T(128)S(1)}, pred[1536,1536]{1,0:T(8,128)(4,1)}, /*...) while((s32[]{:T(128)}, ...), condition=%wide.region_8.9_spmd, body=%wide.region_5.8_spmd.sunk | while | flops 843184128 | bytes 43844768 | solution.py:109
  190.6 3.6 fusion.187
  194.2 3.5 fusion.188
  198.4 5.1 fusion.189
  207.7 3.6 fusion.187
  211.3 3.5 fusion.188
  215.5 5.1 fusion.189
  224.8 3.6 fusion.187
  232.6 5.1 fusion.189
  244.6 6.0 broadcast_select_fusion.1
  250.9 9.3 %collective-permute-done.11 = bf16[384,256]{0,1:T(8,128)(2,1)S(1)} collective-permute-done((bf16[384,256]{0,1:T(8,128)(2,1)S(1)}, bf16[384,256]{0,1:T(8,128)(2,1)S(1)}, u32[]{:S(2)}, u32[]{:S(2)}) %collective-permute-start.11) | collective-permute-done | bytes 196640 | tf_op jit(solution)/shard_map/ppermute | solution.py:181
  260.5 3.6 fusion.146
  272.8 3.7 fusion.43
  292.4 12.2 %collective-permute-done.19 = bf16[384,256]{1,0:T(8,128)(2,1)S(1)} collective-permute-done((bf16[384,256]{1,0:T(8,128)(2,1)}, bf16[384,256]{1,0:T(8,128)(2,1)S(1)}, u32[]{:S(2)}, u32[]{:S(2)}) %collective-permute-start.19) | collective-permute-done | bytes 196640 | tf_op jit(solution)/shard_map/ppermute | solution.py:181
  307.7 149.2 %while.28 = (s32[]{:T(128)}, f32[1536,4,64]{0,2,1:T(8,128)}, f32[1536,4,64]{0,2,1:T(8,128)}, f32[3,512,4,64]{1,0,3,2:T(4,128)}, s32[3]{0:T(128)S(1)}, /*index=5*...) while((s32[]{:T(128)}, f32[1536,4,64]{0,2,1:T(8,128)}, ...), condition=%wide.region_17.18_spmd.clone, body=%wide.region_15.17_spmd.clone.sunk | while | flops 2043672576 | bytes 184590784 | solution.py:158
  316.1 6.0 multiply_reduce_fusion.4
  322.1 4.5 multiply_convert_fusion.11
  328.5 4.9 fusion.202
  334.0 11.1 %dynamic_update_slice.80 = f32[3,512,4,64]{1,0,3,2:T(4,128)} dynamic-update-slice(f32[3,512,4,64]{1,0,3,2:T(4,128)} %get-tuple-element.490, f32[1,512,4,64]{1,0,3,2:T(1,128)S(1)} %copy.97, s32[]{:T(128)} %get-tuple-element.487, s32[]{:T(128)} %constant.202.clone.1..sunk.1, s32[]{:T(128)} %constant.202.clone.1..sunk.1, s32[]{:T(128)} %constant.202.clone.1..sunk.1) | dynamic-update-slice | bytes 1048580 | tf_op jit(solution)/shard_map/while/body/jit(dynamic_update_index_in_dim)/dynamic_update_slice | solution.py:158
  345.1 4.3 fusion.200
  349.4 7.7 fusion.201
  365.6 5.9 multiply_reduce_fusion.4
  371.6 4.5 multiply_convert_fusion.11
  378.0 4.9 fusion.202
  383.5 11.1 %dynamic_update_slice.80 = f32[3,512,4,64]{1,0,3,2:T(4,128)} dynamic-update-slice(f32[3,512,4,64]{1,0,3,2:T(4,128)} %get-tuple-element.490, f32[1,512,4,64]{1,0,3,2:T(1,128)S(1)} %copy.97, s32[]{:T(128)} %get-tuple-element.487, s32[]{:T(128)} %constant.202.clone.1..sunk.1, s32[]{:T(128)} %constant.202.clone.1..sunk.1, s32[]{:T(128)} %constant.202.clone.1..sunk.1) | dynamic-update-slice | bytes 1048580 | tf_op jit(solution)/shard_map/while/body/jit(dynamic_update_index_in_dim)/dynamic_update_slice | solution.py:158
  394.6 4.3 fusion.200
  398.9 8.1 %fusion.201 = f32[1536,4,64]{0,2,1:T(8,128)} fusion(f32[4,512,1536]{2,1,0:T(8,128)} %copy-done, f32[1536,4,64]{0,2,1:T(8,128)} %get-tuple-element.489, pred[]{:T(512)S(6)} %compare.7, bf16[1536,4,64]{0,2,1:T(8,128)(2,1)} %get-tuple-element.510, s32[]{:T(128)S(6)} %select_n.283), kind=kOutput, calls=%fused_computation.25.clone.1 | convolution fusion | flops 406585344 | bytes 15990789 | tf_op jit(solution)/shard_map/while/body/eval_jaxpr/hqk,qhd->khd/dot_general | solution.py:148
  415.5 5.9 multiply_reduce_fusion.4
  421.4 4.5 multiply_convert_fusion.11
  427.9 4.9 fusion.202
  433.4 11.1 %dynamic_update_slice.80 = f32[3,512,4,64]{1,0,3,2:T(4,128)} dynamic-update-slice(f32[3,512,4,64]{1,0,3,2:T(4,128)} %get-tuple-element.490, f32[1,512,4,64]{1,0,3,2:T(1,128)S(1)} %copy.97, s32[]{:T(128)} %get-tuple-element.487, s32[]{:T(128)} %constant.202.clone.1..sunk.1, s32[]{:T(128)} %constant.202.clone.1..sunk.1, s32[]{:T(128)} %constant.202.clone.1..sunk.1) | dynamic-update-slice | bytes 1048580 | tf_op jit(solution)/shard_map/while/body/jit(dynamic_update_index_in_dim)/dynamic_update_slice | solution.py:158
  444.5 4.3 fusion.200
  448.8 8.1 %fusion.201 = f32[1536,4,64]{0,2,1:T(8,128)} fusion(f32[4,512,1536]{2,1,0:T(8,128)} %copy-done, f32[1536,4,64]{0,2,1:T(8,128)} %get-tuple-element.489, pred[]{:T(512)S(6)} %compare.7, bf16[1536,4,64]{0,2,1:T(8,128)(2,1)} %get-tuple-element.510, s32[]{:T(128)S(6)} %select_n.283), kind=kOutput, calls=%fused_computation.25.clone.1 | convolution fusion | flops 406585344 | bytes 15990789 | tf_op jit(solution)/shard_map/while/body/eval_jaxpr/hqk,qhd->khd/dot_general | solution.py:148
  465.3 4.3 convolution_bitcast_fusion
  469.9 3.8 collective-permute-start.23
  475.5 8.1 %collective-permute-done.21 = bf16[192,1024]{1,0:T(8,128)(2,1)S(1)} collective-permute-done((bf16[192,1024]{1,0:T(8,128)(2,1)S(1)}, bf16[192,1024]{1,0:T(8,128)(2,1)S(1)}, u32[]{:S(2)}, u32[]{:S(2)}) %collective-permute-start.21) | collective-permute-done | bytes 393248 | tf_op jit(solution)/shard_map/ppermute | solution.py:181
  483.7 5.2 collective-permute-done.23
  489.5 4.0 collective-permute-start.24
  498.2 13.3 %collective-permute-done.22 = bf16[384,1024]{1,0:T(8,128)(2,1)S(1)} collective-permute-done((bf16[384,1024]{1,0:T(8,128)(2,1)S(1)}, bf16[384,1024]{1,0:T(8,128)(2,1)S(1)}, u32[]{:S(2)}, u32[]{:S(2)}) %collective-permute-start.22) | collective-permute-done | bytes 786464 | tf_op jit(solution)/shard_map/ppermute | solution.py:181
  511.5 13.9 %collective-permute-done.24 = bf16[384,1024]{1,0:T(8,128)(2,1)S(1)} collective-permute-done((bf16[384,1024]{1,0:T(8,128)(2,1)S(1)}, bf16[384,1024]{1,0:T(8,128)(2,1)S(1)}, u32[]{:S(2)}, u32[]{:S(2)}) %collective-permute-start.24) | collective-permute-done | bytes 786464 | tf_op jit(solution)/shard_map/ppermute | solution.py:181
  531.6 3.9 fusion.128
  538.7 3.6 bitcast_add_fusion.1
  545.6 7.1 fusion.145
  563.7 10.2 %pad_maximum_fusion = f32[5,512,1024]{2,1,0:T(8,128)} fusion(f32[2,512,1024]{2,1,0:T(8,128)} %bitcast_add_fusion, f32[2,512,1024]{2,1,0:T(8,128)} %bitcast_add_fusion.1, f32[1,512,1024]{2,1,0:T(8,128)} %add_bitcast_fusion), kind=kLoop, calls=%fused_computation.39 | loop fusion | flops 5242880 | bytes 20971520 | tf_op jit(solution)/shard_map/concatenate | solution.py:368
  575.6 10.5 %collective-permute-done.31 = bf16[5,256,256]{2,1,0:T(8,128)(2,1)} collective-permute-done((bf16[5,256,256]{2,1,0:T(8,128)(2,1)}, bf16[5,256,256]{2,1,0:T(8,128)(2,1)}, u32[]{:S(2)}, u32[]{:S(2)}) %collective-permute-start.31) | collective-permute-done | bytes 655392 | tf_op jit(solution)/shard_map/ppermute | solution.py:181
  596.3 5.7 fusion.89
  601.9 20.3 %collective-permute-done.30 = bf16[5,512,256]{2,1,0:T(8,128)(2,1)S(1)} collective-permute-done((bf16[5,512,256]{2,1,0:T(8,128)(2,1)S(1)}, bf16[5,512,256]{2,1,0:T(8,128)(2,1)S(1)}, u32[]{:S(2)}, u32[]{:S(2)}) %collective-permute-start.30) | collective-permute-done | bytes 1310752 | tf_op jit(solution)/shard_map/ppermute | solution.py:181
  622.2 25.6 %collective-permute-done.32 = bf16[5,512,256]{2,1,0:T(8,128)(2,1)S(1)} collective-permute-done((bf16[5,512,256]{2,1,0:T(8,128)(2,1)S(1)}, bf16[5,512,256]{2,1,0:T(8,128)(2,1)S(1)}, u32[]{:S(2)}, u32[]{:S(2)}) %collective-permute-start.32) | collective-permute-done | bytes 1310752 | tf_op jit(solution)/shard_map/ppermute | solution.py:181
  665.2 4.7 fusion.47
  670.0 87.1 %all-reduce.3.cloned.1.call-done = (bf16[512,5,256]{2,0,1:T(8,128)(2,1)}, bf16[512,6,256]{2,0,1:T(8,128)(2,1)}, bf16[3,512,256]{2,1,0:T(8,128)(2,1)}) async-done(((bf16[512,5,256]{2,0,1:T(8,128)(2,1)}, bf16[512,6,256]{2,0,1:T(8,128)(2,1)}, bf16[3,512,256]{2,1,0:T(8,128)(2,1)}), (bf16[512,5,256]{2,0,1:T(8,128)(2,1)}, bf16[512,6,256]{2,0,1:T(8,128)(2,1)}, ...) | async-done | bytes 3670032 | tf_op jit(solution)/shard_map/psum | solution.py:433
  757.1 7.1 multiply_subtract_fusion
  764.2 3.9 multiply_subtract_fusion.1
  (487 shorter events, 197.3 us)
Async XLA Ops:
  7.2 749.9 %all-reduce.3.cloned.1.call-start = ((), (), s32[]{:S(2)}) async-start(), calls=%async_computation | async-start | bytes 7340032 | tf_op jit(solution)/shard_map/psum | solution.py:433
  9.5 85.1 %collective-permute-start.5 = (bf16[384,1024]{0,1:T(8,128)(2,1)}, bf16[384,1024]{0,1:T(8,128)(2,1)}, u32[]{:S(2)}, u32[]{:S(2)}) collective-permute-start(bf16[384,1024]{0,1:T(8,128)(2,1)} %copy.52), channel_id=1, source_target_pairs={{0,3},{1,0},{2,1},{3,2},{4,7},{5,4},{6,5},{7,6},{8,11},{9,8},{10,9... | collective-permute-start | bytes 2359304 | tf_op jit(solution)/shard_map/ppermute | solution.py:181
  14.6 78.4 %collective-permute-start.6 = (bf16[384,1024]{0,1:T(8,128)(2,1)}, bf16[384,1024]{0,1:T(8,128)(2,1)}, u32[]{:S(2)}, u32[]{:S(2)}) collective-permute-start(bf16[384,1024]{0,1:T(8,128)(2,1)} %copy.52), channel_id=1, source_target_pairs={{0,1},{1,2},{2,3},{3,0},{4,5},{5,6},{6,7},{7,4},{8,9},{9,10},{10,1... | collective-permute-start | bytes 2359304 | tf_op jit(solution)/shard_map/ppermute | solution.py:181
  14.6 15.7 %collective-permute-start = (s32[3]{0:T(128)}, s32[3]{0:T(128)}, u32[]{:S(2)}, u32[]{:S(2)}) collective-permute-start(s32[3]{0:T(128)} %bitcast.301), channel_id=1, source_target_pairs={{0,4},{4,0},{1,5},{5,1},{2,6},{6,2},{3,7},{7,3},{8,12},{12,8},{9,1... | collective-permute-start | bytes 44 | tf_op jit(solution)/shard_map/ppermute | solution.py:181
  19.6 81.2 %collective-permute-start.9 = (bf16[512,3,256]{0,2,1:T(8,128)(2,1)}, bf16[512,3,256]{0,2,1:T(8,128)(2,1)}, u32[]{:S(2)}, u32[]{:S(2)}) collective-permute-start(bf16[512,3,256]{0,2,1:T(8,128)(2,1)} %slice.345), channel_id=1, source_target_pairs={{0,4},{4,0},{1,5},{5,1},{2,6},{6,2},{3,7},{7,3},{8,12},{12,8},{9,1... | collective-permute-start | bytes 2359304 | tf_op jit(solution)/shard_map/ppermute | solution.py:181
  23.6 127.7 %collective-permute-start.14 = (bf16[5,512,256]{2,1,0:T(8,128)(2,1)}, bf16[5,512,256]{2,1,0:T(8,128)(2,1)}, u32[]{:S(2)}, u32[]{:S(2)}) collective-permute-start(bf16[5,512,256]{2,1,0:T(8,128)(2,1)} %pad_maximum_fusion.8), channel_id=1, source_target_pairs={{0,1},{1,2},{2,3},{3,0},{4,5},{5,6},{6,7},{7,4},{8,9},{9,10},{10,1... | collective-permute-start | bytes 3932168 | tf_op jit(solution)/shard_map/ppermute | solution.py:181
  30.2 120.5 %copy-start.52 = (f32[1536,32]{0,1:T(8,128)}, f32[1536,32]{0,1:T(8,128)S(1)}, u32[]{:S(2)}) copy-start(f32[1536,32]{0,1:T(8,128)S(1)} %get-tuple-element.305) | copy-start | bytes 589828
  30.3 120.5 %copy-start.54 = (f32[1536,32]{0,1:T(8,128)}, f32[1536,32]{0,1:T(8,128)S(1)}, u32[]{:S(2)}) copy-start(f32[1536,32]{0,1:T(8,128)S(1)} %get-tuple-element.306) | copy-start | bytes 589828
  34.8 1.5 collective-permute-start.1
  38.5 39.6 %collective-permute-start.2 = (f32[3,6,256]{2,0,1:T(4,128)}, f32[3,6,256]{2,0,1:T(4,128)}, u32[]{:S(2)}, u32[]{:S(2)}) collective-permute-start(f32[3,6,256]{2,0,1:T(4,128)} %get-tuple-element.229), channel_id=1, source_target_pairs={{0,3},{1,0},{2,1},{3,2},{4,7},{5,4},{6,5},{7,6},{8,11},{9,8},{10,9... | collective-permute-start | bytes 55304 | tf_op jit(solution)/shard_map/ppermute | solution.py:181
  42.8 58.0 %copy-start.32 = (bf16[512,5,256]{0,2,1:T(8,128)(2,1)S(1)}, bf16[512,5,256]{0,2,1:T(8,128)(2,1)}, u32[]{:S(2)}) copy-start(bf16[512,5,256]{0,2,1:T(8,128)(2,1)} %copy.55) | copy-start | bytes 3932164
  78.1 4.9 collective-permute-start.3
  83.0 6.1 collective-permute-start.4
  89.1 63.3 %collective-permute-start.13 = (bf16[5,512,256]{2,1,0:T(8,128)(2,1)}, bf16[5,512,256]{2,1,0:T(8,128)(2,1)S(1)}, u32[]{:S(2)}, u32[]{:S(2)}) collective-permute-start(bf16[5,512,256]{2,1,0:T(8,128)(2,1)} %pad_maximum_fusion.8), channel_id=1, source_target_pairs={{0,3},{1,0},{2,1},{3,2},{4,7},{5,4},{6,5},{7,6},{8,11},{9,8},{10,9... | collective-permute-start | bytes 3932168 | tf_op jit(solution)/shard_map/ppermute | solution.py:181
  93.0 50.3 %copy-start.82 = (f32[1,1,1024]{2,0,1:T(1,128)}, f32[1,1,1024]{2,0,1:T(1,128)S(1)}, u32[]{:S(2)}) copy-start(f32[1,1,1024]{2,0,1:T(1,128)S(1)} %get-tuple-element.299) | copy-start | bytes 12292
  93.0 50.3 %copy-start.84 = (f32[1,1,1024]{2,0,1:T(1,128)}, f32[1,1,1024]{2,0,1:T(1,128)S(1)}, u32[]{:S(2)}) copy-start(f32[1,1,1024]{2,0,1:T(1,128)S(1)} %get-tuple-element.300) | copy-start | bytes 12292
  93.0 50.3 %copy-start.86 = (f32[1,1,1024]{2,0,1:T(1,128)}, f32[1,1,1024]{2,0,1:T(1,128)S(1)}, u32[]{:S(2)}) copy-start(f32[1,1,1024]{2,0,1:T(1,128)S(1)} %get-tuple-element.301) | copy-start | bytes 12292
  94.1 37.7 %collective-permute-start.7 = (bf16[192,1024]{0,1:T(8,128)(2,1)S(1)}, bf16[192,1024]{0,1:T(8,128)(2,1)S(1)}, u32[]{:S(2)}, u32[]{:S(2)}) collective-permute-start(bf16[192,1024]{0,1:T(8,128)(2,1)S(1)} %slice.334), channel_id=1, source_target_pairs={{0,1},{1,2},{2,3},{3,0},{4,5},{5,6},{6,7},{7,4},{8,9},{9,10},{10,1... | collective-permute-start | bytes 1179656 | tf_op jit(solution)/shard_map/ppermute | solution.py:181
  95.9 44.3 %collective-permute-start.8 = (bf16[192,1024]{0,1:T(8,128)(2,1)S(1)}, bf16[192,1024]{0,1:T(8,128)(2,1)S(1)}, u32[]{:S(2)}, u32[]{:S(2)}) collective-permute-start(bf16[192,1024]{0,1:T(8,128)(2,1)S(1)} %slice.335), channel_id=1, source_target_pairs={{0,3},{1,0},{2,1},{3,2},{4,7},{5,4},{6,5},{7,6},{8,11},{9,8},{10,9... | collective-permute-start | bytes 1179656 | tf_op jit(solution)/shard_map/ppermute | solution.py:181
  102.1 45.6 %copy-start.76 = (bf16[512,3,256]{0,2,1:T(8,128)(2,1)}, bf16[512,3,256]{0,2,1:T(8,128)(2,1)S(1)}, u32[]{:S(2)}) copy-start(bf16[512,3,256]{0,2,1:T(8,128)(2,1)S(1)} %get-tuple-element.258) | copy-start | bytes 2359300
  102.2 45.6 %copy-start.77 = (bf16[512,3,256]{0,2,1:T(8,128)(2,1)}, bf16[512,3,256]{0,2,1:T(8,128)(2,1)S(1)}, u32[]{:S(2)}) copy-start(bf16[512,3,256]{0,2,1:T(8,128)(2,1)S(1)} %get-tuple-element.259) | copy-start | bytes 2359300
  152.4 19.5 %collective-permute-start.15 = (bf16[5,256,256]{2,1,0:T(8,128)(2,1)S(1)}, bf16[5,256,256]{2,1,0:T(8,128)(2,1)S(1)}, u32[]{:S(2)}, u32[]{:S(2)}) collective-permute-start(bf16[5,256,256]{2,1,0:T(8,128)(2,1)S(1)} %slice.354), channel_id=1, source_target_pairs={{0,1},{1,2},{2,3},{3,0},{4,5},{5,6},{6,7},{7,4},{8,9},{9,10},{10,1... | collective-permute-start | bytes 1966088 | tf_op jit(solution)/shard_map/ppermute | solution.py:181
  152.5 28.0 %copy-start.35 = (bf16[5,512,256]{2,1,0:T(8,128)(2,1)}, bf16[5,512,256]{2,1,0:T(8,128)(2,1)S(1)}, u32[]{:S(2)}) copy-start(bf16[5,512,256]{2,1,0:T(8,128)(2,1)S(1)} %collective-permute-done.13) | copy-start | bytes 3932164
  152.5 27.9 %copy-start.23 = (bf16[3,512,256]{2,1,0:T(8,128)(2,1)S(1)}, bf16[3,512,256]{2,1,0:T(8,128)(2,1)}, u32[]{:S(2)}) copy-start(bf16[3,512,256]{2,1,0:T(8,128)(2,1)} %copy-done.22) | copy-start | bytes 2359300
  152.6 27.9 %copy-start.34 = (bf16[2,512,256]{2,1,0:T(8,128)(2,1)S(1)}, bf16[2,512,256]{2,1,0:T(8,128)(2,1)}, u32[]{:S(2)}) copy-start(bf16[2,512,256]{2,1,0:T(8,128)(2,1)} %copy-done.33) | copy-start | bytes 1572868
  152.6 27.9 %collective-permute-start.16 = (bf16[5,256,256]{2,1,0:T(8,128)(2,1)S(1)}, bf16[5,256,256]{2,1,0:T(8,128)(2,1)S(1)}, u32[]{:S(2)}, u32[]{:S(2)}) collective-permute-start(bf16[5,256,256]{2,1,0:T(8,128)(2,1)S(1)} %slice.355), channel_id=1, source_target_pairs={{0,3},{1,0},{2,1},{3,2},{4,7},{5,4},{6,5},{7,6},{8,11},{9,8},{10,9... | collective-permute-start | bytes 1966088 | tf_op jit(solution)/shard_map/ppermute | solution.py:181
  157.7 28.7 %copy-start.125 = (s32[3]{0:T(128)S(1)}, s32[3]{0:T(128)}, u32[]{:S(2)}) copy-start(s32[3]{0:T(128)} %iota_multiply_fusion) | copy-start | bytes 40
  186.4 58.2 %collective-permute-start.17 = (bf16[5,512,1024]{2,1,0:T(8,128)(2,1)}, bf16[5,512,1024]{2,1,0:T(8,128)(2,1)}, u32[]{:S(2)}, u32[]{:S(2)}) collective-permute-start(bf16[5,512,1024]{2,1,0:T(8,128)(2,1)} %pad_maximum_fusion.1), channel_id=1, source_target_pairs={{0,4},{4,0},{1,5},{5,1},{2,6},{6,2},{3,7},{7,3},{8,12},{12,8},{9,1... | collective-permute-start | bytes 15728648 | tf_op jit(solution)/shard_map/ppermute | solution.py:181
  240.0 20.3 %copy-start.78 = (bf16[384,256]{0,1:T(8,128)(2,1)}, bf16[384,256]{0,1:T(8,128)(2,1)S(1)}, u32[]{:S(2)}) copy-start(bf16[384,256]{0,1:T(8,128)(2,1)S(1)} %get-tuple-element.276) | copy-start | bytes 589828
  240.0 10.9 %collective-permute-start.10 = (bf16[384,256]{0,1:T(8,128)(2,1)S(1)}, bf16[384,256]{0,1:T(8,128)(2,1)S(1)}, u32[]{:S(2)}, u32[]{:S(2)}) collective-permute-start(bf16[384,256]{0,1:T(8,128)(2,1)S(1)} %get-tuple-element.279), channel_id=1, source_target_pairs={{0,3},{1,0},{2,1},{3,2},{4,7},{5,4},{6,5},{7,6},{8,11},{9,8},{10,9... | collective-permute-start | bytes 589832 | tf_op jit(solution)/shard_map/ppermute | solution.py:181
  241.7 18.5 %collective-permute-start.11 = (bf16[384,256]{0,1:T(8,128)(2,1)S(1)}, bf16[384,256]{0,1:T(8,128)(2,1)S(1)}, u32[]{:S(2)}, u32[]{:S(2)}) collective-permute-start(bf16[384,256]{0,1:T(8,128)(2,1)S(1)} %get-tuple-element.278), channel_id=1, source_target_pairs={{0,2},{1,3},{2,0},{3,1},{4,6},{5,7},{6,4},{7,5},{8,10},{9,11},{10,... | collective-permute-start | bytes 589832 | tf_op jit(solution)/shard_map/ppermute | solution.py:181
  242.2 18.1 %collective-permute-start.12 = (bf16[384,256]{0,1:T(8,128)(2,1)S(1)}, bf16[384,256]{0,1:T(8,128)(2,1)S(1)}, u32[]{:S(2)}, u32[]{:S(2)}) collective-permute-start(bf16[384,256]{0,1:T(8,128)(2,1)S(1)} %get-tuple-element.277), channel_id=1, source_target_pairs={{0,1},{1,2},{2,3},{3,0},{4,5},{5,6},{6,7},{7,4},{8,9},{9,10},{10,1... | collective-permute-start | bytes 589832 | tf_op jit(solution)/shard_map/ppermute | solution.py:181
  250.9 13.2 %copy-start.118 = (bf16[384,256]{0,1:T(8,128)(2,1)}, bf16[384,256]{0,1:T(8,128)(2,1)S(1)}, u32[]{:S(2)}) copy-start(bf16[384,256]{0,1:T(8,128)(2,1)S(1)} %collective-permute-done.10) | copy-start | bytes 589828
  264.1 15.8 %copy-start.8 = (f32[384,1024]{1,0:T(8,128)}, f32[384,1024]{1,0:T(8,128)S(1)}, u32[]{:S(2)}) copy-start(f32[384,1024]{1,0:T(8,128)S(1)} %get-tuple-element.227) | copy-start | bytes 4718596
  264.1 15.8 %copy-start.94 = (f32[384]{0:T(512)}, f32[384]{0:T(512)S(1)}, u32[]{:S(2)}) copy-start(f32[384]{0:T(512)S(1)} %broadcast_multiply_fusion.6) | copy-start | bytes 4612
  264.5 15.5 %copy-start.101 = (f32[384]{0:T(512)}, f32[384]{0:T(512)S(1)}, u32[]{:S(2)}) copy-start(f32[384]{0:T(512)S(1)} %add_rsqrt_fusion.2) | copy-start | bytes 4612
  284.3 8.1 %collective-permute-start.18 = (bf16[384,256]{1,0:T(8,128)(2,1)}, bf16[384,256]{1,0:T(8,128)(2,1)S(1)}, u32[]{:S(2)}, u32[]{:S(2)}) collective-permute-start(bf16[384,256]{1,0:T(8,128)(2,1)} %get-tuple-element.274), channel_id=1, source_target_pairs={{0,3},{1,0},{2,1},{3,2},{4,7},{5,4},{6,5},{7,6},{8,11},{9,8},{10,9... | collective-permute-start | bytes 589832 | tf_op jit(solution)/shard_map/ppermute | solution.py:181
  285.0 19.6 %collective-permute-start.19 = (bf16[384,256]{1,0:T(8,128)(2,1)}, bf16[384,256]{1,0:T(8,128)(2,1)S(1)}, u32[]{:S(2)}, u32[]{:S(2)}) collective-permute-start(bf16[384,256]{1,0:T(8,128)(2,1)} %get-tuple-element.273), channel_id=1, source_target_pairs={{0,2},{1,3},{2,0},{3,1},{4,6},{5,7},{6,4},{7,5},{8,10},{9,11},{10,... | collective-permute-start | bytes 589832 | tf_op jit(solution)/shard_map/ppermute | solution.py:181
  287.5 18.3 %collective-permute-start.20 = (bf16[384,256]{1,0:T(8,128)(2,1)}, bf16[384,256]{1,0:T(8,128)(2,1)}, u32[]{:S(2)}, u32[]{:S(2)}) collective-permute-start(bf16[384,256]{1,0:T(8,128)(2,1)} %get-tuple-element.272), channel_id=1, source_target_pairs={{0,1},{1,2},{2,3},{3,0},{4,5},{5,6},{6,7},{7,4},{8,9},{9,10},{10,1... | collective-permute-start | bytes 589832 | tf_op jit(solution)/shard_map/ppermute | solution.py:181
  292.4 202.5 %collective-permute-start.26 = (bf16[512,1024]{1,0:T(8,128)(2,1)}, bf16[512,1024]{1,0:T(8,128)(2,1)}, u32[]{:S(2)}, u32[]{:S(2)}) collective-permute-start(bf16[512,1024]{1,0:T(8,128)(2,1)} %convolution_convert_fusion), channel_id=1, source_target_pairs={{0,4},{4,0},{1,5},{5,1},{2,6},{6,2},{3,7},{7,3},{8,12},{12,8},{9,1... | collective-permute-start | bytes 3145736 | tf_op jit(solution)/shard_map/ppermute | solution.py:181
  382.9 11.7 %copy-start.5 = (f32[1536,4,64]{0,2,1:T(8,128)S(1)}, f32[1536,4,64]{0,2,1:T(8,128)}, u32[]{:S(2)}) copy-start(f32[1536,4,64]{0,2,1:T(8,128)} %get-tuple-element.488) | copy-start | bytes 4718596 | tf_op jit(solution)/shard_map/while
  432.8 11.7 %copy-start.5 = (f32[1536,4,64]{0,2,1:T(8,128)S(1)}, f32[1536,4,64]{0,2,1:T(8,128)}, u32[]{:S(2)}) copy-start(f32[1536,4,64]{0,2,1:T(8,128)} %get-tuple-element.488) | copy-start | bytes 4718596 | tf_op jit(solution)/shard_map/while
  469.8 13.8 %collective-permute-start.21 = (bf16[192,1024]{1,0:T(8,128)(2,1)S(1)}, bf16[192,1024]{1,0:T(8,128)(2,1)S(1)}, u32[]{:S(2)}, u32[]{:S(2)}) collective-permute-start(bf16[192,1024]{1,0:T(8,128)(2,1)S(1)} %get-tuple-element.270), channel_id=1, source_target_pairs={{0,1},{1,2},{2,3},{3,0},{4,5},{5,6},{6,7},{7,4},{8,9},{9,10},{10,1... | collective-permute-start | bytes 1179656 | tf_op jit(solution)/shard_map/ppermute | solution.py:181
  469.9 19.0 %collective-permute-start.23 = (bf16[192,1024]{1,0:T(8,128)(2,1)S(1)}, bf16[192,1024]{1,0:T(8,128)(2,1)S(1)}, u32[]{:S(2)}, u32[]{:S(2)}) collective-permute-start(bf16[192,1024]{1,0:T(8,128)(2,1)S(1)} %get-tuple-element.271), channel_id=1, source_target_pairs={{0,3},{1,0},{2,1},{3,2},{4,7},{5,4},{6,5},{7,6},{8,11},{9,8},{10,9... | collective-permute-start | bytes 1179656 | tf_op jit(solution)/shard_map/ppermute | solution.py:181
  475.3 63.4 %collective-permute-start.27 = (bf16[2,512,1024]{2,1,0:T(8,128)(2,1)S(1)}, bf16[2,512,1024]{2,1,0:T(8,128)(2,1)S(1)}, u32[]{:S(2)}, u32[]{:S(2)}) collective-permute-start(bf16[2,512,1024]{2,1,0:T(8,128)(2,1)S(1)} %convert_bitcast_fusion.1), channel_id=1, source_target_pairs={{0,4},{4,0},{1,5},{5,1},{2,6},{6,2},{3,7},{7,3},{8,12},{12,8},{9,1... | collective-permute-start | bytes 6291464 | tf_op jit(solution)/shard_map/ppermute | solution.py:181
  475.5 17.9 %copy-start.38 = (bf16[384,1024]{1,0:T(8,128)(2,1)S(1)}, bf16[384,1024]{1,0:T(8,128)(2,1)}, u32[]{:S(2)}) copy-start(bf16[384,1024]{1,0:T(8,128)(2,1)} %copy-done.37) | copy-start | bytes 2359300
  475.5 17.9 %copy-start.41 = (bf16[384,2,1024]{2,0,1:T(8,128)(2,1)S(1)}, bf16[384,2,1024]{2,0,1:T(8,128)(2,1)}, u32[]{:S(2)}) copy-start(bf16[384,2,1024]{2,0,1:T(8,128)(2,1)} %copy-done.40) | copy-start | bytes 4718596
  489.2 22.3 %collective-permute-start.22 = (bf16[384,1024]{1,0:T(8,128)(2,1)S(1)}, bf16[384,1024]{1,0:T(8,128)(2,1)S(1)}, u32[]{:S(2)}, u32[]{:S(2)}) collective-permute-start(bf16[384,1024]{1,0:T(8,128)(2,1)S(1)} %pad_maximum_fusion.18), channel_id=1, source_target_pairs={{0,1},{1,2},{2,3},{3,0},{4,5},{5,6},{6,7},{7,4},{8,9},{9,10},{10,1... | collective-permute-start | bytes 2359304 | tf_op jit(solution)/shard_map/ppermute | solution.py:181
  489.5 36.0 %collective-permute-start.24 = (bf16[384,1024]{1,0:T(8,128)(2,1)S(1)}, bf16[384,1024]{1,0:T(8,128)(2,1)S(1)}, u32[]{:S(2)}, u32[]{:S(2)}) collective-permute-start(bf16[384,1024]{1,0:T(8,128)(2,1)S(1)} %pad_maximum_fusion.19), channel_id=1, source_target_pairs={{0,3},{1,0},{2,1},{3,2},{4,7},{5,4},{6,5},{7,6},{8,11},{9,8},{10,9... | collective-permute-start | bytes 2359304 | tf_op jit(solution)/shard_map/ppermute | solution.py:181
  494.7 47.5 %collective-permute-start.28 = (bf16[2,512,1024]{2,1,0:T(8,128)(2,1)S(1)}, bf16[2,512,1024]{2,1,0:T(8,128)(2,1)S(1)}, u32[]{:S(2)}, u32[]{:S(2)}) collective-permute-start(bf16[2,512,1024]{2,1,0:T(8,128)(2,1)S(1)} %convert_bitcast_fusion), channel_id=1, source_target_pairs={{0,4},{4,0},{1,5},{5,1},{2,6},{6,2},{3,7},{7,3},{8,12},{12,8},{9,1... | collective-permute-start | bytes 6291464 | tf_op jit(solution)/shard_map/ppermute | solution.py:181
  498.2 27.7 %copy-start.14 = (bf16[384,1024]{1,0:T(8,128)(2,1)S(1)}, bf16[384,1024]{1,0:T(8,128)(2,1)}, u32[]{:S(2)}) copy-start(bf16[384,1024]{1,0:T(8,128)(2,1)} %param.21) | copy-start | bytes 2359300
  498.2 27.7 %copy-start.100 = (f32[384]{0:T(512)S(1)}, f32[384]{0:T(512)}, u32[]{:S(2)}) copy-start(f32[384]{0:T(512)} %broadcast_multiply_fusion.3) | copy-start | bytes 4612
  535.5 27.6 %collective-permute-start.33 = (f32[3,6,256]{2,0,1:T(4,128)S(1)}, f32[3,6,256]{2,0,1:T(4,128)S(1)}, u32[]{:S(2)}, u32[]{:S(2)}) collective-permute-start(f32[3,6,256]{2,0,1:T(4,128)S(1)} %get-tuple-element.284), channel_id=1, source_target_pairs={{0,3},{1,0},{2,1},{3,2},{4,7},{5,4},{6,5},{7,6},{8,11},{9,8},{10,9... | collective-permute-start | bytes 55304 | tf_op jit(solution)/shard_map/ppermute | solution.py:181
  536.6 26.4 %collective-permute-start.34 = (f32[3,6,256]{2,0,1:T(4,128)S(1)}, f32[3,6,256]{2,0,1:T(4,128)S(1)}, u32[]{:S(2)}, u32[]{:S(2)}) collective-permute-start(f32[3,6,256]{2,0,1:T(4,128)S(1)} %get-tuple-element.286), channel_id=1, source_target_pairs={{0,2},{1,3},{2,0},{3,1},{4,6},{5,7},{6,4},{7,5},{8,10},{9,11},{10,... | collective-permute-start | bytes 55304 | tf_op jit(solution)/shard_map/ppermute | solution.py:181
  538.1 24.9 %collective-permute-start.35 = (f32[3,6,256]{2,0,1:T(4,128)S(1)}, f32[3,6,256]{2,0,1:T(4,128)S(1)}, u32[]{:S(2)}, u32[]{:S(2)}) collective-permute-start(f32[3,6,256]{2,0,1:T(4,128)S(1)} %get-tuple-element.285), channel_id=1, source_target_pairs={{0,1},{1,2},{2,3},{3,0},{4,5},{5,6},{6,7},{7,4},{8,9},{9,10},{10,1... | collective-permute-start | bytes 55304 | tf_op jit(solution)/shard_map/ppermute | solution.py:181
  555.8 19.7 %collective-permute-start.29 = (bf16[5,256,256]{2,1,0:T(8,128)(2,1)}, bf16[5,256,256]{2,1,0:T(8,128)(2,1)}, u32[]{:S(2)}, u32[]{:S(2)}) collective-permute-start(bf16[5,256,256]{2,1,0:T(8,128)(2,1)} %get-tuple-element.245), channel_id=1, source_target_pairs={{0,1},{1,2},{2,3},{3,0},{4,5},{5,6},{6,7},{7,4},{8,9},{9,10},{10,1... | collective-permute-start | bytes 1966088 | tf_op jit(solution)/shard_map/ppermute | solution.py:181
  557.3 28.8 %collective-permute-start.31 = (bf16[5,256,256]{2,1,0:T(8,128)(2,1)}, bf16[5,256,256]{2,1,0:T(8,128)(2,1)}, u32[]{:S(2)}, u32[]{:S(2)}) collective-permute-start(bf16[5,256,256]{2,1,0:T(8,128)(2,1)} %get-tuple-element.246), channel_id=1, source_target_pairs={{0,3},{1,0},{2,1},{3,2},{4,7},{5,4},{6,5},{7,6},{8,11},{9,8},{10,9... | collective-permute-start | bytes 1966088 | tf_op jit(solution)/shard_map/ppermute | solution.py:181
  563.1 29.9 %collective-permute-start.25 = (bf16[512,3,256]{2,0,1:T(8,128)(2,1)}, bf16[512,3,256]{2,0,1:T(8,128)(2,1)}, u32[]{:S(2)}, u32[]{:S(2)}) collective-permute-start(bf16[512,3,256]{2,0,1:T(8,128)(2,1)} %fusion.83), channel_id=1, source_target_pairs={{0,4},{4,0},{1,5},{5,1},{2,6},{6,2},{3,7},{7,3},{8,12},{12,8},{9,1... | collective-permute-start | bytes 2359304 | tf_op jit(solution)/shard_map/ppermute | solution.py:181
  563.1 33.1 %collective-permute-start.36 = (f32[3,6,256]{2,0,1:T(4,128)S(1)}, f32[3,6,256]{2,0,1:T(4,128)S(1)}, u32[]{:S(2)}, u32[]{:S(2)}) collective-permute-start(f32[3,6,256]{2,0,1:T(4,128)S(1)} %add_add_fusion.1), channel_id=1, source_target_pairs={{0,4},{4,0},{1,5},{5,1},{2,6},{6,2},{3,7},{7,3},{8,12},{12,8},{9,1... | collective-permute-start | bytes 55304 | tf_op jit(solution)/shard_map/ppermute | solution.py:181
  573.8 14.7 %copy-start.51 = (bf16[5,256,256]{2,1,0:T(8,128)(2,1)S(1)}, bf16[5,256,256]{2,1,0:T(8,128)(2,1)}, u32[]{:S(2)}) copy-start(bf16[5,256,256]{2,1,0:T(8,128)(2,1)} %get-tuple-element.248) | copy-start | bytes 1966084
  588.7 33.5 %collective-permute-start.30 = (bf16[5,512,256]{2,1,0:T(8,128)(2,1)S(1)}, bf16[5,512,256]{2,1,0:T(8,128)(2,1)S(1)}, u32[]{:S(2)}, u32[]{:S(2)}) collective-permute-start(bf16[5,512,256]{2,1,0:T(8,128)(2,1)S(1)} %pad_maximum_fusion.9), channel_id=1, source_target_pairs={{0,1},{1,2},{2,3},{3,0},{4,5},{5,6},{6,7},{7,4},{8,9},{9,10},{10,1... | collective-permute-start | bytes 3932168 | tf_op jit(solution)/shard_map/ppermute | solution.py:181
  591.0 56.9 %collective-permute-start.32 = (bf16[5,512,256]{2,1,0:T(8,128)(2,1)S(1)}, bf16[5,512,256]{2,1,0:T(8,128)(2,1)S(1)}, u32[]{:S(2)}, u32[]{:S(2)}) collective-permute-start(bf16[5,512,256]{2,1,0:T(8,128)(2,1)S(1)} %pad_maximum_fusion.10), channel_id=1, source_target_pairs={{0,3},{1,0},{2,1},{3,2},{4,7},{5,4},{6,5},{7,6},{8,11},{9,8},{10,9... | collective-permute-start | bytes 3932168 | tf_op jit(solution)/shard_map/ppermute | solution.py:181
  596.2 59.4 %copy-start.39 = (f32[512,3,256]{2,0,1:T(8,128)}, f32[512,3,256]{2,0,1:T(8,128)S(1)}, u32[]{:S(2)}) copy-start(f32[512,3,256]{2,0,1:T(8,128)S(1)} %convert_add_fusion.2) | copy-start | bytes 4718596
  665.2 91.9 %copy-start.27 = (f32[512,6,256]{2,0,1:T(8,128)S(1)}, f32[512,6,256]{2,0,1:T(8,128)}, u32[]{:S(2)}) copy-start(f32[512,6,256]{2,0,1:T(8,128)} %param.27) | copy-start | bytes 9437188
  (117 other events, 579.2 us)
Sparse Core Ops, SparseCore 0:
  660.1 96.9 all-reduce.2

commit v2 on v0

v2 whole, which is shorter than its diff:
```python
from functools import partial
import math

import jax
import jax.numpy as jnp
from jax import lax
from jax.experimental import pallas as pl
from jax.experimental.pallas import tpu as pltpu
from jax.sharding import PartitionSpec as P

HEAD_DIM = 64
NBUCK = 8
BLOCK = 256
BOUNDS = 3

highest = lax.Precision.HIGHEST
norm_epsilon = 1e-06
adam_epsilon = 1e-08
beta_first = 0.9
beta_second = 0.999
inner_rate = 0.05
weight_decay = 0.01
outer_rate = 0.7
outer_beta = 0.9
low = jnp.bfloat16


def time_embedding(flow_time, width_all):
    half_width = width_all // 2
    frequency = jnp.exp(
        jnp.arange(half_width, dtype=jnp.float32) * (-math.log(10000.0) / (half_width - 1))
    )
    angles = 1000.0 * flow_time[:, None] * frequency[None, :]
    return jnp.concatenate([jnp.sin(angles), jnp.cos(angles)], axis=1)


def utterance_rows(ending, indices):
    number = jnp.zeros(indices.shape, jnp.int32)
    begin = jnp.zeros(indices.shape, jnp.int32)
    for u in range(ending.shape[0] - 1):
        after = indices >= ending[u]
        number = number + after.astype(jnp.int32)
        begin = jnp.where(after, ending[u], begin)
    return number, indices - begin


def rotary_tables(position):
    half_width = HEAD_DIM // 2
    frequency = jnp.exp(
        jnp.arange(half_width, dtype=jnp.float32) * (-2.0 * math.log(10000.0) / HEAD_DIM)
    )
    angles = position.astype(jnp.float32)[:, None] * frequency[None, :]
    cosine, sine = jnp.cos(angles), jnp.sin(angles)
    return jnp.concatenate([cosine] * 4, axis=1), jnp.concatenate([-sine, sine, -sine, sine], axis=1)


def normalize(values):
    centered = values - jnp.mean(values, axis=-1, keepdims=True)
    inverse_scale = lax.rsqrt(jnp.mean(centered * centered, axis=-1, keepdims=True) + norm_epsilon)
    return (centered * inverse_scale, inverse_scale)


def normalize_back(grads, normed, inverse_scale):
    return inverse_scale * (
        grads
        - jnp.mean(grads, axis=-1, keepdims=True)
        - normed * jnp.mean(grads * normed, axis=-1, keepdims=True)
    )


def turn(values, cosine, signed_sine):
    lanes = lax.broadcasted_iota(jnp.int32, values.shape, 1)
    swapped = jnp.where(lanes % 64 < 32, pltpu.roll(values, 96, 1), pltpu.roll(values, 32, 1))
    return values * cosine + swapped * signed_sine


def utterance_of(indices, info_ref, count):
    number = jnp.zeros(indices.shape, jnp.int32)
    for u in range(count - 1):
        number = number + (indices >= info_ref[BOUNDS + u]).astype(jnp.int32)
    return number


def by_utterance(number, table):
    out = table[0:1, :]
    for u in range(1, table.shape[0]):
        out = jnp.where(number >= u, table[u : u + 1, :], out)
    return out


def dot_rows(a, b):
    return lax.dot_general(a, b, (((1,), (1,)), ((), ())), preferred_element_type=jnp.float32)


def dot(a, b):
    return jnp.dot(a, b, preferred_element_type=jnp.float32)


def spread(values):
    centered = values - jnp.mean(values, axis=-1, keepdims=True)
    inverse = lax.rsqrt(jnp.mean(centered * centered, axis=-1, keepdims=True) + norm_epsilon)
    return centered * inverse, inverse


def over_rows(total, chunk, body):
    def step(i, carry):
        body(pl.ds(pl.multiple_of(i * chunk, chunk), chunk), i * chunk)
        return carry

    lax.fori_loop(0, total // chunk, step, 0)


def whole(a):
    shape = a.shape
    return pl.BlockSpec(shape, lambda *_: (0,) * len(shape))


def project_kernel(
    count, info_ref, x_ref, m0_ref, m1_ref, m2_ref, m3_ref, here_ref, away_ref, cos_ref, sin_ref, att_ref, qkv_ref, mod_ref
):
    step = pl.program_id(0)
    me, core = info_ref[0], info_ref[1]
    size = x_ref.shape[0]
    width = m0_ref.shape[2]

    @pl.when(step == 0)
    def _():
        mod_ref[...] = jnp.zeros_like(mod_ref)
        for r, piece in enumerate((m0_ref, m1_ref, m2_ref, m3_ref)):
            at = pl.ds(pl.multiple_of(jnp.bitwise_xor(me, r) * width, 128), width)
            mod_ref[:, 0:count, at] = piece[...]

    chunk = 64

    def norm(at, first):
        normed, _ = spread(x_ref[at, :].astype(jnp.float32))
        number = utterance_of(
            lax.broadcasted_iota(jnp.int32, (chunk, 1), 0) + step * size + first, info_ref, count
        )
        shift, scale = by_utterance(number, mod_ref[0, 0:count, :]), by_utterance(number, mod_ref[1, 0:count, :])
        att_ref[at, :] = (normed * (1.0 + scale) + shift).astype(jnp.bfloat16)

    over_rows(size, chunk, norm)
    depth = here_ref.shape[1]
    near = att_ref[:, pl.ds(pl.multiple_of(core * depth, 128), depth)]
    far = att_ref[:, pl.ds(pl.multiple_of((1 - core) * depth, 128), depth)]
    for c in range(3):
        values = dot(near, here_ref[c]) + dot(far, away_ref[c])
        if c < 2:
            for p in range(values.shape[1] // 128):
                lanes = slice(128 * p, 128 * p + 128)
                turned = turn(values[:, lanes], cos_ref[...], sin_ref[...])
                qkv_ref[c, :, lanes] = (turned * 0.125 if c == 0 else turned).astype(jnp.bfloat16)
        else:
            qkv_ref[c] = values.astype(jnp.bfloat16)


def project(info, features_full, mod_pieces, here, away, cosine, sine):
    frames, model_width = features_full.shape
    size = frames // 4
    cycles, count, width = mod_pieces[0].shape
    columns = here.shape[2]
    rows = lambda i, *_: (i, 0)
    return pl.pallas_call(
        partial(project_kernel, count),
        grid_spec=pltpu.PrefetchScalarGridSpec(
            num_scalar_prefetch=1,
            grid=(4,),
            in_specs=[pl.BlockSpec((size, model_width), rows)]
            + [whole(a) for a in (*mod_pieces, here, away)]
            + [pl.BlockSpec((size, 128), rows)] * 2,
            out_specs=[
                pl.BlockSpec((size, model_width), rows),
                pl.BlockSpec((3, size, columns), lambda i, *_: (0, i, 0)),
                pl.BlockSpec((cycles, 8, model_width), lambda *_: (0, 0, 0)),
            ],
        ),
        out_shape=[
            jax.ShapeDtypeStruct((frames, model_width), jnp.bfloat16),
            jax.ShapeDtypeStruct((3, frames, columns), jnp.bfloat16),
            jax.ShapeDtypeStruct((cycles, 8, model_width), jnp.float32),
        ],
        cost_estimate=pl.CostEstimate(
            flops=6 * frames * model_width * columns, transcendentals=0, bytes_accessed=frames * model_width * 6
        ),
        name="project",
    )(info, features_full, *mod_pieces, here, away, cosine, sine)


def forward_kernel(count, info_ref, range_ref, qkv_ref, out0, out1, out2, out3, log_ref, value_t, scores):
    block = pl.program_id(0)
    _, frames, columns = qkv_ref.shape
    size = out0.shape[0]
    pairs = columns // 128
    heads = 2 * pairs

    @pl.when(block == 0)
    def _():
        def rows(i, carry):
            at = pl.ds(pl.multiple_of(i * BLOCK, BLOCK), BLOCK)
            value_t[:, at] = qkv_ref[2, at, :].T
            return carry

        lax.fori_loop(0, frames // BLOCK, rows, 0)

    here = pl.ds(pl.multiple_of(block * size, 128), size)
    query_t = qkv_ref[0, here, :].T
    head_of = lax.broadcasted_iota(jnp.int32, (128, size), 0) < HEAD_DIM
    zero = jnp.zeros((128, size), jnp.bfloat16)
    query_heads = []
    for p in range(pairs):
        part = query_t[128 * p : 128 * p + 128]
        query_heads += [jnp.where(head_of, part, zero), jnp.where(head_of, zero, part)]
    own = utterance_of(lax.broadcasted_iota(jnp.int32, (1, size), 1) + block * size, info_ref, count)
    begin, end = range_ref[0, block], range_ref[1, block]

    def score(i, tops):
        at = pl.ds(pl.multiple_of(i * BLOCK, BLOCK), BLOCK)
        theirs = utterance_of(lax.broadcasted_iota(jnp.int32, (BLOCK, 1), 0) + i * BLOCK, info_ref, count)
        same = theirs == own
        out = []
        for h in range(heads):
            keys = qkv_ref[1, at, 128 * (h // 2) : 128 * (h // 2) + 128]
            s = jnp.dot(keys, query_heads[h], preferred_element_type=jnp.float32)
            s = jnp.where(same, s, -1e30)
            scores[h, at, :] = s
            out.append(jnp.maximum(tops[h], jnp.max(s, axis=0, keepdims=True)))
        return tuple(out)

    lowest = jnp.full((1, size), -1e30, jnp.float32)
    tops = lax.fori_loop(begin, end, score, (lowest,) * heads)

    def weigh(i, carry):
        at = pl.ds(pl.multiple_of(i * BLOCK, BLOCK), BLOCK)
        out = []
        for h in range(heads):
            total, mixed = carry[h]
            p = jnp.exp(scores[h, at, :] - tops[h])
            total = total + jnp.sum(p, axis=0, keepdims=True)
            mixed = mixed + jnp.dot(
                value_t[h * HEAD_DIM : (h + 1) * HEAD_DIM, at], p.astype(jnp.bfloat16), preferred_element_type=jnp.float32
            )
            out.append((total, mixed))
        return tuple(out)

    start = (jnp.zeros((1, size), jnp.float32), jnp.zeros((HEAD_DIM, size), jnp.float32))
    sums = lax.fori_loop(begin, end, weigh, (start,) * heads)
    mixed = jnp.concatenate([sums[h][1] / sums[h][0] for h in range(heads)], axis=0).T.astype(jnp.bfloat16)
    relative = jnp.bitwise_xor(block, info_ref[0])
    for r, out in enumerate((out0, out1, out2, out3)):

        @pl.when(relative == r)
        def _():
            out[...] = mixed

    for h in range(heads):
        log_ref[h : h + 1, here] = tops[h] + jnp.log(sums[h][0])


def backward_kernel(
    count, info_ref, range_ref, qkv_ref, grad0, grad1, grad2, grad3, log_ref, cos_ref, sin_ref, here_ref, away_ref,
    out_ref, part0, part1, part2, part3, key_t, key_sum, value_sum, probs,
    grads, grad_ref
):
    block = pl.program_id(0)
    _, frames, columns = qkv_ref.shape
    size = grad0.shape[0]
    pairs = columns // 128
    heads = 2 * pairs

    @pl.when(block == 0)
    def _():
        key_sum[...] = jnp.zeros_like(key_sum)
        value_sum[...] = jnp.zeros_like(value_sum)

        def rows(i, carry):
            at = pl.ds(pl.multiple_of(i * BLOCK, BLOCK), BLOCK)
            key_t[:, at] = qkv_ref[1, at, :].T
            return carry

        lax.fori_loop(0, frames // BLOCK, rows, 0)

    here = pl.ds(pl.multiple_of(block * size, 128), size)
    relative = jnp.bitwise_xor(block, info_ref[0])
    for r, piece in enumerate((grad0, grad1, grad2, grad3)):

        @pl.when(relative == r)
        def _():
            grad_ref[...] = piece[...]

    upper_t = lax.broadcasted_iota(jnp.int32, (128, size), 0) < HEAD_DIM
    upper = lax.broadcasted_iota(jnp.int32, (size, 128), 1) < HEAD_DIM
    zero_t, zero = jnp.zeros((128, size), jnp.bfloat16), jnp.zeros((size, 128), jnp.bfloat16)
    query_ts, grad_ts, queries, grad_heads = [], [], [], []
    for p in range(pairs):
        query = qkv_ref[0, here, 128 * p : 128 * p + 128]
        grad = grad_ref[:, 128 * p : 128 * p + 128]
        query_t, grad_t = query.T, grad.T
        query_ts += [jnp.where(upper_t, query_t, zero_t), jnp.where(upper_t, zero_t, query_t)]
        grad_ts += [jnp.where(upper_t, grad_t, zero_t), jnp.where(upper_t, zero_t, grad_t)]
        queries += [jnp.where(upper, query, zero), jnp.where(upper, zero, query)]
        grad_heads += [jnp.where(upper, grad, zero), jnp.where(upper, zero, grad)]
    own = utterance_of(lax.broadcasted_iota(jnp.int32, (1, size), 1) + block * size, info_ref, count)
    begin, end = range_ref[0, block], range_ref[1, block]
    logs = [log_ref[h : h + 1, here] for h in range(heads)]

    def first(i, deltas):
        at = pl.ds(pl.multiple_of(i * BLOCK, BLOCK), BLOCK)
        theirs = utterance_of(lax.broadcasted_iota(jnp.int32, (BLOCK, 1), 0) + i * BLOCK, info_ref, count)
        same = theirs == own
        out = []
        for h in range(heads):
            lanes = slice(128 * (h // 2), 128 * (h // 2) + 128)
            s = jnp.dot(qkv_ref[1, at, lanes], query_ts[h], preferred_element_type=jnp.float32)
            p = jnp.exp(jnp.where(same, s, -1e30) - logs[h])
            g = jnp.dot(qkv_ref[2, at, lanes], grad_ts[h], preferred_element_type=jnp.float32)
            probs[h, at, :] = p
            grads[h, at, :] = g
            out.append(deltas[h] + jnp.sum(p * g, axis=0, keepdims=True))
        return tuple(out)

    none = jnp.zeros((1, size), jnp.float32)
    deltas = lax.fori_loop(begin, end, first, (none,) * heads)

    def second(i, sums):
        at = pl.ds(pl.multiple_of(i * BLOCK, BLOCK), BLOCK)
        out = []
        for p in range(pairs):
            lanes = slice(128 * p, 128 * p + 128)
            key_add, value_add = key_sum[at, lanes], value_sum[at, lanes]
            for h in (2 * p, 2 * p + 1):
                weight = probs[h, at, :]
                ds = (weight * (grads[h, at, :] - deltas[h])).astype(jnp.bfloat16)
                out.append(
                    sums[h]
                    + jnp.dot(key_t[h * HEAD_DIM : (h + 1) * HEAD_DIM, at], ds, preferred_element_type=jnp.float32)
                )
                key_add = key_add + jnp.dot(ds, queries[h], preferred_element_type=jnp.float32)
                value_add = value_add + jnp.dot(
                    weight.astype(jnp.bfloat16), grad_heads[h], preferred_element_type=jnp.float32
                )
            key_sum[at, lanes] = key_add
            value_sum[at, lanes] = value_add
        return tuple(out)

    zero_sum = jnp.zeros((HEAD_DIM, size), jnp.float32)
    sums = lax.fori_loop(begin, end, second, (zero_sum,) * heads)
    grad_query = jnp.concatenate(sums, axis=0).T * 0.125
    for p in range(pairs):
        lanes = slice(128 * p, 128 * p + 128)
        out_ref[0, here, lanes] = turn(grad_query[:, lanes], cos_ref[here, :], -sin_ref[here, :]).astype(jnp.bfloat16)

    @pl.when(block == pl.num_programs(0) - 1)
    def _():
        def rows(i, carry):
            at = pl.ds(pl.multiple_of(i * BLOCK, BLOCK), BLOCK)
            for p in range(pairs):
                lanes = slice(128 * p, 128 * p + 128)
                out_ref[1, at, lanes] = turn(key_sum[at, lanes], cos_ref[at, :], -sin_ref[at, :]).astype(jnp.bfloat16)
            out_ref[2, at, :] = value_sum[at, :].astype(jnp.bfloat16)
            return carry

        lax.fori_loop(0, frames // BLOCK, rows, 0)
        depth = here_ref.shape[1]
        for r, part in enumerate((part0, part1, part2, part3)):
            at = pl.ds(pl.multiple_of(jnp.bitwise_xor(info_ref[0], r) * size, 128), size)
            for side, weight in ((info_ref[1], here_ref), (1 - info_ref[1], away_ref)):
                total = dot_rows(out_ref[0, at, :], weight[0])
                for c in (1, 2):
                    total = total + dot_rows(out_ref[c, at, :], weight[c])
                part[:, pl.ds(pl.multiple_of(side * depth, 128), depth)] = total.astype(part.dtype)


def key_ranges(ending, frames, size):
    starting = jnp.concatenate([jnp.zeros((1,), jnp.int32), ending[:-1]])
    begins = jnp.arange(frames // size, dtype=jnp.int32) * size
    first_key = jnp.min(jnp.where(ending[None, :] > begins[:, None], starting[None, :], frames), axis=1)
    last_key = jnp.max(jnp.where(starting[None, :] < begins[:, None] + size, ending[None, :], 0), axis=1)
    return jnp.stack([first_key // BLOCK, (last_key + BLOCK - 1) // BLOCK]).astype(jnp.int32)


def attend(info, ranges, qkv, count):
    _, frames, columns = qkv.shape
    heads = columns // HEAD_DIM
    size = frames // 4
    flat = lambda b, *_: (0, 0)
    return pl.pallas_call(
        partial(forward_kernel, count),
        grid_spec=pltpu.PrefetchScalarGridSpec(
            num_scalar_prefetch=2,
            grid=(4,),
            in_specs=[pl.BlockSpec((3, frames, columns), lambda b, *_: (0, 0, 0))],
            out_specs=[pl.BlockSpec((size, columns), flat)] * 4 + [pl.BlockSpec((heads, frames), flat)],
            scratch_shapes=[
                pltpu.VMEM((columns, frames), jnp.bfloat16),
                pltpu.VMEM((heads, frames, size), jnp.float32),
            ],
        ),
        out_shape=[jax.ShapeDtypeStruct((size, columns), jnp.bfloat16)] * 4
        + [jax.ShapeDtypeStruct((heads, frames), jnp.float32)],
        cost_estimate=pl.CostEstimate(
            flops=8 * frames * frames * columns, transcendentals=heads * frames * frames, bytes_accessed=frames * columns * 8
        ),
        name="attend",
    )(info, ranges, qkv)


def attend_back(info, ranges, qkv, grad_pieces, logs, cosine, sine, here, away, count):
    _, frames, columns = qkv.shape
    heads = columns // HEAD_DIM
    size = frames // 4
    cube = lambda b, *_: (0, 0, 0)
    flat = lambda b, *_: (0, 0)
    return pl.pallas_call(
        partial(backward_kernel, count),
        grid_spec=pltpu.PrefetchScalarGridSpec(
            num_scalar_prefetch=2,
            grid=(4,),
            in_specs=[pl.BlockSpec((3, frames, columns), cube)]
            + [pl.BlockSpec((size, columns), flat)] * 4
            + [pl.BlockSpec((heads, frames), flat), pl.BlockSpec((frames, 128), flat), pl.BlockSpec((frames, 128), flat)]
            + [whole(here), whole(away)],
            out_specs=[pl.BlockSpec((3, frames, columns), cube)] + [pl.BlockSpec((size, 2 * here.shape[1]), flat)] * 4,
            scratch_shapes=[
                pltpu.VMEM((columns, frames), jnp.bfloat16),
                pltpu.VMEM((frames, columns), jnp.float32),
                pltpu.VMEM((frames, columns), jnp.float32),
                pltpu.VMEM((heads, frames, size), jnp.float32),
                pltpu.VMEM((heads, frames, size), jnp.float32),
                pltpu.VMEM((size, columns), jnp.bfloat16),
            ],
        ),
        out_shape=[jax.ShapeDtypeStruct((3, frames, columns), jnp.bfloat16)]
        + [jax.ShapeDtypeStruct((size, 2 * here.shape[1]), jnp.bfloat16 if r else jnp.float32) for r in range(4)],
        cost_estimate=pl.CostEstimate(
            flops=16 * frames * frames * columns, transcendentals=heads * frames * frames, bytes_accessed=frames * columns * 20
        ),
        name="attend_back",
    )(info, ranges, qkv, *grad_pieces, logs, cosine, sine, here, away)


def middle_kernel(
    count, info_ref, x_ref, cot_ref, mixed0, mixed1, mixed2, mixed3, mod_ref, *refs
):
    pieces = refs[:10]
    out_ref, res_ref, g0, g1, g2, g3, sums_ref, ffn_in_ref, hidden_ref, grad_up_ref, grad_attn_ref, grad_ffn_ref = refs[10:22]
    wide, mixed, residual, attn, up, ffn, inverse, sems = refs[22:]
    me, core, group = info_ref[0], info_ref[1], info_ref[2]
    size = x_ref.shape[0]
    width = mixed0.shape[1]
    quarter = pieces[0].shape[2]
    depth = 4 * quarter

    copies = ([], [])
    for side in range(2):
        half = core if side == 0 else 1 - core
        for k, r in [(k, r) for k in range(4) for r in range(4)]:
            if k < 3:
                piece = pieces[5 * side + k].at[r]
            else:
                piece = pieces[5 * side + 3 + r // 2].at[r % 2]
            at = pl.ds(pl.multiple_of(half * depth + jnp.bitwise_xor(group, k) * quarter, 16), quarter)
            lanes = slice(r * width, (r + 1) * width)
            for part, cs in enumerate((slice(0, 1), slice(1, 5))):
                copy = pltpu.make_async_copy(
                    piece.at[cs], wide.at[cs, at, lanes], sems.at[part * 32 + side * 16 + k * 4 + r]
                )
                copies[part].append(copy)
    for copy in copies[0] + copies[1]:
        copy.start()
    for r, piece in enumerate((mixed0, mixed1, mixed2, mixed3)):
        mixed[:, r * width : (r + 1) * width] = piece[...]
    chunk = 64

    def table(c, number):
        return by_utterance(number, mod_ref[c, 0:count, :])

    def numbers(first):
        return utterance_of(lax.broadcasted_iota(jnp.int32, (chunk, 1), 0) + me * size + first, info_ref, count)

    for copy in copies[0]:
        copy.wait()
    attn[...] = dot_rows(mixed[...], wide[0])

    def enter(at, first):
        number = numbers(first)
        value = x_ref[at, :].astype(jnp.float32) + table(2, number) * attn[at, :]
        residual[at, :] = value
        normed, scale = spread(value)
        inverse[at, :] = jnp.broadcast_to(scale, (chunk, 128))
        ffn[at, :] = normed
        ffn_in_ref[at, :] = (normed * (1.0 + table(4, number)) + table(3, number)).astype(jnp.bfloat16)
        grad_ffn_ref[at, :] = (cot_ref[at, :].astype(jnp.float32) * table(5, number)).astype(jnp.bfloat16)

    over_rows(size, chunk, enter)
    for copy in copies[1]:
        copy.wait()
    for c in range(2):
        up[c] = dot(ffn_in_ref[...], wide[3 + c])

    root = math.sqrt(2.0 / math.pi)

    def act(at, first):
        for c in range(2):
            value = up[c, at, :]
            square = value * value
            bend = jnp.tanh(root * (value + 0.044715 * (value * square)))
            hidden_ref[c, at, :] = (0.5 * value * (1.0 + bend)).astype(jnp.bfloat16)
            up[c, at, :] = 0.5 * (1.0 + bend) + 0.5 * value * (1.0 - bend * bend) * (root * (1.0 + 0.134145 * square))

    over_rows(size, chunk, act)
    grad_hidden = [dot(grad_ffn_ref[...], wide[1 + c]) for c in range(2)]
    for c in range(2):
        grad_up_ref[c] = (up[c] * grad_hidden[c]).astype(jnp.bfloat16)
    up[0] = dot_rows(hidden_ref[0], wide[1]) + dot_rows(hidden_ref[1], wide[2])
    up[1] = dot_rows(grad_up_ref[0], wide[3]) + dot_rows(grad_up_ref[1], wide[4])
    sums_ref[...] = jnp.zeros_like(sums_ref)

    def leave(at, first):
        number = numbers(first)
        cot = cot_ref[at, :].astype(jnp.float32)
        ffn_out, grad_in, normed = up[0, at, :], up[1, at, :], ffn[at, :]
        out_ref[at, :] = (residual[at, :] + table(5, number) * ffn_out).astype(jnp.bfloat16)
        h = grad_in * (1.0 + table(4, number))
        grad = cot + inverse[at, 0:1] * (
            h - jnp.mean(h, axis=-1, keepdims=True) - normed * jnp.mean(h * normed, axis=-1, keepdims=True)
        )
        res_ref[at, :] = grad
        grad_attn_ref[at, :] = (grad * table(2, number)).astype(jnp.bfloat16)
        for c, rows in enumerate((grad * attn[at, :], grad_in, grad_in * normed, cot * ffn_out)):
            for u in range(count):
                sums_ref[c, u : u + 1, :] += jnp.sum(jnp.where(number == u, rows, 0.0), axis=0, keepdims=True)

    over_rows(size, chunk, leave)
    grad_mixed = dot(grad_attn_ref[...], wide[0]).astype(jnp.bfloat16)
    for r, piece in enumerate((g0, g1, g2, g3)):
        piece[...] = grad_mixed[:, r * width : (r + 1) * width]


def middle(info, features, cotangent, mixed_pieces, modulation, wide_here, wide_away, count):
    size, model_width = features.shape
    width = mixed_pieces[0].shape[1]
    pieces = (*wide_here, *wide_away)
    shapes = [
        ((size, model_width), jnp.bfloat16),
        ((size, model_width), jnp.float32),
        *[((size, width), jnp.bfloat16)] * 4,
        ((4, 8, model_width), jnp.float32),
        ((size, model_width), jnp.bfloat16),
        ((2, size, 4 * width), jnp.bfloat16),
        ((2, size, 4 * width), jnp.bfloat16),
        ((size, model_width), jnp.bfloat16),
        ((size, model_width), jnp.bfloat16),
    ]
    outs = [jax.ShapeDtypeStruct(shape, kind) for shape, kind in shapes]
    return pl.pallas_call(
        partial(middle_kernel, count),
        grid_spec=pltpu.PrefetchScalarGridSpec(
            num_scalar_prefetch=1,
            grid=(1,),
            in_specs=[whole(a) for a in (features, cotangent, *mixed_pieces, modulation)]
            + [pl.BlockSpec(memory_space=pl.ANY)] * 10,
            out_specs=[whole(a) for a in outs],
            scratch_shapes=[
                pltpu.VMEM((5, model_width, 4 * width), jnp.bfloat16),
                pltpu.VMEM((size, 4 * width), jnp.bfloat16),
                pltpu.VMEM((size, model_width), jnp.float32),
                pltpu.VMEM((size, model_width), jnp.float32),
                pltpu.VMEM((2, size, 4 * width), jnp.float32),
                pltpu.VMEM((size, model_width), jnp.float32),
                pltpu.VMEM((size, 128), jnp.float32),
                pltpu.SemaphoreType.DMA((64,)),
            ],
        ),
        out_shape=outs,
        cost_estimate=pl.CostEstimate(
            flops=20 * size * model_width * 4 * width, transcendentals=size * 8 * width, bytes_accessed=10 * model_width * 4 * width
        ),
        name="middle",
    )(info, features, cotangent, *mixed_pieces, modulation, *pieces)


def wide_grad_kernel(side, summed, info_ref, mixed_ref, hidden_ref, grad_up_ref, *refs):
    grad_refs, other_ref, out_ref, turned = refs[:3], refs[3] if summed else None, refs[-2], refs[-1]
    depth = out_ref.shape[2]
    half = info_ref[1] if side == 0 else 1 - info_ref[1]

    @pl.when(pl.program_id(0) == 0)
    def _():
        at = pl.ds(pl.multiple_of(half * depth, 128), depth)
        for i in range(3):
            turned[i] = grad_refs[i][:, at].T

    def block(c):
        if c == 0:
            return dot(turned[0], mixed_ref[0])
        if c < 3:
            return dot(turned[1], hidden_ref[c - 1])
        return dot(turned[2], grad_up_ref[c - 3])

    for c in range(5):
        value = block(c)
        if summed:
            value = value + other_ref[0, c].astype(jnp.float32)
        out_ref[0, c] = value.astype(jnp.bfloat16)


def wide_grads(info, side, mixed, hidden, grad_up, grad_attn, grad_ffn, ffn_in, other=None):
    _, size, width = mixed.shape
    depth = grad_attn.shape[1] // 2
    lanes = lambda r, info: (0, 0, r)
    target = pl.BlockSpec((1, 5, depth, width), lambda r, info: (jnp.bitwise_xor(info[0], r), 0, 0, 0))
    return pl.pallas_call(
        partial(wide_grad_kernel, side, other is not None),
        grid_spec=pltpu.PrefetchScalarGridSpec(
            num_scalar_prefetch=1,
            grid=(4,),
            in_specs=[
                pl.BlockSpec((1, size, width), lambda r, info: (r, 0, 0)),
                pl.BlockSpec((2, size, width), lanes),
                pl.BlockSpec((2, size, width), lanes),
                whole(grad_attn),
                whole(grad_ffn),
                whole(ffn_in),
            ]
            + ([target] if other is not None else []),
            out_specs=target,
            scratch_shapes=[pltpu.VMEM((3, depth, size), jnp.bfloat16)],
        ),
        out_shape=jax.ShapeDtypeStruct((4, 5, depth, width), jnp.bfloat16),
        cost_estimate=pl.CostEstimate(
            flops=40 * size * depth * width, transcendentals=0, bytes_accessed=60 * depth * width
        ),
        name="wide_grads",
    )(info, mixed, hidden, grad_up, grad_attn, grad_ffn, ffn_in, *([other] if other is not None else []))


def qkv_grad_kernel(side, summed, info_ref, grad_ref, att_ref, *refs):
    other_ref, out_ref, turned = refs[0] if summed else None, refs[-2], refs[-1]
    depth = out_ref.shape[1]
    half = info_ref[1] if side == 0 else 1 - info_ref[1]

    @pl.when(pl.program_id(0) == 0)
    def _():
        turned[...] = att_ref[:, pl.ds(pl.multiple_of(half * depth, 128), depth)].T

    value = dot(turned[...], grad_ref[0])
    if summed:
        value = value + other_ref[0].astype(jnp.float32)
    out_ref[0] = value.astype(out_ref.dtype)


def qkv_grads(info, side, gradients, att_full, other=None, kind=jnp.bfloat16):
    _, frames, columns = gradients.shape
    depth = att_full.shape[1] // 2
    target = pl.BlockSpec((1, depth, columns), lambda c, *_: (c, 0, 0))
    return pl.pallas_call(
        partial(qkv_grad_kernel, side, other is not None),
        grid_spec=pltpu.PrefetchScalarGridSpec(
            num_scalar_prefetch=1,
            grid=(3,),
            in_specs=[pl.BlockSpec((1, frames, columns), lambda c, *_: (c, 0, 0)), whole(att_full)]
            + ([target] if other is not None else []),
            out_specs=target,
            scratch_shapes=[pltpu.VMEM((depth, frames), jnp.bfloat16)],
        ),
        out_shape=jax.ShapeDtypeStruct((3, depth, columns), kind),
        cost_estimate=pl.CostEstimate(
            flops=6 * frames * depth * columns, transcendentals=0, bytes_accessed=frames * depth * 6
        ),
        name="qkv_grads",
    )(info, gradients, att_full, *([other] if other is not None else []))


def inner_step(grads, first, second, weights, steps_done):
    first_new = beta_first * first + (1.0 - beta_first) * grads
    second_new = beta_second * second + (1.0 - beta_second) * grads * grads
    correct_one = 1.0 - beta_first**steps_done
    correct_two = 1.0 - beta_second**steps_done
    difference = inner_rate * (
        first_new / correct_one / (jnp.sqrt(second_new / correct_two) + adam_epsilon)
        + weight_decay * weights
    )
    return (first_new[None], second_new[None], difference)


def outer_step(average, outer, weights):
    outer_new = outer_beta * outer + average
    return (outer_new, weights - outer_rate * (average + outer_beta * outer_new))


def swapped(values, axis, bits):
    size = lax.axis_size(axis)
    return lax.ppermute(values, axis, [(i, i ^ bits) for i in range(size)])


def exchange(blocks, axis="tensor"):
    return [blocks[0]] + [swapped(blocks[r], axis, r) for r in range(1, 4)]


def after(values, *others):
    return lax.optimization_barrier((values, *others))[0]


def dp_rows(own):
    if lax.axis_size("dp") != 2:
        return lax.all_gather(own, "dp", axis=0, tiled=True)
    other = swapped(own, "dp", 1)
    first = lax.axis_index("dp") == 0
    return jnp.concatenate([jnp.where(first, own, other), jnp.where(first, other, own)], axis=0)


def dp_pair(own):
    if lax.axis_size("dp") == 2:
        return own, swapped(own, "dp", 1)
    return tuple(jnp.split(lax.all_gather(own, "dp", axis=1, tiled=True), 2, axis=1))


def gather_wide(half):
    group = lax.axis_index("group")
    quarter = half.shape[1] // 4
    own = lax.dynamic_slice_in_dim(half, group * quarter, quarter, 1)
    stack = jnp.stack(exchange([own] * 4))
    one, two = swapped(stack, "group", 1), swapped(stack, "group", 2)
    return [stack, one, two, swapped(one[:2], "group", 2), swapped(two[2:], "group", 1)]


def wide_halves(own):
    if lax.axis_size("dp") == 2:
        here = gather_wide(own)
        return here, [swapped(piece, "dp", 1) for piece in here]
    halves = dp_pair(own)
    return gather_wide(halves[0]), gather_wide(halves[1])


def group_sum(values):
    group = lax.axis_index("group")
    quarter = values.shape[1] // 4
    parts = exchange([lax.dynamic_slice_in_dim(values, (group ^ r) * quarter, quarter, 1) for r in range(4)], "group")
    total = sum(part.astype(jnp.float32) for part in parts).astype(low)
    out = jnp.zeros_like(values)
    for r, part in enumerate(exchange([total] * 4, "group")):
        out = lax.dynamic_update_slice_in_dim(out, part, (group ^ r) * quarter, 1)
    return out


def per_device(
    features,
    cotangent,
    frame_counts,
    buckets,
    step_count,
    col_weights,
    mod_weights,
    row_weights,
    col_first,
    col_second,
    mod_first,
    mod_second,
    row_first,
    row_second,
    col_outer,
    mod_outer,
    row_outer,
):
    group_count = lax.axis_size("group")
    packs_here = lax.axis_size("dp")
    own_rows, model_width = features.shape
    frames = own_rows * 4
    me = lax.axis_index("tensor")
    core = lax.axis_index("dp")
    group = lax.axis_index("group")
    count = buckets.shape[1]
    share = mod_weights.shape[0]
    width = col_weights.shape[2]

    def columns_first(values):
        return jnp.swapaxes(values, -3, -2)

    features_full = lax.all_gather(features, "tensor", axis=0, tiled=True)

    buckets_all = dp_rows(buckets[0])
    flow_time = ((group * NBUCK + buckets_all).astype(jnp.float32) + 0.5) / (NBUCK * group_count)
    condition_all = jax.nn.silu(time_embedding(flow_time, model_width)).astype(low)
    condition_here = lax.dynamic_slice_in_dim(condition_all, core * share, share, 1)
    mod_terms = jnp.einsum("ud,dcj->cuj", condition_here, mod_weights.astype(low), preferred_element_type=jnp.float32)
    if packs_here != 2:
        mod_part = lax.psum_scatter(mod_terms, "dp", scatter_dimension=1, tiled=True)
    else:
        mod_away = lax.dynamic_slice_in_dim(mod_terms, (1 - core) * count, count, 1)
        mod_part = lax.dynamic_slice_in_dim(mod_terms, core * count, count, 1) + swapped(mod_away, "dp", 1)
    mod_pieces = exchange([mod_part] * 4)

    ending = jnp.cumsum(frame_counts[0]).astype(jnp.int32)
    half_core = core if packs_here == 2 else jnp.zeros_like(core)
    info = jnp.concatenate([jnp.stack([me, half_core, group]).astype(jnp.int32), ending])
    _, position = utterance_rows(ending, jnp.arange(frames, dtype=jnp.int32))
    cosine, sine = rotary_tables(position)
    ranges = key_ranges(ending, frames, own_rows)
    col_major = columns_first(col_weights).astype(low)
    qkv_here, qkv_away = dp_pair(col_major[0:3])
    wide_low = after(jnp.concatenate([row_weights.astype(low), col_major[3:5]], axis=0), *mod_pieces)
    wide_here, wide_away = wide_halves(wide_low)

    att_full, qkv, modulation = project(info, features_full, mod_pieces, qkv_here, qkv_away, cosine, sine)
    *mixed_pieces, log_totals = attend(info, ranges, qkv, count)
    mixed_pieces = exchange(mixed_pieces)

    (output, grad_residual, g0, g1, g2, g3, late_sums, ffn_in, hidden, grad_up, grad_attn, grad_ffn) = middle(
        info, features, cotangent, mixed_pieces, modulation, wide_here, wide_away, count
    )
    grad_pieces = exchange([g0, g1, g2, g3])
    wide_args = (jnp.stack(mixed_pieces), hidden, grad_up, grad_attn, grad_ffn, ffn_in)
    if packs_here == 2:
        wide_blocks = wide_grads(info, 0, *wide_args, other=swapped(wide_grads(info, 1, *wide_args), "dp", 1))
    else:
        both = jnp.concatenate([wide_grads(info, side, *wide_args) for side in range(2)], axis=2).astype(jnp.float32)
        wide_blocks = lax.psum_scatter(both, "dp", scatter_dimension=2, tiled=True).astype(low)
    wide_grad = lax.psum_scatter(wide_blocks, "tensor", scatter_dimension=0, tiled=False).astype(jnp.float32)

    def mod_gradient(sums):
        mine = [lax.dynamic_slice_in_dim(sums, (me ^ r) * width, width, 2) for r in range(4)]
        columns = dp_rows(jnp.swapaxes(sum(exchange(mine)), 0, 1))
        if packs_here != 2:
            return jnp.einsum("ud,ucj->cdj", condition_here.astype(jnp.float32), columns, precision=highest)
        total = 0.0
        for u in range(columns.shape[0]):
            total = total + condition_here[u].astype(jnp.float32)[None, :, None] * columns[u][:, None, :]
        return total

    late_mod = mod_gradient(late_sums[:, :count])
    gradients, *att_parts = attend_back(
        info, ranges, qkv, grad_pieces, log_totals, cosine, sine, qkv_here, qkv_away, count
    )
    att_parts = exchange(att_parts)
    grad_att_in = sum(part.astype(jnp.float32) for part in att_parts)
    if packs_here == 2:
        qkv_away_grad = swapped(qkv_grads(info, 1, gradients, att_full), "dp", 1)
        qkv_share = qkv_grads(info, 0, gradients, att_full, other=qkv_away_grad, kind=jnp.float32)
    else:
        both = [qkv_grads(info, side, gradients, att_full, kind=jnp.float32) for side in range(2)]
        qkv_share = lax.psum_scatter(jnp.concatenate(both, axis=1), "dp", scatter_dimension=1, tiled=True)

    number_own, _ = utterance_rows(ending, me * own_rows + jnp.arange(own_rows, dtype=jnp.int32))
    number_own = number_own[:, None]
    normed, inverse_scale = normalize(features.astype(jnp.float32))
    grad_features = grad_residual + normalize_back(
        grad_att_in * (1.0 + by_utterance(number_own, modulation[1, :count])), normed, inverse_scale
    )
    early_rows = (grad_att_in, grad_att_in * normed)
    early_sums = jnp.stack(
        [
            jnp.stack([jnp.sum(jnp.where(number_own == u, rows, 0.0), axis=0) for u in range(count)])
            for rows in early_rows
        ]
    )
    early_mod = mod_gradient(early_sums)

    steps_done = step_count[0].astype(jnp.float32)
    row_first_new, row_second_new, row_diff = inner_step(
        wide_grad[0:3], row_first[0], row_second[0], row_weights, steps_done
    )
    col_first_new, col_second_new, col_diff = inner_step(
        columns_first(jnp.concatenate([qkv_share, wide_grad[3:5]], axis=0)), col_first[0], col_second[0], col_weights, steps_done
    )
    mod_first_new, mod_second_new, mod_diff = inner_step(
        columns_first(jnp.concatenate([early_mod, late_mod], axis=0)), mod_first[0], mod_second[0], mod_weights, steps_done
    )

    diffs = jnp.concatenate(
        [row_diff.astype(low), columns_first(col_diff).astype(low), columns_first(mod_diff).astype(low)], axis=0
    )
    averages = group_sum(diffs).astype(jnp.float32) / group_count
    row_average, col_average, mod_average = averages[0:3], columns_first(averages[3:8]), columns_first(averages[8:14])
    col_outer_new, col_new = outer_step(col_average, col_outer, col_weights)
    mod_outer_new, mod_new = outer_step(mod_average, mod_outer, mod_weights)
    row_outer_new, row_new = outer_step(row_average, row_outer, row_weights)
    return (
        output,
        grad_features,
        col_first_new,
        col_second_new,
        col_average,
        col_outer_new,
        col_new,
        mod_first_new,
        mod_second_new,
        mod_average,
        mod_outer_new,
        mod_new,
        row_first_new,
        row_second_new,
        row_average,
        row_outer_new,
        row_new,
    )


def solution(mesh):
    placed = (
        P(("group", "dp", "tensor"), None),
        P(("group", "dp", "tensor"), None),
        P(("group", "dp"), None),
        P(("group", "dp"), None),
        P(),
        P("dp", None, "tensor"),
        P("dp", None, "tensor"),
        P(None, "dp", "tensor"),
        P("group", "dp", None, "tensor"),
        P("group", "dp", None, "tensor"),
        P("group", "dp", None, "tensor"),
        P("group", "dp", None, "tensor"),
        P("group", None, "dp", "tensor"),
        P("group", None, "dp", "tensor"),
        P("dp", None, "tensor"),
        P("dp", None, "tensor"),
        P(None, "dp", "tensor"),
    )
    return jax.shard_map(
        per_device,
        mesh=mesh,
        in_specs=placed,
        out_specs=(
            P(("group", "dp", "tensor"), None),
            P(("group", "dp", "tensor"), None),
            P("group", "dp", None, "tensor"),
            P("group", "dp", None, "tensor"),
            P("dp", None, "tensor"),
            P("dp", None, "tensor"),
            P("dp", None, "tensor"),
            P("group", "dp", None, "tensor"),
            P("group", "dp", None, "tensor"),
            P("dp", None, "tensor"),
            P("dp", None, "tensor"),
            P("dp", None, "tensor"),
            P("group", None, "dp", "tensor"),
            P("group", None, "dp", "tensor"),
            P(None, "dp", "tensor"),
            P(None, "dp", "tensor"),
            P(None, "dp", "tensor"),
        ),
        check_vma=False,
    )
```

time: 1260 us -> 569 us (0.45)
  waiting for transfers between devices: 868 us -> 263 us
  matrix products: 153 us -> 0.31 us
  Pallas kernels: 0 us -> 112 us
  starting transfers between devices: 1.12 us -> 97.7 us
  local copies, waits for them, and re-layouts: 84.9 us -> 14.5 us
  other arithmetic: 99.5 us -> 59.9 us
  blocking collectives: 13.6 us -> 0 us
    reduce_scatter x7 -> x1, waiting for transfers between devices: 449 us -> 0.01 us  [per_device(): lax.psum_scatter(wide_blocks, 'tensor', scatter_dimension=0, tiled=False)]
    ppermute x0 -> x43, waiting for transfers between devices: none -> 262 us  [swapped(): return lax.ppermute(values, axis, [(i, i ^ bits) for i in range(size)])]
    all_gather x7 -> x1, waiting for transfers between devices: 258 us -> 0.01 us  [per_device(): features_full = lax.all_gather(features, 'tensor', axis=0, tiled=True)]
    dot_general x37 -> x1, matrix products: 153 us -> 0.31 us  [per_device(): jnp.einsum('ud,dcj->cuj', condition_here, mod_weights.astype(low), prefer...]
    psum x1 -> x0, waiting for transfers between devices: 152 us -> none  [per_device(): lax.psum((col_diff, mod_diff, row_diff), 'group')]
    pallas_call x0 -> x8, Pallas kernels: none -> 112 us  [the longest x1 29.2 us: attend_back(): pl.pallas_call(partial(backward_kernel, count), grid_spec=pltpu.PrefetchS...]
    ppermute x0 -> x43, starting transfers between devices: none -> 97.7 us  [swapped(): return lax.ppermute(values, axis, [(i, i ^ bits) for i in range(size)])]
    dynamic_update_slice x6 -> x3, local copies, waits for them, and re-layouts: 37.5 us -> 0.28 us  [group_sum(): out = lax.dynamic_update_slice_in_dim(out, part, (group ^ r) * quarter, 1)]
  transfers between devices with their start and end apart: 16 -> 45, of which waited for: 14 -> 24; matrix products, arithmetic and copies ran while one was open for 10% -> 9% of each run, Pallas kernels for 0% -> 12%
where the time goes in v2:
time: 569 us; the launch traced here: 563 us
  waiting for transfers between devices  263 us (46%)
  Pallas kernels  112 us (20%)
  starting transfers between devices  97.7 us (17%)
  other arithmetic  59.9 us (11%)
  between operations  15.9 us (3%)
  local copies, waits for them, and re-layouts  14.5 us (3%)
    ppermute x43, waiting for transfers between devices, swapped(): return lax.ppermute(values, axis, [(i, i ^ bits) for i in range(size)])  262 us
    ppermute x43, starting transfers between devices, swapped(): return lax.ppermute(values, axis, [(i, i ^ bits) for i in range(size)])  97.7 us
    pallas_call x1, Pallas kernels, attend_back(): pl.pallas_call(partial(backward_kernel, count), grid_spec=pltpu.PrefetchS...  29.2 us
    pallas_call x1, Pallas kernels, middle(): pl.pallas_call(partial(middle_kernel, count), grid_spec=pltpu.PrefetchSca...  23.5 us
    pallas_call x2, Pallas kernels, wide_grads(): pl.pallas_call(partial(wide_grad_kernel, side, other is not None), grid_s...  18.6 us
    pallas_call x1, Pallas kernels, attend(): pl.pallas_call(partial(forward_kernel, count), grid_spec=pltpu.PrefetchSc...  15 us
    pallas_call x1, Pallas kernels, project(): pl.pallas_call(partial(project_kernel, count), grid_spec=pltpu.PrefetchSc...  13.1 us
    pallas_call x2, Pallas kernels, qkv_grads(): pl.pallas_call(partial(qkv_grad_kernel, side, other is not None), grid_sp...  13.1 us
  transfers between devices with their start and end apart: 45, of which 24 were waited for; matrix products, arithmetic and copies ran while one was open for 9% of the time, Pallas kernels for 12%

profile of v2, /device:TPU:0, one launch (start us, length us, event | category | flops | bytes accessed | tf_op | source)
XLA Modules:
  0.0 563.5 jit_solution(10712721615217089728)
XLA Ops:
  8.5 1.9 convert_bitcast_fusion
  12.4 2.5 convert_element_type.192
  14.9 2.5 pad_maximum_fusion.1
  19.4 5.0 collective-permute-start.4
  25.2 1.6 collective-permute-done.4.m3_ref
  26.8 3.2 collective-permute-done.3.m2_ref
  34.1 2.4 collective-permute-start.11
  38.4 27.3 %collective-permute-done.10 = bf16[5,128,256]{2,1,0:T(8,128)(2,1)S(1)} collective-permute-done((bf16[5,128,256]{2,1,0:T(8,128)(2,1)S(1)}, bf16[5,128,256]{2,1,0:T(8,128)(2,1)S(1)}, u32[]{:S(2)}, u32[]{:S(2)}) %collective-permute-start.10) | collective-permute-done | bytes 327712 | tf_op jit(solution)/shard_map/ppermute | solution.py:694
  65.7 11.9 %collective-permute-done.11 = bf16[5,128,256]{2,1,0:T(8,128)(2,1)S(1)} collective-permute-done((bf16[5,128,256]{2,1,0:T(8,128)(2,1)S(1)}, bf16[5,128,256]{2,1,0:T(8,128)(2,1)S(1)}, u32[]{:S(2)}, u32[]{:S(2)}) %collective-permute-start.11) | collective-permute-done | bytes 327712 | tf_op jit(solution)/shard_map/ppermute | solution.py:694
  78.8 1.5 collective-permute-start.13
  80.3 1.5 collective-permute-start.12
  84.4 2.8 fusion.23
  87.2 2.4 pad_maximum_fusion.3
  89.7 18.8 %collective-permute-done.13.refs_2_ = bf16[4,5,128,256]{3,2,1,0:T(8,128)(2,1)} collective-permute-done((bf16[4,5,128,256]{3,2,1,0:T(8,128)(2,1)}, bf16[4,5,128,256]{3,2,1,0:T(8,128)(2,1)}, u32[]{:S(2)}, u32[]{:S(2)}) %collective-permute-start.13) | collective-permute-done | bytes 1310752 | tf_op jit(solution)/shard_map/ppermute | solution.py:694
  108.5 2.0 slice.170
  110.5 1.5 collective-permute-start.15
  112.0 2.0 slice.169
  113.9 1.5 collective-permute-start.14
  116.0 13.1 %project.1 = (bf16[1536,1024]{1,0:T(8,128)(2,1)}, bf16[3,1536,256]{2,1,0:T(8,128)(2,1)}, f32[6,8,1024]{2,1,0:T(8,128)}) custom-call(s32[6]{0:T(128)} %pad_add_fusion.1.info_ref, bf16[1536,1024]{1,0:T(8,128)(2,1)} %all-gather.2.cloned.1.call-done.x_ref, f32[6,3,256]{2,1,0:T(4,128)} %copy-done.19, f32[6,3,256]{2,1,0:T(4,128)} %copy-done.24, ...), custom_call_target="tpu_custom_call" | custom-call | flops 2415919104 | bytes 9437184 | tf_op jit(solution)/shard_map/project/pallas_call | solution.py:164
  129.1 15.0 %attend.1 = (bf16[384,256]{1,0:T(8,128)(2,1)}, bf16[384,256]{1,0:T(8,128)(2,1)}, bf16[384,256]{1,0:T(8,128)(2,1)}, bf16[384,256]{1,0:T(8,128)(2,1)}, f32[4,1536]{1,0:T(4,128)}) custom-call(s32[6]{0:T(128)} %pad_add_fusion.1.info_ref, s32[2,4]{1,0:T(2,128)} %pad_add_fusion.range_ref, bf16[3,1536,256]{2,1,0:T(8,128)(2,1)} %get-tuple-element.43.qkv_ref), custom_call_target="tpu_custom_call" | custom-call | flops 4831838208 | bytes 3145728 | tf_op jit(solution)/shard_map/attend/pallas_call | solution.py:387
  144.1 22.2 %collective-permute-start.6 = (bf16[384,256]{1,0:T(8,128)(2,1)}, bf16[384,256]{1,0:T(8,128)(2,1)S(1)}, u32[]{:S(2)}, u32[]{:S(2)}) collective-permute-start(bf16[384,256]{1,0:T(8,128)(2,1)} %get-tuple-element.45), channel_id=1, source_target_pairs={{0,1},{1,0},{2,3},{3,2},{4,5},{5,4},{6,7},{7,6},{8,9},{9,8},{10,11... | collective-permute-start | bytes 589832 | tf_op jit(solution)/shard_map/ppermute | solution.py:694
  166.3 7.9 %collective-permute-done.6.mixed1 = bf16[384,256]{1,0:T(8,128)(2,1)S(1)} collective-permute-done((bf16[384,256]{1,0:T(8,128)(2,1)}, bf16[384,256]{1,0:T(8,128)(2,1)S(1)}, u32[]{:S(2)}, u32[]{:S(2)}) %collective-permute-start.6) | collective-permute-done | bytes 196640 | tf_op jit(solution)/shard_map/ppermute | solution.py:694
  174.2 2.6 collective-permute-start.8
  176.8 6.8 %collective-permute-done.7.mixed2 = bf16[384,256]{1,0:T(8,128)(2,1)S(1)} collective-permute-done((bf16[384,256]{1,0:T(8,128)(2,1)}, bf16[384,256]{1,0:T(8,128)(2,1)S(1)}, u32[]{:S(2)}, u32[]{:S(2)}) %collective-permute-start.7) | collective-permute-done | bytes 196640 | tf_op jit(solution)/shard_map/ppermute | solution.py:694
  184.4 1.9 pad_maximum_fusion.5.mixed_ref
  187.0 23.5 %middle.1 = (bf16[384,1024]{1,0:T(8,128)(2,1)}, f32[384,1024]{1,0:T(8,128)}, bf16[384,256]{1,0:T(8,128)(2,1)}, bf16[384,256]{1,0:T(8,128)(2,1)}, bf16[384,256]{1...) custom-call(s32[6]{0:T(128)} %pad_add_fusion.1.info_ref, ...), custom_call_target="tpu_custom_call" | custom-call | flops 8053063680 | bytes 10485760 | tf_op jit(solution)/shard_map/middle/pallas_call | solution.py:556
  210.5 8.7 %wide_grads.2 = bf16[4,5,512,256]{3,2,1,0:T(8,128)(2,1)} custom-call(s32[6]{0:T(128)} %pad_add_fusion.1.info_ref, bf16[4,384,256]{2,1,0:T(8,128)(2,1)} %pad_maximum_fusion.5.mixed_ref, bf16[2,384,1024]{2,1,0:T(8,128)(2,1)} %get-tuple-element.63.hidden_ref, bf16[2,384,1024]{2,1,0:T(8,128)(2,1)} %get-tuple-element.64.grad_up_ref, ...), custom_call_target="tpu_custom_call" | custom-call | flops 2013265920 | bytes 7864320 | tf_op jit(solution)/shard_map/wide_grads/pallas_call | solution.py:613
  219.4 8.9 %collective-permute-done.28.refs_3_ = bf16[4,5,512,256]{3,2,1,0:T(8,128)(2,1)} collective-permute-done((bf16[4,5,512,256]{3,2,1,0:T(8,128)(2,1)}, bf16[4,5,512,256]{3,2,1,0:T(8,128)(2,1)}, u32[]{:S(2)}, u32[]{:S(2)}) %collective-permute-start.28) | collective-permute-done | bytes 5242912 | tf_op jit(solution)/shard_map/ppermute | solution.py:694
  228.3 9.8 %wide_grads.3 = bf16[4,5,512,256]{3,2,1,0:T(8,128)(2,1)} custom-call(s32[6]{0:T(128)} %pad_add_fusion.1.info_ref, bf16[4,384,256]{2,1,0:T(8,128)(2,1)} %pad_maximum_fusion.5.mixed_ref, bf16[2,384,1024]{2,1,0:T(8,128)(2,1)} %get-tuple-element.63.hidden_ref, bf16[2,384,1024]{2,1,0:T(8,128)(2,1)} %get-tuple-element.64.grad_up_ref, ...), custom_call_target="tpu_custom_call" | custom-call | flops 2013265920 | bytes 7864320 | tf_op jit(solution)/shard_map/wide_grads/pallas_call | solution.py:613
  239.0 1.3 fusion.35
  241.6 1.5 fusion.11
  243.2 2.8 collective-permute-start.33
  248.4 2.9 collective-permute-start.21
  251.4 2.4 collective-permute-start.23
  254.8 15.5 %collective-permute-done.21.grad1 = bf16[384,256]{1,0:T(8,128)(2,1)S(1)} collective-permute-done((bf16[384,256]{1,0:T(8,128)(2,1)}, bf16[384,256]{1,0:T(8,128)(2,1)S(1)}, u32[]{:S(2)}, u32[]{:S(2)}) %collective-permute-start.21) | collective-permute-done | bytes 196640 | tf_op jit(solution)/shard_map/ppermute | solution.py:694
  270.3 4.2 collective-permute-done.22.grad2
  274.4 4.7 collective-permute-done.23.grad3
  279.1 29.2 %attend_back.1 = (bf16[3,1536,256]{2,1,0:T(8,128)(2,1)}, f32[384,1024]{1,0:T(8,128)}, bf16[384,1024]{1,0:T(8,128)(2,1)}, bf16[384,1024]{1,0:T(8,128)(2,1)}, bf16[384,1024]{1,0:T(8,128)(2,1)}) custom-call(s32[6]{0:T(128)} %pad_add_fusion.1.info_ref, s32[2,4]{1,0:T(2,128)} %pad_add_fusion.range_ref, bf16[3,1536,256]{2,1,0:T(8,128)(2,1)} %get-tuple-element.43.qkv_ref, ...), custom_call_target="tpu_custom_call" | custom-call | flops 9663676416 | bytes 7864320 | tf_op jit(solution)/shard_map/attend_back/pallas_call | solution.py:414
  308.4 16.4 %collective-permute-start.24 = (bf16[384,1024]{1,0:T(8,128)(2,1)}, bf16[384,1024]{1,0:T(8,128)(2,1)}, u32[]{:S(2)}, u32[]{:S(2)}) collective-permute-start(bf16[384,1024]{1,0:T(8,128)(2,1)} %get-tuple-element.58), channel_id=1, source_target_pairs={{0,1},{1,0},{2,3},{3,2},{4,5},{5,4},{6,7},{7,6},{8,9},{9,8},{10,11... | collective-permute-start | bytes 2359304 | tf_op jit(solution)/shard_map/ppermute | solution.py:694
  324.7 2.4 collective-permute-start.26
  327.2 6.4 %qkv_grads.2 = bf16[3,512,256]{2,1,0:T(8,128)(2,1)} custom-call(s32[6]{0:T(128)} %pad_add_fusion.1.info_ref, bf16[3,1536,256]{2,1,0:T(8,128)(2,1)} %get-tuple-element.61.grad_ref, bf16[1536,1024]{1,0:T(8,128)(2,1)} %get-tuple-element.62.att_ref), custom_call_target="tpu_custom_call" | custom-call | flops 1207959552 | bytes 4718592 | tf_op jit(solution)/shard_map/qkv_grads/pallas_call | solution.py:657
  333.6 42.9 %collective-permute-done.24 = bf16[384,1024]{1,0:T(8,128)(2,1)} collective-permute-done((bf16[384,1024]{1,0:T(8,128)(2,1)}, bf16[384,1024]{1,0:T(8,128)(2,1)}, u32[]{:S(2)}, u32[]{:S(2)}) %collective-permute-start.24) | collective-permute-done | bytes 786464 | tf_op jit(solution)/shard_map/ppermute | solution.py:694
  376.5 26.7 %collective-permute-done.25 = bf16[384,1024]{1,0:T(8,128)(2,1)} collective-permute-done((bf16[384,1024]{1,0:T(8,128)(2,1)}, bf16[384,1024]{1,0:T(8,128)(2,1)}, u32[]{:S(2)}, u32[]{:S(2)}) %collective-permute-start.25) | collective-permute-done | bytes 786464 | tf_op jit(solution)/shard_map/ppermute | solution.py:694
  403.3 5.1 select_reduce_fusion.2
  408.5 16.0 %collective-permute-start.29 = (f32[2,3,256]{2,0,1:T(2,128)S(1)}, f32[2,3,256]{2,0,1:T(2,128)S(1)}, u32[]{:S(2)}, u32[]{:S(2)}) collective-permute-start(f32[2,3,256]{2,0,1:T(2,128)S(1)} %get-tuple-element.114), channel_id=1, source_target_pairs={{0,1},{1,0},{2,3},{3,2},{4,5},{5,4},{6,7},{7,6},{8,9},{9,8},{10,11... | collective-permute-start | bytes 18440 | tf_op jit(solution)/shard_map/ppermute | solution.py:694
  424.6 2.4 collective-permute-start.31
  427.0 2.0 multiply_add_fusion.2
  430.2 6.7 %qkv_grads.3 = f32[3,512,256]{2,1,0:T(8,128)} custom-call(s32[6]{0:T(128)} %pad_add_fusion.1.info_ref, bf16[3,1536,256]{2,1,0:T(8,128)(2,1)} %get-tuple-element.61.grad_ref, bf16[1536,1024]{1,0:T(8,128)(2,1)} %get-tuple-element.62.att_ref, bf16[3,512,256]{2,1,0:T(8,128)(2,1)} %collective-permute-done.27.refs_0_), custom_call_target="tpu_custom_call" | custom-call | flops 1207959552 | bytes 4718592 | tf_op jit(solution)/shard_map/qkv_grads/pallas_call | solution.py:657
  437.4 6.8 %fusion.22 = (f32[1,512,6,256]{3,1,2,0:T(8,128)}, bf16[6,512,256]{2,1,0:T(8,128)(2,1)}, f32[1,512,6,256]{3,1,2,0:T(8,128)}) fusion(f32[4,512,256]{2,1,0:T(8,128)} %multiply_add_fusion.2, f32[2,512,256]{2,1,0:T(8,128)S(1)} %multiply_add_fusion.4, f32[1,512,6,256]{3,1,2,0:T(8,128)} %param.28, f32[512,6,256]{2,0,1:T(8,128)S(1)} %copy-done, f32[]{:T(128)} %bitcast.36, ...), kind=kLoop, calls=%fused_computation.66 | loop fusion | flops 12582912 | bytes 20447240 | tf_op jit(solution)/shard_map/broadcast_in_dim | solution.py:684
  444.3 1.7 convert_element_type.199
  447.0 2.8 fusion.21
  451.9 3.5 fusion.16
  456.1 1.4 collective-permute-start.37
  457.5 1.8 collective-permute-start.39
  459.7 19.7 %collective-permute-done.37 = bf16[14,128,256]{2,1,0:T(8,128)(2,1)S(1)} collective-permute-done((bf16[14,128,256]{2,1,0:T(8,128)(2,1)S(1)}, bf16[14,128,256]{2,1,0:T(8,128)(2,1)S(1)}, u32[]{:S(2)}, u32[]{:S(2)}) %collective-permute-start.37) | collective-permute-done | bytes 917536 | tf_op jit(solution)/shard_map/ppermute | solution.py:694
  479.4 20.4 %collective-permute-done.39 = bf16[14,128,256]{2,1,0:T(8,128)(2,1)S(1)} collective-permute-done((bf16[14,128,256]{2,1,0:T(8,128)(2,1)S(1)}, bf16[14,128,256]{2,1,0:T(8,128)(2,1)S(1)}, u32[]{:S(2)}, u32[]{:S(2)}) %collective-permute-start.39) | collective-permute-done | bytes 917536 | tf_op jit(solution)/shard_map/ppermute | solution.py:694
  499.8 1.4 collective-permute-done.38
  503.9 1.8 collective-permute-start.42
  505.7 1.9 fusion.10
  507.6 17.8 %collective-permute-done.40 = bf16[14,128,256]{2,1,0:T(8,128)(2,1)S(1)} collective-permute-done((bf16[14,128,256]{2,1,0:T(8,128)(2,1)S(1)}, bf16[14,128,256]{2,1,0:T(8,128)(2,1)S(1)}, u32[]{:S(2)}, u32[]{:S(2)}) %collective-permute-start.40) | collective-permute-done | bytes 917536 | tf_op jit(solution)/shard_map/ppermute | solution.py:694
  525.5 17.9 %collective-permute-done.41 = bf16[14,128,256]{2,1,0:T(8,128)(2,1)S(1)} collective-permute-done((bf16[14,128,256]{2,1,0:T(8,128)(2,1)S(1)}, bf16[14,128,256]{2,1,0:T(8,128)(2,1)S(1)}, u32[]{:S(2)}, u32[]{:S(2)}) %collective-permute-start.41) | collective-permute-done | bytes 917536 | tf_op jit(solution)/shard_map/ppermute | solution.py:694
  545.0 2.5 multiply_subtract_fusion.2
  547.8 3.9 multiply_subtract_fusion.1
  551.7 4.5 multiply_subtract_fusion
  (172 shorter events, 33.6 us)
Async XLA Ops:
  7.2 108.8 %all-gather.2.cloned.1.call-start = ((), (), s32[]{:S(2)}) async-start(), calls=%async_computation.1 | async-start | bytes 3932160 | tf_op jit(solution)/shard_map/all_gather | solution.py:780
  7.9 436.3 %reduce-scatter.2.cloned.1.call-start = ((), (), s32[]{:S(2)}) async-start(), calls=%async_computation.2 | async-start | bytes 6553600 | tf_op jit(solution)/shard_map/reduce_scatter | solution.py:819
  8.0 9.4 %collective-permute-start = (s32[3]{0:T(128)}, s32[3]{0:T(128)S(1)}, u32[]{:S(2)}, u32[]{:S(2)}) collective-permute-start(s32[3]{0:T(128)} %bitcast.238), channel_id=1, source_target_pairs={{0,4},{4,0},{1,5},{5,1},{2,6},{6,2},{3,7},{7,3},{8,12},{12,8},{9,1... | collective-permute-start | bytes 44 | tf_op jit(solution)/shard_map/ppermute | solution.py:694
  11.3 104.1 %collective-permute-start.5 = (bf16[3,512,256]{2,1,0:T(8,128)(2,1)}, bf16[3,512,256]{2,1,0:T(8,128)(2,1)}, u32[]{:S(2)}, u32[]{:S(2)}) collective-permute-start(bf16[3,512,256]{2,1,0:T(8,128)(2,1)} %slice.167.here_ref), channel_id=1, source_target_pairs={{0,4},{4,0},{1,5},{5,1},{2,6},{6,2},{3,7},{7,3},{8,12},{12,8},{9,1... | collective-permute-start | bytes 2359304 | tf_op jit(solution)/shard_map/ppermute | solution.py:694
  12.4 5.0 copy-start.20
  12.4 5.3 copy-start
  18.0 1.4 collective-permute-start.1
  19.4 67.8 %copy-start.19 = (f32[6,3,256]{2,1,0:T(4,128)}, f32[6,3,256]{2,1,0:T(4,128)S(1)}, u32[]{:S(2)}) copy-start(f32[6,3,256]{2,1,0:T(4,128)S(1)} %bitcast_add_fusion.3.m0_ref) | copy-start | bytes 55300
  19.4 7.3 %collective-permute-start.4 = (f32[6,3,256]{2,1,0:T(4,128)S(1)}, f32[6,3,256]{2,1,0:T(4,128)S(1)}, u32[]{:S(2)}, u32[]{:S(2)}) collective-permute-start(f32[6,3,256]{2,1,0:T(4,128)S(1)} %bitcast_add_fusion.3.m0_ref), channel_id=1, source_target_pairs={{0,3},{1,2},{2,1},{3,0},{4,7},{5,6},{6,5},{7,4},{8,11},{9,10},{10,... | collective-permute-start | bytes 55304 | tf_op jit(solution)/shard_map/ppermute | solution.py:694
  24.4 5.5 collective-permute-start.3
  24.4 6.6 %collective-permute-start.2 = (f32[6,3,256]{2,1,0:T(4,128)S(1)}, f32[6,3,256]{2,1,0:T(4,128)S(1)}, u32[]{:S(2)}, u32[]{:S(2)}) collective-permute-start(f32[6,3,256]{2,1,0:T(4,128)S(1)} %bitcast_add_fusion.3.m0_ref), channel_id=1, source_target_pairs={{0,1},{1,0},{2,3},{3,2},{4,5},{5,4},{6,7},{7,6},{8,9},{9,8},{10,11... | collective-permute-start | bytes 55304 | tf_op jit(solution)/shard_map/ppermute | solution.py:694
  26.8 60.4 %copy-start.22 = (f32[6,3,256]{2,1,0:T(4,128)}, f32[6,3,256]{2,1,0:T(4,128)S(1)}, u32[]{:S(2)}) copy-start(f32[6,3,256]{2,1,0:T(4,128)S(1)} %collective-permute-done.4.m3_ref) | copy-start | bytes 55300
  29.9 57.3 %copy-start.23 = (f32[6,3,256]{2,1,0:T(4,128)}, f32[6,3,256]{2,1,0:T(4,128)S(1)}, u32[]{:S(2)}) copy-start(f32[6,3,256]{2,1,0:T(4,128)S(1)} %collective-permute-done.3.m2_ref) | copy-start | bytes 55300
  31.0 56.2 %copy-start.24 = (f32[6,3,256]{2,1,0:T(4,128)}, f32[6,3,256]{2,1,0:T(4,128)S(1)}, u32[]{:S(2)}) copy-start(f32[6,3,256]{2,1,0:T(4,128)S(1)} %collective-permute-done.2.m1_ref) | copy-start | bytes 55300
  32.0 33.6 %collective-permute-start.10 = (bf16[5,128,256]{2,1,0:T(8,128)(2,1)S(1)}, bf16[5,128,256]{2,1,0:T(8,128)(2,1)S(1)}, u32[]{:S(2)}, u32[]{:S(2)}) collective-permute-start(bf16[5,128,256]{2,1,0:T(8,128)(2,1)S(1)} %constant_dynamic-slice_fusion.6), channel_id=1, source_target_pairs={{0,2},{1,3},{2,0},{3,1},{4,6},{5,7},{6,4},{7,5},{8,10},{9,11},{10,... | collective-permute-start | bytes 983048 | tf_op jit(solution)/shard_map/ppermute | solution.py:694
  32.9 32.8 %collective-permute-start.9 = (bf16[5,128,256]{2,1,0:T(8,128)(2,1)S(1)}, bf16[5,128,256]{2,1,0:T(8,128)(2,1)S(1)}, u32[]{:S(2)}, u32[]{:S(2)}) collective-permute-start(bf16[5,128,256]{2,1,0:T(8,128)(2,1)S(1)} %constant_dynamic-slice_fusion.6), channel_id=1, source_target_pairs={{0,1},{1,0},{2,3},{3,2},{4,5},{5,4},{6,7},{7,6},{8,9},{9,8},{10,11... | collective-permute-start | bytes 983048 | tf_op jit(solution)/shard_map/ppermute | solution.py:694
  34.1 43.5 %collective-permute-start.11 = (bf16[5,128,256]{2,1,0:T(8,128)(2,1)S(1)}, bf16[5,128,256]{2,1,0:T(8,128)(2,1)S(1)}, u32[]{:S(2)}, u32[]{:S(2)}) collective-permute-start(bf16[5,128,256]{2,1,0:T(8,128)(2,1)S(1)} %constant_dynamic-slice_fusion.6), channel_id=1, source_target_pairs={{0,3},{1,2},{2,1},{3,0},{4,7},{5,6},{6,5},{7,4},{8,11},{9,10},{10,... | collective-permute-start | bytes 983048 | tf_op jit(solution)/shard_map/ppermute | solution.py:694
  78.8 29.7 %collective-permute-start.13 = (bf16[4,5,128,256]{3,2,1,0:T(8,128)(2,1)}, bf16[4,5,128,256]{3,2,1,0:T(8,128)(2,1)}, u32[]{:S(2)}, u32[]{:S(2)}) collective-permute-start(bf16[4,5,128,256]{3,2,1,0:T(8,128)(2,1)} %pad_maximum_fusion.2.refs_0_), channel_id=1, source_target_pairs={{0,16},{8,24},{16,0},{24,8},{1,17},{9,25},{17,1},{25,9},{2,18},{10... | collective-permute-start | bytes 3932168 | tf_op jit(solution)/shard_map/ppermute | solution.py:694
  80.3 31.7 %collective-permute-start.12 = (bf16[4,5,128,256]{3,2,1,0:T(8,128)(2,1)}, bf16[4,5,128,256]{3,2,1,0:T(8,128)(2,1)}, u32[]{:S(2)}, u32[]{:S(2)}) collective-permute-start(bf16[4,5,128,256]{3,2,1,0:T(8,128)(2,1)} %pad_maximum_fusion.2.refs_0_), channel_id=1, source_target_pairs={{0,8},{8,0},{16,24},{24,16},{1,9},{9,1},{17,25},{25,17},{2,10},{10... | collective-permute-start | bytes 3932168 | tf_op jit(solution)/shard_map/ppermute | solution.py:694
  89.7 96.6 %collective-permute-start.16 = (bf16[4,5,128,256]{3,2,1,0:T(8,128)(2,1)}, bf16[4,5,128,256]{3,2,1,0:T(8,128)(2,1)}, u32[]{:S(2)}, u32[]{:S(2)}) collective-permute-start(bf16[4,5,128,256]{3,2,1,0:T(8,128)(2,1)} %pad_maximum_fusion.2.refs_0_), channel_id=1, source_target_pairs={{0,4},{4,0},{1,5},{5,1},{2,6},{6,2},{3,7},{7,3},{8,12},{12,8},{9,1... | collective-permute-start | bytes 3932168 | tf_op jit(solution)/shard_map/ppermute | solution.py:694
  110.5 33.6 %collective-permute-start.15 = (bf16[2,5,128,256]{3,2,1,0:T(8,128)(2,1)}, bf16[2,5,128,256]{3,2,1,0:T(8,128)(2,1)}, u32[]{:S(2)}, u32[]{:S(2)}) collective-permute-start(bf16[2,5,128,256]{3,2,1,0:T(8,128)(2,1)} %slice.170), channel_id=1, source_target_pairs={{0,8},{8,0},{16,24},{24,16},{1,9},{9,1},{17,25},{25,17},{2,10},{10... | collective-permute-start | bytes 1966088 | tf_op jit(solution)/shard_map/ppermute | solution.py:694
  113.9 52.4 %collective-permute-start.14 = (bf16[2,5,128,256]{3,2,1,0:T(8,128)(2,1)}, bf16[2,5,128,256]{3,2,1,0:T(8,128)(2,1)}, u32[]{:S(2)}, u32[]{:S(2)}) collective-permute-start(bf16[2,5,128,256]{3,2,1,0:T(8,128)(2,1)} %slice.169), channel_id=1, source_target_pairs={{0,16},{8,24},{16,0},{24,8},{1,17},{9,25},{17,1},{25,9},{2,18},{10... | collective-permute-start | bytes 1966088 | tf_op jit(solution)/shard_map/ppermute | solution.py:694
  115.5 71.6 %collective-permute-start.18 = (bf16[4,5,128,256]{3,2,1,0:T(8,128)(2,1)}, bf16[4,5,128,256]{3,2,1,0:T(8,128)(2,1)}, u32[]{:S(2)}, u32[]{:S(2)}) collective-permute-start(bf16[4,5,128,256]{3,2,1,0:T(8,128)(2,1)} %collective-permute-done.13.refs_2_), channel_id=1, source_target_pairs={{0,4},{4,0},{1,5},{5,1},{2,6},{6,2},{3,7},{7,3},{8,12},{12,8},{9,1... | collective-permute-start | bytes 3932168 | tf_op jit(solution)/shard_map/ppermute | solution.py:694
  115.5 71.6 %collective-permute-start.17 = (bf16[4,5,128,256]{3,2,1,0:T(8,128)(2,1)}, bf16[4,5,128,256]{3,2,1,0:T(8,128)(2,1)}, u32[]{:S(2)}, u32[]{:S(2)}) collective-permute-start(bf16[4,5,128,256]{3,2,1,0:T(8,128)(2,1)} %collective-permute-done.12.refs_1_), channel_id=1, source_target_pairs={{0,4},{4,0},{1,5},{5,1},{2,6},{6,2},{3,7},{7,3},{8,12},{12,8},{9,1... | collective-permute-start | bytes 3932168 | tf_op jit(solution)/shard_map/ppermute | solution.py:694
  144.1 30.1 %collective-permute-start.6 = (bf16[384,256]{1,0:T(8,128)(2,1)}, bf16[384,256]{1,0:T(8,128)(2,1)S(1)}, u32[]{:S(2)}, u32[]{:S(2)}) collective-permute-start(bf16[384,256]{1,0:T(8,128)(2,1)} %get-tuple-element.45), channel_id=1, source_target_pairs={{0,1},{1,0},{2,3},{3,2},{4,5},{5,4},{6,7},{7,6},{8,9},{9,8},{10,11... | collective-permute-start | bytes 589832 | tf_op jit(solution)/shard_map/ppermute | solution.py:694
  166.3 17.3 %collective-permute-start.7 = (bf16[384,256]{1,0:T(8,128)(2,1)}, bf16[384,256]{1,0:T(8,128)(2,1)S(1)}, u32[]{:S(2)}, u32[]{:S(2)}) collective-permute-start(bf16[384,256]{1,0:T(8,128)(2,1)} %get-tuple-element.46), channel_id=1, source_target_pairs={{0,2},{1,3},{2,0},{3,1},{4,6},{5,7},{6,4},{7,5},{8,10},{9,11},{10,... | collective-permute-start | bytes 589832 | tf_op jit(solution)/shard_map/ppermute | solution.py:694
  174.2 12.8 %copy-start.15 = (bf16[384,256]{1,0:T(8,128)(2,1)}, bf16[384,256]{1,0:T(8,128)(2,1)S(1)}, u32[]{:S(2)}) copy-start(bf16[384,256]{1,0:T(8,128)(2,1)S(1)} %collective-permute-done.6.mixed1) | copy-start | bytes 589828
  174.2 9.4 %collective-permute-start.8 = (bf16[384,256]{1,0:T(8,128)(2,1)}, bf16[384,256]{1,0:T(8,128)(2,1)S(1)}, u32[]{:S(2)}, u32[]{:S(2)}) collective-permute-start(bf16[384,256]{1,0:T(8,128)(2,1)} %get-tuple-element.47), channel_id=1, source_target_pairs={{0,3},{1,2},{2,1},{3,0},{4,7},{5,6},{6,5},{7,4},{8,11},{9,10},{10,... | collective-permute-start | bytes 589832 | tf_op jit(solution)/shard_map/ppermute | solution.py:694
  183.6 3.4 copy-start.16
  183.6 2.6 collective-permute-start.20
  183.7 3.4 collective-permute-start.19
  219.2 9.1 %collective-permute-start.28 = (bf16[4,5,512,256]{3,2,1,0:T(8,128)(2,1)}, bf16[4,5,512,256]{3,2,1,0:T(8,128)(2,1)}, u32[]{:S(2)}, u32[]{:S(2)}) collective-permute-start(bf16[4,5,512,256]{3,2,1,0:T(8,128)(2,1)} %wide_grads.2), channel_id=1, source_target_pairs={{0,4},{4,0},{1,5},{5,1},{2,6},{6,2},{3,7},{7,3},{8,12},{12,8},{9,1... | collective-permute-start | bytes 15728648 | tf_op jit(solution)/shard_map/ppermute | solution.py:694
  238.1 5.0 copy-start.18
  243.2 8.2 %collective-permute-start.33 = (f32[4,3,256]{2,1,0:T(4,128)S(1)}, f32[4,3,256]{2,1,0:T(4,128)S(1)}, u32[]{:S(2)}, u32[]{:S(2)}) collective-permute-start(f32[4,3,256]{2,1,0:T(4,128)S(1)} %get-tuple-element.109), channel_id=1, source_target_pairs={{0,1},{1,0},{2,3},{3,2},{4,5},{5,4},{6,7},{7,6},{8,9},{9,8},{10,11... | collective-permute-start | bytes 36872 | tf_op jit(solution)/shard_map/ppermute | solution.py:694
  246.0 7.8 %collective-permute-start.35 = (f32[4,3,256]{2,1,0:T(4,128)S(1)}, f32[4,3,256]{2,1,0:T(4,128)S(1)}, u32[]{:S(2)}, u32[]{:S(2)}) collective-permute-start(f32[4,3,256]{2,1,0:T(4,128)S(1)} %get-tuple-element.110), channel_id=1, source_target_pairs={{0,3},{1,2},{2,1},{3,0},{4,7},{5,6},{6,5},{7,4},{8,11},{9,10},{10,... | collective-permute-start | bytes 36872 | tf_op jit(solution)/shard_map/ppermute | solution.py:694
  247.2 7.3 %collective-permute-start.34 = (f32[4,3,256]{2,1,0:T(4,128)S(1)}, f32[4,3,256]{2,1,0:T(4,128)S(1)}, u32[]{:S(2)}, u32[]{:S(2)}) collective-permute-start(f32[4,3,256]{2,1,0:T(4,128)S(1)} %get-tuple-element.111), channel_id=1, source_target_pairs={{0,2},{1,3},{2,0},{3,1},{4,6},{5,7},{6,4},{7,5},{8,10},{9,11},{10,... | collective-permute-start | bytes 36872 | tf_op jit(solution)/shard_map/ppermute | solution.py:694
  248.4 21.8 %collective-permute-start.21 = (bf16[384,256]{1,0:T(8,128)(2,1)}, bf16[384,256]{1,0:T(8,128)(2,1)S(1)}, u32[]{:S(2)}, u32[]{:S(2)}) collective-permute-start(bf16[384,256]{1,0:T(8,128)(2,1)} %get-tuple-element.53), channel_id=1, source_target_pairs={{0,1},{1,0},{2,3},{3,2},{4,5},{5,4},{6,7},{7,6},{8,9},{9,8},{10,11... | collective-permute-start | bytes 589832 | tf_op jit(solution)/shard_map/ppermute | solution.py:694
  251.4 23.0 %collective-permute-start.22 = (bf16[384,256]{1,0:T(8,128)(2,1)}, bf16[384,256]{1,0:T(8,128)(2,1)}, u32[]{:S(2)}, u32[]{:S(2)}) collective-permute-start(bf16[384,256]{1,0:T(8,128)(2,1)} %get-tuple-element.54), channel_id=1, source_target_pairs={{0,2},{1,3},{2,0},{3,1},{4,6},{5,7},{6,4},{7,5},{8,10},{9,11},{10,... | collective-permute-start | bytes 589832 | tf_op jit(solution)/shard_map/ppermute | solution.py:694
  251.4 27.7 %collective-permute-start.23 = (bf16[384,256]{1,0:T(8,128)(2,1)}, bf16[384,256]{1,0:T(8,128)(2,1)}, u32[]{:S(2)}, u32[]{:S(2)}) collective-permute-start(bf16[384,256]{1,0:T(8,128)(2,1)} %get-tuple-element.55), channel_id=1, source_target_pairs={{0,3},{1,2},{2,1},{3,0},{4,7},{5,6},{6,5},{7,4},{8,11},{9,10},{10,... | collective-permute-start | bytes 589832 | tf_op jit(solution)/shard_map/ppermute | solution.py:694
  254.5 72.6 %collective-permute-start.36 = (f32[3,4,256]{2,0,1:T(4,128)S(1)}, f32[3,4,256]{2,0,1:T(4,128)S(1)}, u32[]{:S(2)}, u32[]{:S(2)}) collective-permute-start(f32[3,4,256]{2,0,1:T(4,128)S(1)} %add_bitcast_fusion), channel_id=1, source_target_pairs={{0,4},{4,0},{1,5},{5,1},{2,6},{6,2},{3,7},{7,3},{8,12},{12,8},{9,1... | collective-permute-start | bytes 36872 | tf_op jit(solution)/shard_map/ppermute | solution.py:694
  270.2 8.9 %copy-start.21 = (bf16[384,256]{1,0:T(8,128)(2,1)}, bf16[384,256]{1,0:T(8,128)(2,1)S(1)}, u32[]{:S(2)}) copy-start(bf16[384,256]{1,0:T(8,128)(2,1)S(1)} %collective-permute-done.21.grad1) | copy-start | bytes 589828
  308.4 68.2 %collective-permute-start.24 = (bf16[384,1024]{1,0:T(8,128)(2,1)}, bf16[384,1024]{1,0:T(8,128)(2,1)}, u32[]{:S(2)}, u32[]{:S(2)}) collective-permute-start(bf16[384,1024]{1,0:T(8,128)(2,1)} %get-tuple-element.58), channel_id=1, source_target_pairs={{0,1},{1,0},{2,3},{3,2},{4,5},{5,4},{6,7},{7,6},{8,9},{9,8},{10,11... | collective-permute-start | bytes 2359304 | tf_op jit(solution)/shard_map/ppermute | solution.py:694
  324.7 78.5 %collective-permute-start.25 = (bf16[384,1024]{1,0:T(8,128)(2,1)}, bf16[384,1024]{1,0:T(8,128)(2,1)}, u32[]{:S(2)}, u32[]{:S(2)}) collective-permute-start(bf16[384,1024]{1,0:T(8,128)(2,1)} %get-tuple-element.59), channel_id=1, source_target_pairs={{0,2},{1,3},{2,0},{3,1},{4,6},{5,7},{6,4},{7,5},{8,10},{9,11},{10,... | collective-permute-start | bytes 2359304 | tf_op jit(solution)/shard_map/ppermute | solution.py:694
  324.7 78.5 %collective-permute-start.26 = (bf16[384,1024]{1,0:T(8,128)(2,1)}, bf16[384,1024]{1,0:T(8,128)(2,1)}, u32[]{:S(2)}, u32[]{:S(2)}) collective-permute-start(bf16[384,1024]{1,0:T(8,128)(2,1)} %get-tuple-element.60), channel_id=1, source_target_pairs={{0,3},{1,2},{2,1},{3,0},{4,7},{5,6},{6,5},{7,4},{8,11},{9,10},{10,... | collective-permute-start | bytes 2359304 | tf_op jit(solution)/shard_map/ppermute | solution.py:694
  333.6 96.6 %collective-permute-start.27 = (bf16[3,512,256]{2,1,0:T(8,128)(2,1)}, bf16[3,512,256]{2,1,0:T(8,128)(2,1)}, u32[]{:S(2)}, u32[]{:S(2)}) collective-permute-start(bf16[3,512,256]{2,1,0:T(8,128)(2,1)} %qkv_grads.2), channel_id=1, source_target_pairs={{0,4},{4,0},{1,5},{5,1},{2,6},{6,2},{3,7},{7,3},{8,12},{12,8},{9,1... | collective-permute-start | bytes 2359304 | tf_op jit(solution)/shard_map/ppermute | solution.py:694
  408.5 20.5 %collective-permute-start.29 = (f32[2,3,256]{2,0,1:T(2,128)S(1)}, f32[2,3,256]{2,0,1:T(2,128)S(1)}, u32[]{:S(2)}, u32[]{:S(2)}) collective-permute-start(f32[2,3,256]{2,0,1:T(2,128)S(1)} %get-tuple-element.114), channel_id=1, source_target_pairs={{0,1},{1,0},{2,3},{3,2},{4,5},{5,4},{6,7},{7,6},{8,9},{9,8},{10,11... | collective-permute-start | bytes 18440 | tf_op jit(solution)/shard_map/ppermute | solution.py:694
  424.5 4.5 collective-permute-start.30
  424.6 5.4 collective-permute-start.31
  430.1 6.8 %collective-permute-start.32 = (f32[3,2,256]{2,1,0:T(2,128)S(1)}, f32[3,2,256]{2,1,0:T(2,128)S(1)}, u32[]{:S(2)}, u32[]{:S(2)}) collective-permute-start(f32[3,2,256]{2,1,0:T(2,128)S(1)} %add_bitcast_fusion.1), channel_id=1, source_target_pairs={{0,4},{4,0},{1,5},{5,1},{2,6},{6,2},{3,7},{7,3},{8,12},{12,8},{9,1... | collective-permute-start | bytes 18440 | tf_op jit(solution)/shard_map/ppermute | solution.py:694
  447.0 2.8 copy-start.1
  447.0 2.8 copy-start.5
  447.0 4.1 copy-start.8
  447.0 4.9 copy-start.9
  451.9 3.5 copy-start.4
  456.1 23.3 %collective-permute-start.37 = (bf16[14,128,256]{2,1,0:T(8,128)(2,1)S(1)}, bf16[14,128,256]{2,1,0:T(8,128)(2,1)S(1)}, u32[]{:S(2)}, u32[]{:S(2)}) collective-permute-start(bf16[14,128,256]{2,1,0:T(8,128)(2,1)S(1)} %get-tuple-element.103), channel_id=1, source_target_pairs={{0,8},{8,0},{16,24},{24,16},{1,9},{9,1},{17,25},{25,17},{2,10},{10... | collective-permute-start | bytes 2752520 | tf_op jit(solution)/shard_map/ppermute | solution.py:694
  457.5 42.3 %collective-permute-start.39 = (bf16[14,128,256]{2,1,0:T(8,128)(2,1)S(1)}, bf16[14,128,256]{2,1,0:T(8,128)(2,1)S(1)}, u32[]{:S(2)}, u32[]{:S(2)}) collective-permute-start(bf16[14,128,256]{2,1,0:T(8,128)(2,1)S(1)} %get-tuple-element.104), channel_id=1, source_target_pairs={{0,24},{8,16},{16,8},{24,0},{1,25},{9,17},{17,9},{25,1},{2,26},{10... | collective-permute-start | bytes 2752520 | tf_op jit(solution)/shard_map/ppermute | solution.py:694
  459.3 41.8 %collective-permute-start.38 = (bf16[14,128,256]{2,1,0:T(8,128)(2,1)S(1)}, bf16[14,128,256]{2,1,0:T(8,128)(2,1)S(1)}, u32[]{:S(2)}, u32[]{:S(2)}) collective-permute-start(bf16[14,128,256]{2,1,0:T(8,128)(2,1)S(1)} %get-tuple-element.105), channel_id=1, source_target_pairs={{0,16},{8,24},{16,0},{24,8},{1,17},{9,25},{17,1},{25,9},{2,18},{10... | collective-permute-start | bytes 2752520 | tf_op jit(solution)/shard_map/ppermute | solution.py:694
  501.5 4.2 copy-start.2
  501.5 4.2 copy-start.6
  501.5 4.2 copy-start.14
  502.1 23.3 %collective-permute-start.40 = (bf16[14,128,256]{2,1,0:T(8,128)(2,1)S(1)}, bf16[14,128,256]{2,1,0:T(8,128)(2,1)S(1)}, u32[]{:S(2)}, u32[]{:S(2)}) collective-permute-start(bf16[14,128,256]{2,1,0:T(8,128)(2,1)S(1)} %get-tuple-element.89), channel_id=1, source_target_pairs={{0,8},{8,0},{16,24},{24,16},{1,9},{9,1},{17,25},{25,17},{2,10},{10... | collective-permute-start | bytes 2752520 | tf_op jit(solution)/shard_map/ppermute | solution.py:694
  502.7 40.7 %collective-permute-start.41 = (bf16[14,128,256]{2,1,0:T(8,128)(2,1)S(1)}, bf16[14,128,256]{2,1,0:T(8,128)(2,1)S(1)}, u32[]{:S(2)}, u32[]{:S(2)}) collective-permute-start(bf16[14,128,256]{2,1,0:T(8,128)(2,1)S(1)} %get-tuple-element.89), channel_id=1, source_target_pairs={{0,16},{8,24},{16,0},{24,8},{1,17},{9,25},{17,1},{25,9},{2,18},{10... | collective-permute-start | bytes 2752520 | tf_op jit(solution)/shard_map/ppermute | solution.py:694
  503.9 39.6 %collective-permute-start.42 = (bf16[14,128,256]{2,1,0:T(8,128)(2,1)S(1)}, bf16[14,128,256]{2,1,0:T(8,128)(2,1)S(1)}, u32[]{:S(2)}, u32[]{:S(2)}) collective-permute-start(bf16[14,128,256]{2,1,0:T(8,128)(2,1)S(1)} %get-tuple-element.89), channel_id=1, source_target_pairs={{0,24},{8,16},{16,8},{24,0},{1,25},{9,17},{17,9},{25,1},{2,26},{10... | collective-permute-start | bytes 2752520 | tf_op jit(solution)/shard_map/ppermute | solution.py:694
  547.8 3.9 copy-start.7
  (7 other events, 13.5 us)
Sparse Core Ops, SparseCore 0:
  9.6 95.9 all-gather.1
  238.3 134.0 reduce-scatter.1
